TPU v7x, 128 devices: a whole 4x4x4 slice. The times are simulated.
128 devices in a mesh: row: 8 (over y_hi, x), col: 16 (over y_lo, z, core).
Axes of the slice: x: 4, y: 4 (y_hi: 2, y_lo: 2; y = y_hi * 2 + y_lo), z: 4, core: 2. Of those that a mesh axis runs over, the one named last changes fastest.
Arguments:
- amplitudes: bfloat16 [6144, 63488], P('col', 'row'), may hold values from -6 to 6
- integrals: bfloat16 [63488, 256], P(('row', 'col')), may hold values from -0.09375 to 0.09375
- cd_irrep: int32 [496], P('row'), may hold values from 0 to 3
- ab_irrep: int32 [4], replicated, may hold values from 0 to 3
- pair_energy: float32 [6144], P('col'), may hold values from -2 to -0.5
- panel_energy: float32 [256], replicated, may hold values from 2 to 6
Outputs:
- update: bfloat16 [6144, 256], P('col', 'row')
All inputs are finite; a program needn't handle non-finite values.
Results may differ from a plain program's by a relative error of at most 0.001.
Values may be sent and summed in bfloat16 or wider, within the bound.
No kernel may reach another device: no remote copies, remote signals or barrier semaphores. Data moves between devices by JAX's collectives and lax.ppermute only.
A program may use at most 64 MiB of HBM per device.

v0:
```python
import jax
import jax.numpy as jnp
from jax import lax
from jax.sharding import PartitionSpec as P

KBLK = 128
ABLK = 64


def shards(amplitudes, integrals, cd_irrep, ab_irrep, pair_energy, panel_energy):
    width = integrals.shape[1]
    block_labels = jnp.repeat(cd_irrep, KBLK)
    panel_labels = jnp.repeat(ab_irrep, ABLK)
    piece = lax.all_gather(integrals, "col", axis=0, tiled=True)
    masked = jnp.where(block_labels[:, None] == panel_labels[None, :], piece, jnp.zeros_like(piece))
    partial_sum = jnp.dot(amplitudes, masked, preferred_element_type=jnp.float32)
    row_count = lax.axis_size("row")
    row_place = lax.axis_index("row")
    summed = lax.psum_scatter(partial_sum, "row", scatter_dimension=1, tiled=True)
    share = width // row_count
    energy_cols = lax.dynamic_slice_in_dim(panel_energy, row_place * share, share, 0)
    denom = energy_cols[None, :] - pair_energy[:, None]
    return (summed / denom).astype(jnp.bfloat16)


def solution(mesh):
    in_specs = (P("col", "row"), P(("row", "col"), None), P("row"), P(), P("col"), P())
    out_specs = P("col", "row")
    return jax.shard_map(shards, mesh=mesh, in_specs=in_specs, out_specs=out_specs, check_vma=False)
```

profile of v0, /device:TPU:0, one launch (start us, length us, event | category | flops | bytes accessed | tf_op | source)
XLA Modules:
  0.0 137.5 jit_solution(2164292498672394844)
XLA Ops:
  6.5 0.0 copy-start
  6.5 0.0 all-gather.2.cloned.1.call-start
  6.5 0.7 all-gather.2.cloned.1.call-update
  7.3 0.0 reduce-scatter.2.cloned.1.call-start
  7.3 0.7 broadcast_in_dim.12
  8.0 0.1 eq.19
  8.1 0.0 copy-done
  8.1 0.1 broadcast_bitcast_fusion
  8.2 0.0 copy-start.2
  8.2 0.0 copy-start.1
  8.2 40.6 %all-gather.2.cloned.1.call-done = bf16[7936,256]{1,0:T(8,128)(2,1)} async-done(((bf16[496,256]{1,0:T(8,128)(2,1)}), bf16[7936,256]{1,0:T(8,128)(2,1)}) %all-gather.2.cloned.1.call-update) | async-done | bytes 4063248 | tf_op jit(solution)/shard_map/all_gather | solution.py:14
  48.8 8.5 %fusion.4 = f32[384,256]{0,1:T(8,128)} fusion(bf16[384,7936]{1,0:T(8,128)(2,1)} %param.6, bf16[7936,256]{1,0:T(8,128)(2,1)} %all-gather.2.cloned.1.call-done, s32[256]{0:T(256)S(1)} %eq.19, s32[7936]{0:T(1024)S(1)} %broadcast_bitcast_fusion), kind=kOutput, calls=%fused_computation.5 | convolution fusion | flops 1564344320 | bytes 10584064 | tf_op jit(solution)/shard_map/dot_general | solution.py:16
  57.3 0.0 reduce-scatter.2.cloned.1.call-update
  57.3 0.0 copy-done.2
  57.3 0.1 dynamic_slice.3
  57.4 71.8 %reduce-scatter.2.cloned.1.call-done = f32[384,32]{0,1:T(8,128)} async-done(((f32[384,256]{0,1:T(8,128)}), f32[384,32]{0,1:T(8,128)}) %reduce-scatter.2.cloned.1.call-update) | async-done | bytes 49168 | tf_op jit(solution)/shard_map/reduce_scatter | solution.py:19
  129.2 0.0 copy-done.1
  129.2 1.5 %divide_convert_fusion = bf16[384,32]{0,1:T(8,128)(2,1)} fusion(f32[384,32]{0,1:T(8,128)} %reduce-scatter.2.cloned.1.call-done, f32[384]{0:T(512)S(1)} %copy-done.1, f32[32]{0:T(128)S(1)} %dynamic_slice.3), kind=kLoop, calls=%fused_computation.6 | loop fusion | flops 36864 | bytes 75392 | tf_op jit(solution)/shard_map/convert_element_type | solution.py:23
Async XLA Ops:
  6.5 1.6 %copy-start = (s32[62]{0:T(128)S(1)}, s32[62]{0:T(128)}, u32[]{:S(2)}) copy-start(s32[62]{0:T(128)} %param.8) | copy-start | bytes 748
  6.5 42.3 %all-gather.2.cloned.1.call-start = ((), (), s32[]{:S(2)}) async-start(), calls=%async_computation.1 | async-start | bytes 4317184 | tf_op jit(solution)/shard_map/all_gather | solution.py:14
  7.3 121.9 %reduce-scatter.2.cloned.1.call-start = ((), (), s32[]{:S(2)}) async-start(), calls=%async_computation.2 | async-start | bytes 442368 | tf_op jit(solution)/shard_map/reduce_scatter | solution.py:19
  8.2 49.1 %copy-start.2 = (f32[256]{0:T(256)S(1)}, f32[256]{0:T(256)}, u32[]{:S(2)}) copy-start(f32[256]{0:T(256)} %param.11) | copy-start | bytes 3076
  8.2 121.0 %copy-start.1 = (f32[384]{0:T(512)S(1)}, f32[384]{0:T(512)}, u32[]{:S(2)}) copy-start(f32[384]{0:T(512)} %param.10) | copy-start | bytes 4612
Sparse Core Ops, SparseCore 0:
  9.0 39.7 all-gather.1
  57.4 71.7 reduce-scatter.1
where the time goes:
time: 138 us
  waiting for transfers between devices  113 us (82%)
  between operations  13.4 us (10%)
  matrix products  8.47 us (6%)
  other arithmetic  1.49 us (1%)
    reduce_scatter x1, waiting for transfers between devices, shards(): lax.psum_scatter(partial_sum, 'row', scatter_dimension=1, tiled=True)  71.8 us
    all_gather x1, waiting for transfers between devices, shards(): piece = lax.all_gather(integrals, 'col', axis=0, tiled=True)  40.6 us
    dot_general x1, matrix products, shards(): jnp.dot(amplitudes, masked, preferred_element_type=jnp.float32)  8.47 us
  transfers between devices with their start and end apart: 2, of which 2 were waited for; matrix products, arithmetic and copies ran while one was open for 1% of the time, Pallas kernels for 0%

commit v1 on v0

v1 whole, which is shorter than its diff:
```python
import functools

import jax
import jax.numpy as jnp
from jax import lax
from jax.experimental import pallas as pl
from jax.experimental.pallas import tpu as pltpu
from jax.sharding import PartitionSpec as P

KBLK = 128
ABLK = 64
SUB = 16
LANES = 128
VMEM = pltpu.VMEM
SMEM = pltpu.SMEM


def swap_halves(x):
    return jnp.concatenate([x[:, ABLK:], x[:, :ABLK]], axis=1)


def selectors(ab_ref, base):
    lane = lax.broadcasted_iota(jnp.int32, (1, LANES), 1)
    low = lane < ABLK
    rank = []
    for b in range(4):
        count = jnp.int32(-base)
        for earlier in range(b):
            count = count + jnp.where(ab_ref[earlier] == ab_ref[b], 1, 0)
        rank.append(count)
    rows = []
    for t in range(2):
        label = jnp.where(low, ab_ref[2 * t], ab_ref[2 * t + 1])
        slot = jnp.where(low, rank[2 * t], rank[2 * t + 1])
        half = jnp.where(low, 0, 1)
        rows.append((label, slot == half, slot == 1 - half))
    return rows


def factors(row, label):
    own, same, other = row
    match = own == label
    one = lambda m: jnp.where(m, 1.0, 0.0).astype(jnp.bfloat16)
    return one(match & same), one(match & other)


def pack_kernel(base, cd_ref, ab_ref, place_ref, v_ref, o_ref):
    rows = selectors(ab_ref, base)
    subs = v_ref.shape[0] // SUB
    first = place_ref[0] * subs
    for j in range(subs):
        label = cd_ref[(first + j) // (KBLK // SUB)]
        straight = crossed = None
        for t in range(2):
            x = v_ref[j * SUB:(j + 1) * SUB, t * LANES:(t + 1) * LANES]
            same, other = factors(rows[t], label)
            s, c = x * same, x * other
            straight = s if straight is None else straight + s
            crossed = c if crossed is None else crossed + c
        o_ref[j * SUB:(j + 1) * SUB, :] = straight + swap_halves(crossed)


def ladder_kernel(base, cd_ref, ab_ref, place_ref, t_ref, own_ref, other_ref, o_ref, held, masked):
    core = lax.rem(place_ref[0], 2)
    shards = 8
    depth = own_ref.shape[0] // shards
    for k in range(shards):
        for ref, c in ((own_ref, core), (other_ref, 1 - core)):
            at = pl.multiple_of((2 * k + c) * depth, SUB)
            held[pl.ds(at, depth), :] = ref[k * depth:(k + 1) * depth, :]
    rows = selectors(ab_ref, base)
    for blk in range(held.shape[0] // KBLK):
        x = held[blk * KBLK:(blk + 1) * KBLK, :]
        y = swap_halves(x)
        for t in range(2):
            same, other = factors(rows[t], cd_ref[blk])
            masked[blk * KBLK:(blk + 1) * KBLK, t * LANES:(t + 1) * LANES] = x * same + y * other
    total = jnp.dot(t_ref[...], masked[...], preferred_element_type=jnp.float32)
    o_ref[...] = total.T


SAME_CORE = [[2 * i + c for i in range(8)] for c in range(2)]
Z_GROUPS = [[y * 8 + z * 2 + c for z in range(4)] for y in range(2) for c in range(2)]
Y_GROUPS = [[y * 8 + z * 2 + c for y in range(2)] for z in range(4) for c in range(2)]
CORE_SWAP = [(i, i ^ 1) for i in range(16)]
SPREAD = "ag"


def partial_ladder(base, amplitudes, integrals, cd_irrep, ab_irrep, place):
    smem, vmem = pl.BlockSpec(memory_space=SMEM), pl.BlockSpec(memory_space=VMEM)
    depth, width = integrals.shape
    packed = pl.pallas_call(
        functools.partial(pack_kernel, base),
        out_shape=jax.ShapeDtypeStruct((depth, LANES), jnp.bfloat16),
        in_specs=[smem, smem, smem, vmem],
        out_specs=vmem,
        name="pack",
    )(cd_irrep, ab_irrep, place, integrals)
    if SPREAD == "ag":
        own = lax.all_gather(packed, "col", axis=0, tiled=True, axis_index_groups=Y_GROUPS)
        own = lax.all_gather(own.reshape(2, depth, LANES), "col", axis=1, tiled=True, axis_index_groups=Z_GROUPS).reshape(8 * depth, LANES)
    else:
        own = lax.all_to_all(jnp.broadcast_to(packed[None], (8, depth, LANES)), "col", 0, 0, tiled=True, axis_index_groups=SAME_CORE).reshape(8 * depth, LANES)
    other = lax.ppermute(own, "col", CORE_SWAP)
    ij = amplitudes.shape[0]
    cds = amplitudes.shape[1]
    return pl.pallas_call(
        functools.partial(ladder_kernel, base),
        out_shape=jax.ShapeDtypeStruct((width, ij), jnp.float32),
        in_specs=[smem, smem, smem, vmem, vmem, vmem],
        out_specs=vmem,
        scratch_shapes=[VMEM((cds, LANES), jnp.bfloat16), VMEM((cds, width), jnp.bfloat16)],
        compiler_params=pltpu.CompilerParams(vmem_limit_bytes=60 * 2**20),
        cost_estimate=pl.CostEstimate(flops=2 * ij * cds * width, bytes_accessed=2 * ij * cds, transcendentals=0),
        name="ladder",
    )(cd_irrep, ab_irrep, place, amplitudes, own, other)


def shards(amplitudes, integrals, cd_irrep, ab_irrep, pair_energy, panel_energy):
    place = lax.axis_index("col").astype(jnp.int32).reshape(1)
    args = (amplitudes, integrals, cd_irrep, ab_irrep, place)
    partial_sum = partial_ladder(0, *args)
    most = jnp.max(jnp.sum(ab_irrep[:, None] == ab_irrep[None, :], axis=0))
    partial_sum = lax.cond(most > 2, lambda p, *a: p + partial_ladder(2, *a), lambda p, *a: p, partial_sum, *args)
    width = partial_sum.shape[0]
    row_count = lax.axis_size("row")
    share = width // row_count
    parts = lax.all_to_all(partial_sum, "row", 0, 0, tiled=True)
    summed = jnp.sum(parts.reshape(row_count, share, -1), axis=0)
    energy_cols = lax.dynamic_slice_in_dim(panel_energy, lax.axis_index("row") * share, share, 0)
    denom = energy_cols[:, None] - pair_energy[None, :]
    return (summed / denom).astype(jnp.bfloat16).T


def solution(mesh):
    in_specs = (P("col", "row"), P(("row", "col"), None), P("row"), P(), P("col"), P())
    out_specs = P("col", "row")
    return jax.shard_map(shards, mesh=mesh, in_specs=in_specs, out_specs=out_specs, check_vma=False)
```

time: 138 us -> 52.6 us (0.38)
  waiting for transfers between devices: 113 us -> 10.9 us
  blocking collectives: 0 us -> 21.5 us
  between operations: 13.4 us -> 0.71 us
  matrix products: 8.47 us -> 0 us
  Pallas kernels: 0 us -> 8.4 us
  starting transfers between devices: 0.04 us -> 6.95 us
    reduce_scatter x1 -> x0, waiting for transfers between devices: 71.8 us -> none  [shards(): lax.psum_scatter(partial_sum, 'row', scatter_dimension=1, tiled=True)]
    all_gather x1 -> x0, waiting for transfers between devices: 40.6 us -> none  [shards(): piece = lax.all_gather(integrals, 'col', axis=0, tiled=True)]
    all_gather x0 -> x2, blocking collectives: none -> 21.5 us  [the longest x1 15.5 us: partial_ladder(): lax.all_gather(own.reshape(2, depth, LANES), 'col', axis=1, tiled=True, a...]
    all_to_all x0 -> x1, waiting for transfers between devices: none -> 10.4 us  [shards(): parts = lax.all_to_all(partial_sum, 'row', 0, 0, tiled=True)]
    dot_general x1 -> x0, matrix products: 8.47 us -> none  [shards(): jnp.dot(amplitudes, masked, preferred_element_type=jnp.float32)]
    pallas_call x0 -> x2, Pallas kernels: none -> 8.4 us  [the longest x1 6.48 us: partial_ladder(): pl.pallas_call(functools.partial(ladder_kernel, base), out_shape=jax.Shap...]
    all_to_all x0 -> x1, starting transfers between devices: none -> 6.94 us  [shards(): parts = lax.all_to_all(partial_sum, 'row', 0, 0, tiled=True)]
  transfers between devices with their start and end apart: 2 -> 2, of which waited for: 2 -> 2; matrix products, arithmetic and copies ran while one was open for 1% -> 3% of each run, Pallas kernels for 0% -> 0%
where the time goes in v1:
time: 52.6 us; the launch traced here: 51.7 us
  blocking collectives  21.5 us (41%)
  waiting for transfers between devices  10.9 us (21%)
  Pallas kernels  8.4 us (16%)
  starting transfers between devices  6.95 us (13%)
  other arithmetic  2.17 us (4%)
  local copies, waits for them, and re-layouts  1.11 us (2%)
  between operations  0.71 us (1%)
    all_gather x1, blocking collectives, partial_ladder(): lax.all_gather(own.reshape(2, depth, LANES), 'col', axis=1, tiled=True, a...  15.5 us
    all_to_all x1, waiting for transfers between devices, shards(): parts = lax.all_to_all(partial_sum, 'row', 0, 0, tiled=True)  10.4 us
    all_to_all x1, starting transfers between devices, shards(): parts = lax.all_to_all(partial_sum, 'row', 0, 0, tiled=True)  6.94 us
    pallas_call x1, Pallas kernels, partial_ladder(): pl.pallas_call(functools.partial(ladder_kernel, base), out_shape=jax.Shap...  6.48 us
    all_gather x1, blocking collectives, partial_ladder(): lax.all_gather(packed, 'col', axis=0, tiled=True, axis_index_groups=Y_GRO...  6.01 us
    pallas_call x1, Pallas kernels, partial_ladder(): pl.pallas_call(functools.partial(pack_kernel, base), out_shape=jax.ShapeD...  1.92 us
  transfers between devices with their start and end apart: 2, of which 2 were waited for; matrix products, arithmetic and copies ran while one was open for 3% of the time, Pallas kernels for 0%

profile of v1, /device:TPU:0, one launch (start us, length us, event | category | flops | bytes accessed | tf_op | source)
XLA Modules:
  0.0 51.7 jit_solution(3904278484536038488)
XLA Ops:
  0.0 0.0 copy-start.5
  0.0 0.0 copy-start.6
  0.0 0.0 copy-start.4
  0.0 1.9 %pack.3 = bf16[496,128]{1,0:T(8,128)(2,1)} custom-call(s32[62]{0:T(128)} %cd_ref.3, s32[4]{0:T(128)} %ab_ref.3, s32[1]{0:T(128)} %bitcast.2.place_ref, bf16[496,256]{1,0:T(8,128)(2,1)} %v_ref.1), custom_call_target="tpu_custom_call" | custom-call | tf_op jit(solution)/shard_map/pack/pallas_call | solution.py:92
  1.9 6.0 %all_gather.12 = bf16[992,128]{1,0:T(8,128)(2,1)S(1)} all-gather(bf16[496,128]{1,0:T(8,128)(2,1)} %pack.3), channel_id=1, replica_groups={{0,8},{1,9},{2,10},{3,11},{4,12},{5,13},{6,14},{7,15},{16,24},{17,25},{..., dimensions={0}, use_global_device_ids=true | all-gather | bytes 380928 | tf_op jit(solution)/shard_map/all_gather | solution.py:100
  7.9 15.5 %all_gather.13 = bf16[2,1984,128]{2,1,0:T(8,128)(2,1)S(1)} all-gather(bf16[2,496,128]{2,1,0:T(8,128)(2,1)S(1)} %bitcast.14), channel_id=1, replica_groups={{0,2,4,6},{1,3,5,7},{8,10,12,14},{9,11,13,15},{16,18,20,22},{17,19,21,2..., dimensions={1}, use_global_device_ids=true | all-gather | bytes 1269760 | tf_op jit(solution)/shard_map/all_gather | solution.py:101
  23.4 0.0 copy-start
  23.4 0.0 collective-permute-start.1
  23.4 0.8 %convert_reduce_fusion = s32[4]{0:T(128)S(1)} fusion(s32[4]{0:T(128)} %ab_ref.3), kind=kLoop, calls=%fused_computation.2 | loop fusion | flops 44 | bytes 32 | tf_op jit(solution)/shard_map/reduce_sum | solution.py:123
  24.2 0.6 %reduce_max.9 = s32[]{:T(128)} reduce(s32[4]{0:T(128)S(1)} %convert_reduce_fusion, s32[]{:T(128)} %constant.4.clone.1), dimensions={0}, to_apply=%region_1.0 | reduce | flops 3 | bytes 24 | tf_op jit(solution)/shard_map/reduce_max | solution.py:123
  25.5 0.5 collective-permute-done.1.other_ref
  26.0 0.0 copy-done
  26.0 0.0 copy-start.2
  26.0 1.0 %copy-done.2 = bf16[3968,128]{1,0:T(8,128)(2,1)} copy-done((bf16[3968,128]{1,0:T(8,128)(2,1)}, bf16[3968,128]{1,0:T(8,128)(2,1)S(1)}, u32[]{:S(2)}) %copy-start.2) | copy-done | bytes 1015832
  27.0 6.5 %ladder.3 = f32[256,384]{1,0:T(8,128)} custom-call(s32[62]{0:T(128)} %cd_ref.3, s32[4]{0:T(128)} %ab_ref.3, s32[1]{0:T(128)} %bitcast.2.place_ref, bf16[384,7936]{1,0:T(8,128)(2,1)} %t_ref.1, bf16[3968,128]{1,0:T(8,128)(2,1)} %bitcast.11, bf16[3968,128]{1,0:T(8,128)(2,1)} %copy-done.2), custom_call_target="tpu_custom_call" | custom-call | flops 1560281088 | bytes 6094848 | tf_op jit(solution)/shard_map/ladder/pallas_call | solution.py:107
  33.5 0.0 copy-done.5
  33.5 0.0 copy-done.6
  33.5 0.0 copy-done.4
  33.5 0.0 copy-start.8
  33.5 0.0 copy-start.7
  33.6 6.9 %all-to-all-start = ((f32[8,32,384]{2,1,0:T(8,128)}), f32[8,32,384]{2,1,0:T(8,128)S(1)}, u32[]{:S(2)}, u32[]{:S(2)}) async-start(f32[8,32,384]{2,1,0:T(8,128)} %bitcast.5), calls=%async_computation | async-start | bytes 786432 | tf_op jit(solution)/shard_map/all_to_all | solution.py:128
  40.5 0.0 copy-done.8
  40.5 0.1 dynamic_slice.3
  40.6 10.4 %all-to-all-done = f32[8,32,384]{2,1,0:T(8,128)S(1)} async-done(((f32[8,32,384]{2,1,0:T(8,128)}), f32[8,32,384]{2,1,0:T(8,128)S(1)}, u32[]{:S(2)}, u32[]{:S(2)}) %all-to-all-start) | async-done | bytes 393248 | tf_op jit(solution)/shard_map/all_to_all | solution.py:128
  51.0 0.0 copy-done.7
  51.0 0.7 %fusion = bf16[384,32]{0,1:T(8,128)(2,1)} fusion(f32[32,384]{1,0:T(8,128)S(1)} %reduce_sum.21, f32[384]{0:T(512)S(1)} %copy-done.7, f32[32]{0:T(128)S(1)} %dynamic_slice.3), kind=kLoop, calls=%fused_computation.1 | loop fusion | flops 36864 | bytes 75392 | tf_op jit(solution)/shard_map/convert_element_type | solution.py:132
  (2 shorter events, 0.0 us)
Async XLA Ops:
  0.0 33.5 %copy-start.5 = (s32[4]{0:T(128)S(1)}, s32[4]{0:T(128)}, u32[]{:S(2)}) copy-start(s32[4]{0:T(128)} %ab_ref.3) | copy-start | bytes 52
  0.0 33.5 %copy-start.6 = (s32[62]{0:T(128)S(1)}, s32[62]{0:T(128)}, u32[]{:S(2)}) copy-start(s32[62]{0:T(128)} %cd_ref.3) | copy-start | bytes 748
  0.0 33.5 %copy-start.4 = (bf16[496,256]{1,0:T(8,128)(2,1)S(1)}, bf16[496,256]{1,0:T(8,128)(2,1)}, u32[]{:S(2)}) copy-start(bf16[496,256]{1,0:T(8,128)(2,1)} %v_ref.1) | copy-start | bytes 761860
  23.4 2.6 %copy-start = (bf16[2,1984,128]{2,1,0:T(8,128)(2,1)}, bf16[2,1984,128]{2,1,0:T(8,128)(2,1)S(1)}, u32[]{:S(2)}) copy-start(bf16[2,1984,128]{2,1,0:T(8,128)(2,1)S(1)} %all_gather.13) | copy-start | bytes 3047428
  23.4 2.6 %collective-permute-start.1 = (bf16[3968,128]{1,0:T(8,128)(2,1)S(1)}, bf16[3968,128]{1,0:T(8,128)(2,1)S(1)}, u32[]{:S(2)}, u32[]{:S(2)}) collective-permute-start(bf16[3968,128]{1,0:T(8,128)(2,1)S(1)} %bitcast.10), channel_id=1, source_target_pairs={{0,1},{1,0},{2,3},{3,2},{4,5},{5,4},{6,7},{7,6},{8,9},{9,8},{10,11... | collective-permute-start | bytes 3047432 | tf_op jit(solution)/shard_map/ppermute | solution.py:104
  26.0 1.0 %copy-start.2 = (bf16[3968,128]{1,0:T(8,128)(2,1)}, bf16[3968,128]{1,0:T(8,128)(2,1)S(1)}, u32[]{:S(2)}) copy-start(bf16[3968,128]{1,0:T(8,128)(2,1)S(1)} %collective-permute-done.1.other_ref) | copy-start | bytes 3047428
  33.5 7.0 %copy-start.8 = (f32[256]{0:T(256)S(1)}, f32[256]{0:T(256)}, u32[]{:S(2)}) copy-start(f32[256]{0:T(256)} %param.13) | copy-start | bytes 3076
  33.5 17.5 %copy-start.7 = (f32[384]{0:T(512)S(1)}, f32[384]{0:T(512)}, u32[]{:S(2)}) copy-start(f32[384]{0:T(512)} %param.12) | copy-start | bytes 4612
  33.6 17.5 %all-to-all-start = ((f32[8,32,384]{2,1,0:T(8,128)}), f32[8,32,384]{2,1,0:T(8,128)S(1)}, u32[]{:S(2)}, u32[]{:S(2)}) async-start(f32[8,32,384]{2,1,0:T(8,128)} %bitcast.5), calls=%async_computation | async-start | bytes 786432 | tf_op jit(solution)/shard_map/all_to_all | solution.py:128

commit v2 on v0

v2 whole, which is shorter than its diff:
```python
import functools

import jax
import jax.numpy as jnp
from jax import lax
from jax.experimental import pallas as pl
from jax.experimental.pallas import tpu as pltpu
from jax.sharding import PartitionSpec as P


KBLK = 128
ABLK = 64
SUB = 16
LANES = 128
LABELS = 4
VMEM = pltpu.VMEM
SMEM = pltpu.SMEM
IN_SMEM = pl.BlockSpec(memory_space=SMEM)
IN_VMEM = pl.BlockSpec(memory_space=VMEM)


def swap_halves(x):
    return jnp.concatenate([x[:, ABLK:], x[:, :ABLK]], axis=1)


def ranks(ab_ref, base):
    out = []
    for b in range(4):
        count = jnp.int32(-base)
        for earlier in range(b):
            count = count + jnp.where(ab_ref[earlier] == ab_ref[b], 1, 0)
        out.append(count)
    return out


def fill_factors(ab_ref, base, table):
    lane = lax.broadcasted_iota(jnp.int32, (SUB, LANES), 1)
    low = lane < ABLK
    rank = ranks(ab_ref, base)
    for t in range(2):
        own = jnp.where(low, ab_ref[2 * t], ab_ref[2 * t + 1])
        slot = jnp.where(low, rank[2 * t], rank[2 * t + 1])
        half = jnp.where(low, 0, 1)
        for label in range(LABELS):
            for kind, want in enumerate((half, 1 - half)):
                hit = jnp.where(own == label, jnp.where(slot == want, 1.0, 0.0), 0.0)
                table[(label * 2 + t) * 2 + kind] = hit.astype(jnp.bfloat16)


def half_of(t_ref, place_ref, dy, dst, sem):
    cols = dst.shape[1]
    at = pl.multiple_of(half_place(place_ref, dy) * cols, LANES)
    return pltpu.make_async_copy(t_ref.at[:, pl.ds(at, cols)], dst, sem)


def pack_kernel(base, cd_ref, ab_ref, place_ref, v_ref, o_ref, most_ref, table):
    fill_factors(ab_ref, base, table)
    most = jnp.int32(0)
    for count in ranks(ab_ref, 0):
        most = jnp.maximum(most, count)
    most_ref[0] = most + 1
    subs = v_ref.shape[0] // SUB
    first = place_ref[0] * subs
    for j in range(subs):
        label = cd_ref[(first + j) // (KBLK // SUB)]
        straight = crossed = None
        for t in range(2):
            x = v_ref[j * SUB:(j + 1) * SUB, t * LANES:(t + 1) * LANES]
            s, c = x * table[label * 4 + t * 2], x * table[label * 4 + t * 2 + 1]
            straight = s if straight is None else straight + s
            crossed = c if crossed is None else crossed + c
        o_ref[j * SUB:(j + 1) * SUB, :] = straight + swap_halves(crossed)


def pack(base, cd_irrep, ab_irrep, place, integrals):
    return pl.pallas_call(
        functools.partial(pack_kernel, base),
        out_shape=(
            jax.ShapeDtypeStruct((integrals.shape[0], LANES), jnp.bfloat16),
            jax.ShapeDtypeStruct((1,), jnp.int32),
            jax.ShapeDtypeStruct((LABELS * 4, SUB, LANES), jnp.bfloat16),
        ),
        in_specs=[IN_SMEM, IN_SMEM, IN_SMEM, IN_VMEM],
        out_specs=(IN_VMEM, IN_SMEM, IN_VMEM),
        compiler_params=pltpu.CompilerParams(vmem_limit_bytes=2 * 2**20),
        name="pack",
    )(cd_irrep, ab_irrep, place, integrals)


def half_ladder(dy, cd_ref, place_ref, table, piece_refs, held, masked):
    col = place_ref[0]
    core, z = lax.rem(col, 2), lax.rem(col // 2, 4)
    half = half_place(place_ref, dy)
    depth = piece_refs[0].shape[0]
    for n, ref in enumerate(piece_refs):
        dz = STEPS[n % 4]
        from_core = core if n < 4 else 1 - core
        at = (lax.rem(z + 4 - dz, 4) * 2 + from_core) * depth
        held[pl.ds(pl.multiple_of(at, SUB), depth), :] = ref[...]
    blocks = held.shape[0] // KBLK
    for blk in range(blocks):
        at = slice(blk * KBLK, (blk + 1) * KBLK)
        x = held[at, :]
        y = swap_halves(x)
        label = cd_ref[half * blocks + blk]
        for t in range(2):
            same, other = [jnp.concatenate([table[label * 4 + t * 2 + kind]] * (KBLK // SUB), 0) for kind in range(2)]
            masked[at, t * LANES:(t + 1) * LANES] = x * same + y * other


def half_place(place_ref, dy):
    return lax.rem(place_ref[0] // 8 + dy, 2)


def fetch_kernel(place_ref, t_ref, block, rest, sems):
    copies = [half_of(t_ref, place_ref, dy, dst, sems.at[dy]) for dy, dst in enumerate((block, rest))]
    for copy in copies:
        copy.start()
    for copy in copies:
        copy.wait()


def first_kernel(cd_ref, place_ref, table, block, *refs):
    piece_refs = refs[:8]
    o_ref, held, masked = refs[8:]
    half_ladder(0, cd_ref, place_ref, table, piece_refs, held, masked)
    o_ref[...] = jnp.dot(block[...], masked[...], preferred_element_type=jnp.float32)


def last_kernel(cd_ref, place_ref, table, block, before_ref, *refs):
    piece_refs = refs[:8]
    o_ref, held, masked = refs[8:]
    half_ladder(1, cd_ref, place_ref, table, piece_refs, held, masked)
    o_ref[...] = (before_ref[...] + jnp.dot(block[...], masked[...], preferred_element_type=jnp.float32)).T


STEPS = (0, 2, 1, 3)
CORE_SWAP = [(i, i ^ 1) for i in range(16)]


def hop(dy, dz):
    return [(i, ((i // 8 ^ dy) * 4 + (i // 2 + dz) % 4) * 2 + i % 2) for i in range(16)]


def partial_ladder(packed, table, amplitudes, cd_irrep, place):
    across = lax.ppermute(packed, "col", hop(1, 0))
    pieces = []
    for start in (packed, across):
        mine = [start]
        for dz in STEPS[1:]:
            mine.append(lax.ppermute(start, "col", hop(0, dz)))
        theirs = []
        for dz, piece in zip(STEPS, mine):
            theirs.append(lax.ppermute(piece, "col", CORE_SWAP))
        pieces.append(mine + theirs)
    ij, cds = amplitudes.shape
    width, cols = 2 * LANES, cds // 2
    scratch = [VMEM((cols, LANES), jnp.bfloat16), VMEM((cols, width), jnp.bfloat16)]
    cost = pl.CostEstimate(flops=ij * cds * width, bytes_accessed=ij * cds, transcendentals=0)
    limits = pltpu.CompilerParams(vmem_limit_bytes=12 * 2**20)
    block, rest = pl.pallas_call(
        fetch_kernel,
        out_shape=[jax.ShapeDtypeStruct((ij, cols), jnp.bfloat16)] * 2,
        in_specs=[IN_SMEM, pl.BlockSpec(memory_space=pl.ANY)],
        out_specs=[IN_VMEM] * 2,
        scratch_shapes=[pltpu.SemaphoreType.DMA((2,))],
        compiler_params=pltpu.CompilerParams(vmem_limit_bytes=8 * 2**20),
        cost_estimate=pl.CostEstimate(flops=0, bytes_accessed=2 * ij * cds, transcendentals=0),
        name="fetch",
    )(place, amplitudes)
    half = pl.pallas_call(
        first_kernel,
        out_shape=jax.ShapeDtypeStruct((ij, width), jnp.float32),
        in_specs=[IN_SMEM] * 2 + [IN_VMEM] * 10,
        out_specs=IN_VMEM,
        scratch_shapes=scratch,
        compiler_params=limits,
        cost_estimate=cost,
        name="ladder_first",
    )(cd_irrep, place, table, block, *pieces[0])
    return pl.pallas_call(
        last_kernel,
        out_shape=jax.ShapeDtypeStruct((width, ij), jnp.float32),
        in_specs=[IN_SMEM] * 2 + [IN_VMEM] * 11,
        out_specs=IN_VMEM,
        scratch_shapes=scratch,
        compiler_params=limits,
        cost_estimate=cost,
        name="ladder_last",
    )(cd_irrep, place, table, rest, half, *pieces[1])


def shards(amplitudes, integrals, cd_irrep, ab_irrep, pair_energy, panel_energy):
    place = lax.axis_index("col").astype(jnp.int32).reshape(1)
    packed, most, table = pack(0, cd_irrep, ab_irrep, place, integrals)
    partial_sum = partial_ladder(packed, table, amplitudes, cd_irrep, place)

    def more(p, amplitudes, integrals, cd_irrep, ab_irrep, place):
        rest, _, table = pack(2, cd_irrep, ab_irrep, place, integrals)
        return p + partial_ladder(rest, table, amplitudes, cd_irrep, place)

    partial_sum = lax.cond(most[0] > 2, more, lambda p, *a: p, partial_sum, amplitudes, integrals, cd_irrep, ab_irrep, place)
    width = partial_sum.shape[0]
    row_count = lax.axis_size("row")
    share = width // row_count
    parts = lax.all_to_all(partial_sum, "row", 0, 0, tiled=True)
    summed = jnp.sum(parts.reshape(row_count, share, -1), axis=0)
    energy_cols = lax.dynamic_slice_in_dim(panel_energy, lax.axis_index("row") * share, share, 0)
    denom = energy_cols[:, None] - pair_energy[None, :]
    return (summed / denom).astype(jnp.bfloat16).T


def solution(mesh):
    in_specs = (P("col", "row"), P(("row", "col"), None), P("row"), P(), P("col"), P())
    out_specs = P("col", "row")
    return jax.shard_map(shards, mesh=mesh, in_specs=in_specs, out_specs=out_specs, check_vma=False)
```

time: 138 us -> 49.7 us (0.36)
  waiting for transfers between devices: 113 us -> 15.4 us
  starting transfers between devices: 0.04 us -> 23 us
  between operations: 13.4 us -> 0.77 us
  Pallas kernels: 0 us -> 8.94 us
  matrix products: 8.47 us -> 0 us
    reduce_scatter x1 -> x0, waiting for transfers between devices: 71.8 us -> none  [shards(): lax.psum_scatter(partial_sum, 'row', scatter_dimension=1, tiled=True)]
    all_gather x1 -> x0, waiting for transfers between devices: 40.6 us -> none  [shards(): piece = lax.all_gather(integrals, 'col', axis=0, tiled=True)]
    ppermute x0 -> x15, starting transfers between devices: none -> 16.1 us  [the longest x6 12.9 us: partial_ladder(): mine.append(lax.ppermute(start, 'col', hop(0, dz)))]
    all_to_all x0 -> x1, waiting for transfers between devices: none -> 10.3 us  [shards(): parts = lax.all_to_all(partial_sum, 'row', 0, 0, tiled=True)]
    pallas_call x0 -> x4, Pallas kernels: none -> 8.94 us  [the longest x1 2.82 us: partial_ladder(): pl.pallas_call(fetch_kernel, out_shape=[jax.ShapeDtypeStruct((ij, cols),...]
    dot_general x1 -> x0, matrix products: 8.47 us -> none  [shards(): jnp.dot(amplitudes, masked, preferred_element_type=jnp.float32)]
    all_to_all x0 -> x1, starting transfers between devices: none -> 6.94 us  [shards(): parts = lax.all_to_all(partial_sum, 'row', 0, 0, tiled=True)]
    ppermute x0 -> x15, waiting for transfers between devices: none -> 5.11 us  [the longest x6 5.08 us: partial_ladder(): mine.append(lax.ppermute(start, 'col', hop(0, dz)))]
  transfers between devices with their start and end apart: 2 -> 16, of which waited for: 2 -> 4; matrix products, arithmetic and copies ran while one was open for 1% -> 0% of each run, Pallas kernels for 0% -> 9%
where the time goes in v2:
time: 49.7 us; the launch traced here: 48.9 us
  starting transfers between devices  23 us (46%)
  waiting for transfers between devices  15.4 us (31%)
  Pallas kernels  8.94 us (18%)
  between operations  0.77 us (2%)
  other arithmetic  0.72 us (1%)
    ppermute x6, starting transfers between devices, partial_ladder(): mine.append(lax.ppermute(start, 'col', hop(0, dz)))  12.9 us
    all_to_all x1, waiting for transfers between devices, shards(): parts = lax.all_to_all(partial_sum, 'row', 0, 0, tiled=True)  10.3 us
    all_to_all x1, starting transfers between devices, shards(): parts = lax.all_to_all(partial_sum, 'row', 0, 0, tiled=True)  6.94 us
    ppermute x6, waiting for transfers between devices, partial_ladder(): mine.append(lax.ppermute(start, 'col', hop(0, dz)))  5.08 us
    pallas_call x1, Pallas kernels, partial_ladder(): pl.pallas_call(fetch_kernel, out_shape=[jax.ShapeDtypeStruct((ij, cols),...  2.82 us
    pallas_call x1, Pallas kernels, partial_ladder(): pl.pallas_call(last_kernel, out_shape=jax.ShapeDtypeStruct((width, ij), j...  2.64 us
    pallas_call x1, Pallas kernels, partial_ladder(): pl.pallas_call(first_kernel, out_shape=jax.ShapeDtypeStruct((ij, width),...  1.81 us
    pallas_call x1, Pallas kernels, pack(): pl.pallas_call(functools.partial(pack_kernel, base), out_shape=(jax.Shape...  1.67 us
  transfers between devices with their start and end apart: 16, of which 4 were waited for; matrix products, arithmetic and copies ran while one was open for 0% of the time, Pallas kernels for 9%

profile of v2, /device:TPU:0, one launch (start us, length us, event | category | flops | bytes accessed | tf_op | source)
XLA Modules:
  0.0 48.9 jit_solution(925356208675479732)
XLA Ops:
  0.0 1.7 %pack.3 = (bf16[496,128]{1,0:T(8,128)(2,1)S(1)}, s32[1]{0:T(128)}, bf16[16,16,128]{2,1,0:T(8,128)(2,1)S(1)}) custom-call(s32[62]{0:T(128)} %cd_ref.5, s32[4]{0:T(128)} %ab_ref.1, s32[1]{0:T(128)} %bitcast.place_ref, bf16[496,256]{1,0:T(8,128)(2,1)} %v_ref.1), custom_call_target="tpu_custom_call" | custom-call | tf_op jit(solution)/shard_map/pack/pallas_call | solution.py:76
  1.7 4.1 %collective-permute-start.15 = (bf16[496,128]{1,0:T(8,128)(2,1)S(1)}, bf16[496,128]{1,0:T(8,128)(2,1)S(1)}, u32[]{:S(2)}, u32[]{:S(2)}) collective-permute-start(bf16[496,128]{1,0:T(8,128)(2,1)S(1)} %get-tuple-element.40.refs_0_), channel_id=1, source_target_pairs={{0,4},{1,5},{2,6},{3,7},{4,0},{5,1},{6,2},{7,3},{8,12},{9,13},{10,... | collective-permute-start | bytes 380936 | tf_op jit(solution)/shard_map/ppermute | solution.py:151
  5.7 1.0 %collective-permute-start.16 = (bf16[496,128]{1,0:T(8,128)(2,1)S(1)}, bf16[496,128]{1,0:T(8,128)(2,1)S(1)}, u32[]{:S(2)}, u32[]{:S(2)}) collective-permute-start(bf16[496,128]{1,0:T(8,128)(2,1)S(1)} %get-tuple-element.40.refs_0_), channel_id=1, source_target_pairs={{0,2},{1,3},{2,4},{3,5},{4,6},{5,7},{6,0},{7,1},{8,10},{9,11},{10,... | collective-permute-start | bytes 380936 | tf_op jit(solution)/shard_map/ppermute | solution.py:151
  6.8 1.6 %collective-permute-start.22 = (bf16[496,128]{1,0:T(8,128)(2,1)S(1)}, bf16[496,128]{1,0:T(8,128)(2,1)S(1)}, u32[]{:S(2)}, u32[]{:S(2)}) collective-permute-start(bf16[496,128]{1,0:T(8,128)(2,1)S(1)} %get-tuple-element.40.refs_0_), channel_id=1, source_target_pairs={{0,8},{1,9},{2,10},{3,11},{4,12},{5,13},{6,14},{7,15},{8,0},{9,1},... | collective-permute-start | bytes 380936 | tf_op jit(solution)/shard_map/ppermute | solution.py:146
  8.3 2.2 %collective-permute-start.17 = (bf16[496,128]{1,0:T(8,128)(2,1)S(1)}, bf16[496,128]{1,0:T(8,128)(2,1)S(1)}, u32[]{:S(2)}, u32[]{:S(2)}) collective-permute-start(bf16[496,128]{1,0:T(8,128)(2,1)S(1)} %get-tuple-element.40.refs_0_), channel_id=1, source_target_pairs={{0,6},{1,7},{2,0},{3,1},{4,2},{5,3},{6,4},{7,5},{8,14},{9,15},{10,... | collective-permute-start | bytes 380936 | tf_op jit(solution)/shard_map/ppermute | solution.py:151
  10.6 0.0 collective-permute-start.18
  10.6 0.0 collective-permute-done.15.refs_1_
  10.6 0.5 %collective-permute-start.19 = (bf16[496,128]{1,0:T(8,128)(2,1)S(1)}, bf16[496,128]{1,0:T(8,128)(2,1)S(1)}, u32[]{:S(2)}, u32[]{:S(2)}) collective-permute-start(bf16[496,128]{1,0:T(8,128)(2,1)S(1)} %collective-permute-done.15.refs_1_), channel_id=1, source_target_pairs={{0,1},{1,0},{2,3},{3,2},{4,5},{5,4},{6,7},{7,6},{8,9},{9,8},{10,11... | collective-permute-start | bytes 380936 | tf_op jit(solution)/shard_map/ppermute | solution.py:154
  11.1 1.2 %collective-permute-done.16.refs_2_ = bf16[496,128]{1,0:T(8,128)(2,1)S(1)} collective-permute-done((bf16[496,128]{1,0:T(8,128)(2,1)S(1)}, bf16[496,128]{1,0:T(8,128)(2,1)S(1)}, u32[]{:S(2)}, u32[]{:S(2)}) %collective-permute-start.16) | collective-permute-done | bytes 127008 | tf_op jit(solution)/shard_map/ppermute | solution.py:151
  12.3 0.0 collective-permute-start.20
  12.3 0.0 collective-permute-done.22.refs_0_
  12.3 2.4 %collective-permute-start.23 = (bf16[496,128]{1,0:T(8,128)(2,1)S(1)}, bf16[496,128]{1,0:T(8,128)(2,1)S(1)}, u32[]{:S(2)}, u32[]{:S(2)}) collective-permute-start(bf16[496,128]{1,0:T(8,128)(2,1)S(1)} %collective-permute-done.22.refs_0_), channel_id=1, source_target_pairs={{0,4},{1,5},{2,6},{3,7},{4,0},{5,1},{6,2},{7,3},{8,12},{9,13},{10,... | collective-permute-start | bytes 380936 | tf_op jit(solution)/shard_map/ppermute | solution.py:151
  14.7 0.0 collective-permute-done.17.refs_3_
  14.7 0.1 collective-permute-start.24
  14.8 0.0 collective-permute-done.18.refs_4_
  14.8 3.2 %collective-permute-start.25 = (bf16[496,128]{1,0:T(8,128)(2,1)S(1)}, bf16[496,128]{1,0:T(8,128)(2,1)S(1)}, u32[]{:S(2)}, u32[]{:S(2)}) collective-permute-start(bf16[496,128]{1,0:T(8,128)(2,1)S(1)} %collective-permute-done.22.refs_0_), channel_id=1, source_target_pairs={{0,6},{1,7},{2,0},{3,1},{4,2},{5,3},{6,4},{7,5},{8,14},{9,15},{10,... | collective-permute-start | bytes 380936 | tf_op jit(solution)/shard_map/ppermute | solution.py:151
  17.9 0.0 collective-permute-done.19.refs_5_
  17.9 0.0 collective-permute-start.21
  17.9 0.0 collective-permute-done.20.refs_6_
  17.9 0.5 %collective-permute-start.26 = (bf16[496,128]{1,0:T(8,128)(2,1)S(1)}, bf16[496,128]{1,0:T(8,128)(2,1)S(1)}, u32[]{:S(2)}, u32[]{:S(2)}) collective-permute-start(bf16[496,128]{1,0:T(8,128)(2,1)S(1)} %collective-permute-done.22.refs_0_), channel_id=1, source_target_pairs={{0,1},{1,0},{2,3},{3,2},{4,5},{5,4},{6,7},{7,6},{8,9},{9,8},{10,11... | collective-permute-start | bytes 380936 | tf_op jit(solution)/shard_map/ppermute | solution.py:154
  18.5 1.6 %collective-permute-done.23.refs_1_ = bf16[496,128]{1,0:T(8,128)(2,1)S(1)} collective-permute-done((bf16[496,128]{1,0:T(8,128)(2,1)S(1)}, bf16[496,128]{1,0:T(8,128)(2,1)S(1)}, u32[]{:S(2)}, u32[]{:S(2)}) %collective-permute-start.23) | collective-permute-done | bytes 127008 | tf_op jit(solution)/shard_map/ppermute | solution.py:151
  20.1 0.0 collective-permute-start.27
  20.1 2.3 %collective-permute-done.24.refs_2_ = bf16[496,128]{1,0:T(8,128)(2,1)S(1)} collective-permute-done((bf16[496,128]{1,0:T(8,128)(2,1)S(1)}, bf16[496,128]{1,0:T(8,128)(2,1)S(1)}, u32[]{:S(2)}, u32[]{:S(2)}) %collective-permute-start.24) | collective-permute-done | bytes 127008 | tf_op jit(solution)/shard_map/ppermute | solution.py:151
  22.3 0.0 collective-permute-start.28
  22.3 0.0 collective-permute-done.25.refs_3_
  22.3 0.5 %collective-permute-start.29 = (bf16[496,128]{1,0:T(8,128)(2,1)S(1)}, bf16[496,128]{1,0:T(8,128)(2,1)S(1)}, u32[]{:S(2)}, u32[]{:S(2)}) collective-permute-start(bf16[496,128]{1,0:T(8,128)(2,1)S(1)} %collective-permute-done.25.refs_3_), channel_id=1, source_target_pairs={{0,1},{1,0},{2,3},{3,2},{4,5},{5,4},{6,7},{7,6},{8,9},{9,8},{10,11... | collective-permute-start | bytes 380936 | tf_op jit(solution)/shard_map/ppermute | solution.py:154
  23.5 0.0 copy-start.1
  23.5 2.8 %fetch.3 = (bf16[384,3968]{1,0:T(8,128)(2,1)S(1)}, bf16[384,3968]{1,0:T(8,128)(2,1)S(1)}) custom-call(s32[1]{0:T(128)} %bitcast.place_ref, bf16[384,7936]{1,0:T(8,128)(2,1)} %t_ref.1), custom_call_target="tpu_custom_call" | custom-call | bytes 6094848 | tf_op jit(solution)/shard_map/fetch/pallas_call | solution.py:161
  26.3 0.0 collective-permute-done.21.refs_7_
  26.3 0.0 copy-done.1
  26.3 1.8 %ladder_first.3.before_ref = f32[384,256]{1,0:T(8,128)S(1)} custom-call(s32[62]{0:T(128)S(1)} %copy-done.1, s32[1]{0:T(128)} %bitcast.place_ref, bf16[16,16,128]{2,1,0:T(8,128)(2,1)S(1)} %get-tuple-element.37.table, bf16[384,3968]{1,0:T(8,128)(2,1)S(1)} %get-tuple-element.39.block, bf16[496,128]{1,0:T(8,128)(2,1)S(1)} %get-tuple-element.40.refs_0_, ...), custom_call_target="tpu_custom_call" | custom-call | flops 780140544 | bytes 3047424 | tf_op jit(solution)/shard_map/ladder_first/pallas_call | solution.py:171
  28.2 0.0 copy-start
  28.2 0.0 copy-start.2
  28.2 0.0 collective-permute-done.26.refs_4_
  28.2 0.0 collective-permute-done.27.refs_5_
  28.2 0.0 collective-permute-done.28.refs_6_
  28.2 0.0 collective-permute-done.29.refs_7_
  28.2 2.6 %ladder_last.3 = f32[256,384]{1,0:T(8,128)} custom-call(s32[62]{0:T(128)S(1)} %copy-done.1, s32[1]{0:T(128)} %bitcast.place_ref, bf16[16,16,128]{2,1,0:T(8,128)(2,1)S(1)} %get-tuple-element.37.table, bf16[384,3968]{1,0:T(8,128)(2,1)S(1)} %get-tuple-element.38.block, f32[384,256]{1,0:T(8,128)S(1)} %ladder_first.3.before_ref, ...), custom_call_target="tpu_custom_call" | custom-call | flops 780140544 | bytes 3047424 | tf_op jit(solution)/shard_map/ladder_last/pallas_call | solution.py:181
  30.9 0.0 copy-done
  30.9 0.0 copy-done.2
  30.9 0.0 copy-start.4
  30.9 0.0 copy-start.3
  30.9 6.9 %all-to-all-start = ((f32[8,32,384]{2,1,0:T(8,128)}), f32[8,32,384]{2,1,0:T(8,128)S(1)}, u32[]{:S(2)}, u32[]{:S(2)}) async-start(f32[8,32,384]{2,1,0:T(8,128)} %bitcast.2), calls=%async_computation | async-start | bytes 786432 | tf_op jit(solution)/shard_map/all_to_all | solution.py:206
  37.8 0.0 copy-done.4
  37.8 0.1 dynamic_slice.3
  37.9 10.3 %all-to-all-done = f32[8,32,384]{2,1,0:T(8,128)S(1)} async-done(((f32[8,32,384]{2,1,0:T(8,128)}), f32[8,32,384]{2,1,0:T(8,128)S(1)}, u32[]{:S(2)}, u32[]{:S(2)}) %all-to-all-start) | async-done | bytes 393248 | tf_op jit(solution)/shard_map/all_to_all | solution.py:206
  48.2 0.0 copy-done.3
  48.2 0.7 %fusion = bf16[384,32]{0,1:T(8,128)(2,1)} fusion(f32[32,384]{1,0:T(8,128)S(1)} %reduce_sum.11, f32[384]{0:T(512)S(1)} %copy-done.3, f32[32]{0:T(128)S(1)} %dynamic_slice.3), kind=kLoop, calls=%fused_computation.1 | loop fusion | flops 36864 | bytes 75392 | tf_op jit(solution)/shard_map/convert_element_type | solution.py:210
  (2 shorter events, 0.0 us)
Async XLA Ops:
  1.7 8.9 %collective-permute-start.15 = (bf16[496,128]{1,0:T(8,128)(2,1)S(1)}, bf16[496,128]{1,0:T(8,128)(2,1)S(1)}, u32[]{:S(2)}, u32[]{:S(2)}) collective-permute-start(bf16[496,128]{1,0:T(8,128)(2,1)S(1)} %get-tuple-element.40.refs_0_), channel_id=1, source_target_pairs={{0,4},{1,5},{2,6},{3,7},{4,0},{5,1},{6,2},{7,3},{8,12},{9,13},{10,... | collective-permute-start | bytes 380936 | tf_op jit(solution)/shard_map/ppermute | solution.py:151
  5.7 6.5 %collective-permute-start.16 = (bf16[496,128]{1,0:T(8,128)(2,1)S(1)}, bf16[496,128]{1,0:T(8,128)(2,1)S(1)}, u32[]{:S(2)}, u32[]{:S(2)}) collective-permute-start(bf16[496,128]{1,0:T(8,128)(2,1)S(1)} %get-tuple-element.40.refs_0_), channel_id=1, source_target_pairs={{0,2},{1,3},{2,4},{3,5},{4,6},{5,7},{6,0},{7,1},{8,10},{9,11},{10,... | collective-permute-start | bytes 380936 | tf_op jit(solution)/shard_map/ppermute | solution.py:151
  6.8 5.5 %collective-permute-start.22 = (bf16[496,128]{1,0:T(8,128)(2,1)S(1)}, bf16[496,128]{1,0:T(8,128)(2,1)S(1)}, u32[]{:S(2)}, u32[]{:S(2)}) collective-permute-start(bf16[496,128]{1,0:T(8,128)(2,1)S(1)} %get-tuple-element.40.refs_0_), channel_id=1, source_target_pairs={{0,8},{1,9},{2,10},{3,11},{4,12},{5,13},{6,14},{7,15},{8,0},{9,1},... | collective-permute-start | bytes 380936 | tf_op jit(solution)/shard_map/ppermute | solution.py:146
  8.3 6.3 %collective-permute-start.17 = (bf16[496,128]{1,0:T(8,128)(2,1)S(1)}, bf16[496,128]{1,0:T(8,128)(2,1)S(1)}, u32[]{:S(2)}, u32[]{:S(2)}) collective-permute-start(bf16[496,128]{1,0:T(8,128)(2,1)S(1)} %get-tuple-element.40.refs_0_), channel_id=1, source_target_pairs={{0,6},{1,7},{2,0},{3,1},{4,2},{5,3},{6,4},{7,5},{8,14},{9,15},{10,... | collective-permute-start | bytes 380936 | tf_op jit(solution)/shard_map/ppermute | solution.py:151
  10.6 4.2 %collective-permute-start.18 = (bf16[496,128]{1,0:T(8,128)(2,1)S(1)}, bf16[496,128]{1,0:T(8,128)(2,1)S(1)}, u32[]{:S(2)}, u32[]{:S(2)}) collective-permute-start(bf16[496,128]{1,0:T(8,128)(2,1)S(1)} %get-tuple-element.40.refs_0_), channel_id=1, source_target_pairs={{0,1},{1,0},{2,3},{3,2},{4,5},{5,4},{6,7},{7,6},{8,9},{9,8},{10,11... | collective-permute-start | bytes 380936 | tf_op jit(solution)/shard_map/ppermute | solution.py:154
  10.6 7.4 %collective-permute-start.19 = (bf16[496,128]{1,0:T(8,128)(2,1)S(1)}, bf16[496,128]{1,0:T(8,128)(2,1)S(1)}, u32[]{:S(2)}, u32[]{:S(2)}) collective-permute-start(bf16[496,128]{1,0:T(8,128)(2,1)S(1)} %collective-permute-done.15.refs_1_), channel_id=1, source_target_pairs={{0,1},{1,0},{2,3},{3,2},{4,5},{5,4},{6,7},{7,6},{8,9},{9,8},{10,11... | collective-permute-start | bytes 380936 | tf_op jit(solution)/shard_map/ppermute | solution.py:154
  12.3 5.7 %collective-permute-start.20 = (bf16[496,128]{1,0:T(8,128)(2,1)S(1)}, bf16[496,128]{1,0:T(8,128)(2,1)S(1)}, u32[]{:S(2)}, u32[]{:S(2)}) collective-permute-start(bf16[496,128]{1,0:T(8,128)(2,1)S(1)} %collective-permute-done.16.refs_2_), channel_id=1, source_target_pairs={{0,1},{1,0},{2,3},{3,2},{4,5},{5,4},{6,7},{7,6},{8,9},{9,8},{10,11... | collective-permute-start | bytes 380936 | tf_op jit(solution)/shard_map/ppermute | solution.py:154
  12.3 7.8 %collective-permute-start.23 = (bf16[496,128]{1,0:T(8,128)(2,1)S(1)}, bf16[496,128]{1,0:T(8,128)(2,1)S(1)}, u32[]{:S(2)}, u32[]{:S(2)}) collective-permute-start(bf16[496,128]{1,0:T(8,128)(2,1)S(1)} %collective-permute-done.22.refs_0_), channel_id=1, source_target_pairs={{0,4},{1,5},{2,6},{3,7},{4,0},{5,1},{6,2},{7,3},{8,12},{9,13},{10,... | collective-permute-start | bytes 380936 | tf_op jit(solution)/shard_map/ppermute | solution.py:151
  14.7 7.6 %collective-permute-start.24 = (bf16[496,128]{1,0:T(8,128)(2,1)S(1)}, bf16[496,128]{1,0:T(8,128)(2,1)S(1)}, u32[]{:S(2)}, u32[]{:S(2)}) collective-permute-start(bf16[496,128]{1,0:T(8,128)(2,1)S(1)} %collective-permute-done.22.refs_0_), channel_id=1, source_target_pairs={{0,2},{1,3},{2,4},{3,5},{4,6},{5,7},{6,0},{7,1},{8,10},{9,11},{10,... | collective-permute-start | bytes 380936 | tf_op jit(solution)/shard_map/ppermute | solution.py:151
  14.8 7.6 %collective-permute-start.25 = (bf16[496,128]{1,0:T(8,128)(2,1)S(1)}, bf16[496,128]{1,0:T(8,128)(2,1)S(1)}, u32[]{:S(2)}, u32[]{:S(2)}) collective-permute-start(bf16[496,128]{1,0:T(8,128)(2,1)S(1)} %collective-permute-done.22.refs_0_), channel_id=1, source_target_pairs={{0,6},{1,7},{2,0},{3,1},{4,2},{5,3},{6,4},{7,5},{8,14},{9,15},{10,... | collective-permute-start | bytes 380936 | tf_op jit(solution)/shard_map/ppermute | solution.py:151
  17.9 8.4 %collective-permute-start.21 = (bf16[496,128]{1,0:T(8,128)(2,1)S(1)}, bf16[496,128]{1,0:T(8,128)(2,1)S(1)}, u32[]{:S(2)}, u32[]{:S(2)}) collective-permute-start(bf16[496,128]{1,0:T(8,128)(2,1)S(1)} %collective-permute-done.17.refs_3_), channel_id=1, source_target_pairs={{0,1},{1,0},{2,3},{3,2},{4,5},{5,4},{6,7},{7,6},{8,9},{9,8},{10,11... | collective-permute-start | bytes 380936 | tf_op jit(solution)/shard_map/ppermute | solution.py:154
  17.9 10.2 %collective-permute-start.26 = (bf16[496,128]{1,0:T(8,128)(2,1)S(1)}, bf16[496,128]{1,0:T(8,128)(2,1)S(1)}, u32[]{:S(2)}, u32[]{:S(2)}) collective-permute-start(bf16[496,128]{1,0:T(8,128)(2,1)S(1)} %collective-permute-done.22.refs_0_), channel_id=1, source_target_pairs={{0,1},{1,0},{2,3},{3,2},{4,5},{5,4},{6,7},{7,6},{8,9},{9,8},{10,11... | collective-permute-start | bytes 380936 | tf_op jit(solution)/shard_map/ppermute | solution.py:154
  20.1 8.1 %collective-permute-start.27 = (bf16[496,128]{1,0:T(8,128)(2,1)S(1)}, bf16[496,128]{1,0:T(8,128)(2,1)S(1)}, u32[]{:S(2)}, u32[]{:S(2)}) collective-permute-start(bf16[496,128]{1,0:T(8,128)(2,1)S(1)} %collective-permute-done.23.refs_1_), channel_id=1, source_target_pairs={{0,1},{1,0},{2,3},{3,2},{4,5},{5,4},{6,7},{7,6},{8,9},{9,8},{10,11... | collective-permute-start | bytes 380936 | tf_op jit(solution)/shard_map/ppermute | solution.py:154
  22.3 5.9 %collective-permute-start.28 = (bf16[496,128]{1,0:T(8,128)(2,1)S(1)}, bf16[496,128]{1,0:T(8,128)(2,1)S(1)}, u32[]{:S(2)}, u32[]{:S(2)}) collective-permute-start(bf16[496,128]{1,0:T(8,128)(2,1)S(1)} %collective-permute-done.24.refs_2_), channel_id=1, source_target_pairs={{0,1},{1,0},{2,3},{3,2},{4,5},{5,4},{6,7},{7,6},{8,9},{9,8},{10,11... | collective-permute-start | bytes 380936 | tf_op jit(solution)/shard_map/ppermute | solution.py:154
  22.3 5.9 %collective-permute-start.29 = (bf16[496,128]{1,0:T(8,128)(2,1)S(1)}, bf16[496,128]{1,0:T(8,128)(2,1)S(1)}, u32[]{:S(2)}, u32[]{:S(2)}) collective-permute-start(bf16[496,128]{1,0:T(8,128)(2,1)S(1)} %collective-permute-done.25.refs_3_), channel_id=1, source_target_pairs={{0,1},{1,0},{2,3},{3,2},{4,5},{5,4},{6,7},{7,6},{8,9},{9,8},{10,11... | collective-permute-start | bytes 380936 | tf_op jit(solution)/shard_map/ppermute | solution.py:154
  23.5 2.9 %copy-start.1 = (s32[62]{0:T(128)S(1)}, s32[62]{0:T(128)}, u32[]{:S(2)}) copy-start(s32[62]{0:T(128)} %cd_ref.5) | copy-start | bytes 748
  28.2 2.7 %copy-start = (bf16[496,256]{1,0:T(8,128)(2,1)S(1)}, bf16[496,256]{1,0:T(8,128)(2,1)}, u32[]{:S(2)}) copy-start(bf16[496,256]{1,0:T(8,128)(2,1)} %v_ref.1) | copy-start | bytes 761860
  28.2 2.7 %copy-start.2 = (s32[4]{0:T(128)S(1)}, s32[4]{0:T(128)}, u32[]{:S(2)}) copy-start(s32[4]{0:T(128)} %ab_ref.1) | copy-start | bytes 52
  30.9 7.0 %copy-start.4 = (f32[256]{0:T(256)S(1)}, f32[256]{0:T(256)}, u32[]{:S(2)}) copy-start(f32[256]{0:T(256)} %param.13) | copy-start | bytes 3076
  30.9 17.3 %copy-start.3 = (f32[384]{0:T(512)S(1)}, f32[384]{0:T(512)}, u32[]{:S(2)}) copy-start(f32[384]{0:T(512)} %param.12) | copy-start | bytes 4612
  30.9 17.3 %all-to-all-start = ((f32[8,32,384]{2,1,0:T(8,128)}), f32[8,32,384]{2,1,0:T(8,128)S(1)}, u32[]{:S(2)}, u32[]{:S(2)}) async-start(f32[8,32,384]{2,1,0:T(8,128)} %bitcast.2), calls=%async_computation | async-start | bytes 786432 | tf_op jit(solution)/shard_map/all_to_all | solution.py:206

commit v3 on v2

--- a/solution.py
+++ b/solution.py
@@ -45,12 +45,6 @@
             for kind, want in enumerate((half, 1 - half)):
                 hit = jnp.where(own == label, jnp.where(slot == want, 1.0, 0.0), 0.0)
                 table[(label * 2 + t) * 2 + kind] = hit.astype(jnp.bfloat16)
-
-
-def half_of(t_ref, place_ref, dy, dst, sem):
-    cols = dst.shape[1]
-    at = pl.multiple_of(half_place(place_ref, dy) * cols, LANES)
-    return pltpu.make_async_copy(t_ref.at[:, pl.ds(at, cols)], dst, sem)
 
 
 def pack_kernel(base, cd_ref, ab_ref, place_ref, v_ref, o_ref, most_ref, table):
@@ -83,6 +77,7 @@
         in_specs=[IN_SMEM, IN_SMEM, IN_SMEM, IN_VMEM],
         out_specs=(IN_VMEM, IN_SMEM, IN_VMEM),
         compiler_params=pltpu.CompilerParams(vmem_limit_bytes=2 * 2**20),
+        cost_estimate=pl.CostEstimate(flops=10**10, bytes_accessed=2 * integrals.size, transcendentals=0),
         name="pack",
     )(cd_irrep, ab_irrep, place, integrals)
 
@@ -112,26 +107,44 @@
     return lax.rem(place_ref[0] // 8 + dy, 2)
 
 
-def fetch_kernel(place_ref, t_ref, block, rest, sems):
-    copies = [half_of(t_ref, place_ref, dy, dst, sems.at[dy]) for dy, dst in enumerate((block, rest))]
-    for copy in copies:
-        copy.start()
-    for copy in copies:
-        copy.wait()
-
-
-def first_kernel(cd_ref, place_ref, table, block, *refs):
+def half_product(dy, place_ref, t_ref, masked):
+    depth = masked.shape[0]
+    cols = pl.ds(pl.multiple_of(half_place(place_ref, dy) * depth, LANES), depth)
+    return jnp.dot(t_ref[:, cols], masked[...], preferred_element_type=jnp.float32)
+
+
+def first_kernel(cd_ref, place_ref, table, t_ref, *refs):
     piece_refs = refs[:8]
     o_ref, held, masked = refs[8:]
     half_ladder(0, cd_ref, place_ref, table, piece_refs, held, masked)
-    o_ref[...] = jnp.dot(block[...], masked[...], preferred_element_type=jnp.float32)
-
-
-def last_kernel(cd_ref, place_ref, table, block, before_ref, *refs):
-    piece_refs = refs[:8]
-    o_ref, held, masked = refs[8:]
+    o_ref[...] = half_product(0, place_ref, t_ref, masked)
+
+
+def last_kernel(cd_ref, place_ref, table, t_ref, before_ref, *refs):
+    piece_refs, out_refs = refs[:8], refs[8:16]
+    held, masked, total = refs[16:]
     half_ladder(1, cd_ref, place_ref, table, piece_refs, held, masked)
-    o_ref[...] = (before_ref[...] + jnp.dot(block[...], masked[...], preferred_element_type=jnp.float32)).T
+    total[...] = (before_ref[...] + half_product(1, place_ref, t_ref, masked)).T
+    row = place_ref[1]
+    y, x = row // 4, lax.rem(row, 4)
+    for (dy, dx), ref in zip(TARGETS, out_refs):
+        target = lax.rem(y + dy, 2) * 4 + lax.rem(x + dx, 4)
+        share = ref.shape[0]
+        ref[...] = total[pl.ds(pl.multiple_of(target * share, 8), share), :]
+
+
+TARGETS = [(0, 0), (1, 2), (1, 1), (1, 3), (1, 0), (0, 2), (0, 1), (0, 3)]
+
+
+def row_hop(dy, dx):
+    return [(i, (i // 4 ^ dy) * 4 + (i % 4 + dx) % 4) for i in range(8)]
+
+
+def reduce_parts(blocks):
+    parts = [blocks[0]]
+    for n, block in enumerate(blocks[1:], 1):
+        parts.append(lax.ppermute(block, "row", row_hop(*TARGETS[n])))
+    return parts
 
 
 STEPS = (0, 2, 1, 3)
@@ -158,16 +171,6 @@
     scratch = [VMEM((cols, LANES), jnp.bfloat16), VMEM((cols, width), jnp.bfloat16)]
     cost = pl.CostEstimate(flops=ij * cds * width, bytes_accessed=ij * cds, transcendentals=0)
     limits = pltpu.CompilerParams(vmem_limit_bytes=12 * 2**20)
-    block, rest = pl.pallas_call(
-        fetch_kernel,
-        out_shape=[jax.ShapeDtypeStruct((ij, cols), jnp.bfloat16)] * 2,
-        in_specs=[IN_SMEM, pl.BlockSpec(memory_space=pl.ANY)],
-        out_specs=[IN_VMEM] * 2,
-        scratch_shapes=[pltpu.SemaphoreType.DMA((2,))],
-        compiler_params=pltpu.CompilerParams(vmem_limit_bytes=8 * 2**20),
-        cost_estimate=pl.CostEstimate(flops=0, bytes_accessed=2 * ij * cds, transcendentals=0),
-        name="fetch",
-    )(place, amplitudes)
     half = pl.pallas_call(
         first_kernel,
         out_shape=jax.ShapeDtypeStruct((ij, width), jnp.float32),
@@ -177,37 +180,42 @@
         compiler_params=limits,
         cost_estimate=cost,
         name="ladder_first",
-    )(cd_irrep, place, table, block, *pieces[0])
+    )(cd_irrep, place, table, amplitudes, *pieces[0])
     return pl.pallas_call(
         last_kernel,
-        out_shape=jax.ShapeDtypeStruct((width, ij), jnp.float32),
+        out_shape=[jax.ShapeDtypeStruct((width // 8, ij), jnp.float32)] * 8,
         in_specs=[IN_SMEM] * 2 + [IN_VMEM] * 11,
-        out_specs=IN_VMEM,
-        scratch_shapes=scratch,
+        out_specs=[IN_VMEM] * 8,
+        scratch_shapes=scratch + [VMEM((width, ij), jnp.float32)],
         compiler_params=limits,
         cost_estimate=cost,
         name="ladder_last",
-    )(cd_irrep, place, table, rest, half, *pieces[1])
+    )(cd_irrep, place, table, amplitudes, half, *pieces[1])
 
 
 def shards(amplitudes, integrals, cd_irrep, ab_irrep, pair_energy, panel_energy):
-    place = lax.axis_index("col").astype(jnp.int32).reshape(1)
+    place = jnp.stack([lax.axis_index("col"), lax.axis_index("row")]).astype(jnp.int32)
     packed, most, table = pack(0, cd_irrep, ab_irrep, place, integrals)
-    partial_sum = partial_ladder(packed, table, amplitudes, cd_irrep, place)
-
-    def more(p, amplitudes, integrals, cd_irrep, ab_irrep, place):
+    parts = reduce_parts(partial_ladder(packed, table, amplitudes, cd_irrep, place))
+
+    def finish(parts, pair_energy, panel_energy):
+        share = parts[0].shape[0]
+        summed = sum(parts[1:], parts[0])
+        energy_cols = lax.dynamic_slice_in_dim(panel_energy, lax.axis_index("row") * share, share, 0)
+        denom = energy_cols[:, None] - pair_energy[None, :]
+        return (summed / denom).astype(jnp.bfloat16).T
+
+    def more(parts, pair_energy, panel_energy, amplitudes, integrals, cd_irrep, ab_irrep, place):
         rest, _, table = pack(2, cd_irrep, ab_irrep, place, integrals)
-        return p + partial_ladder(rest, table, amplitudes, cd_irrep, place)
-
-    partial_sum = lax.cond(most[0] > 2, more, lambda p, *a: p, partial_sum, amplitudes, integrals, cd_irrep, ab_irrep, place)
-    width = partial_sum.shape[0]
-    row_count = lax.axis_size("row")
-    share = width // row_count
-    parts = lax.all_to_all(partial_sum, "row", 0, 0, tiled=True)
-    summed = jnp.sum(parts.reshape(row_count, share, -1), axis=0)
-    energy_cols = lax.dynamic_slice_in_dim(panel_energy, lax.axis_index("row") * share, share, 0)
-    denom = energy_cols[:, None] - pair_energy[None, :]
-    return (summed / denom).astype(jnp.bfloat16).T
+        extra = reduce_parts(partial_ladder(rest, table, amplitudes, cd_irrep, place))
+        return finish([p + e for p, e in zip(parts, extra)], pair_energy, panel_energy)
+
+    def enough(parts, pair_energy, panel_energy, *unused):
+        return finish(parts, pair_energy, panel_energy)
+
+    parts = lax.optimization_barrier(parts)
+    operands = (parts, pair_energy, panel_energy, amplitudes, integrals, cd_irrep, ab_irrep, place)
+    return lax.cond(most[0] > 2, more, enough, *operands)
 
 
 def solution(mesh):

time: 49.7 us -> 45.8 us (0.922); the launches traced: 48.9 us -> 45.6 us
  waiting for transfers between devices: 15.4 us -> 7.67 us
  starting transfers between devices: 23 us -> 30.4 us
  Pallas kernels: 8.94 us -> 5.62 us
  local copies, waits for them, and re-layouts: 0.1 us -> 0.71 us
  other arithmetic: 0.72 us -> 0.16 us
    ppermute x0 -> x7, starting transfers between devices: none -> 14.3 us  [reduce_parts(): parts.append(lax.ppermute(block, 'row', row_hop(*TARGETS[n])))]
    all_to_all x1 -> x0, waiting for transfers between devices: 10.3 us -> none  [shards(): parts = lax.all_to_all(partial_sum, 'row', 0, 0, tiled=True)]
    all_to_all x1 -> x0, starting transfers between devices: 6.94 us -> none  [shards(): parts = lax.all_to_all(partial_sum, 'row', 0, 0, tiled=True)]
    pallas_call x2 -> x1, Pallas kernels: 5.46 us -> 1.98 us  [partial_ladder(): pl.pallas_call(last_kernel, out_shape=[jax.ShapeDtypeStruct((width // 8,...]
    ppermute x0 -> x7, waiting for transfers between devices: none -> 2.56 us  [reduce_parts(): parts.append(lax.ppermute(block, 'row', row_hop(*TARGETS[n])))]
    convert_element_type x1 -> x0, other arithmetic: 0.69 us -> none  [shards(): return (summed / denom).astype(jnp.bfloat16).T]
    unnamed x10 -> x14, local copies, waits for them, and re-layouts: 0.03 us -> 0.64 us
  transfers between devices with their start and end apart: 16 -> 22, of which waited for: 4 -> 7; matrix products, arithmetic and copies ran while one was open for 0% -> 0% of each run, Pallas kernels for 9% -> 4%
where the time goes in v3:
time: 45.8 us; the launch traced here: 45.6 us
  starting transfers between devices  30.4 us (66%)
  waiting for transfers between devices  7.67 us (17%)
  Pallas kernels  5.62 us (12%)
  between operations  0.81 us (2%)
  local copies, waits for them, and re-layouts  0.71 us (2%)
    ppermute x7, starting transfers between devices, reduce_parts(): parts.append(lax.ppermute(block, 'row', row_hop(*TARGETS[n])))  14.3 us
    ppermute x6, starting transfers between devices, partial_ladder(): mine.append(lax.ppermute(start, 'col', hop(0, dz)))  12.9 us
    ppermute x6, waiting for transfers between devices, partial_ladder(): mine.append(lax.ppermute(start, 'col', hop(0, dz)))  5.08 us
    ppermute x7, waiting for transfers between devices, reduce_parts(): parts.append(lax.ppermute(block, 'row', row_hop(*TARGETS[n])))  2.56 us
    pallas_call x1, Pallas kernels, partial_ladder(): pl.pallas_call(last_kernel, out_shape=[jax.ShapeDtypeStruct((width // 8,...  1.98 us
    pallas_call x1, Pallas kernels, pack(): pl.pallas_call(functools.partial(pack_kernel, base), out_shape=(jax.Shape...  1.83 us
    pallas_call x1, Pallas kernels, partial_ladder(): pl.pallas_call(first_kernel, out_shape=jax.ShapeDtypeStruct((ij, width),...  1.81 us
    ppermute x1, starting transfers between devices, partial_ladder(): across = lax.ppermute(packed, 'col', hop(1, 0))  1.58 us
  transfers between devices with their start and end apart: 22, of which 7 were waited for; matrix products, arithmetic and copies ran while one was open for 0% of the time, Pallas kernels for 4%

profile of v3, /device:TPU:0, one launch (start us, length us, event | category | flops | bytes accessed | tf_op | source)
XLA Modules:
  0.0 45.6 jit_solution(5497023850214090975)
XLA Ops:
  0.0 0.1 pad_add_fusion.place_ref
  0.1 0.0 copy-start
  0.1 1.8 %pack.3 = (bf16[496,128]{1,0:T(8,128)(2,1)S(1)}, s32[1]{0:T(128)}, bf16[16,16,128]{2,1,0:T(8,128)(2,1)S(1)}) custom-call(s32[62]{0:T(128)} %cd_ref.5, s32[4]{0:T(128)} %ab_ref.1, s32[2]{0:T(128)S(1)} %pad_add_fusion.place_ref, bf16[496,256]{1,0:T(8,128)(2,1)} %v_ref.1), custom_call_target="tpu_custom_call" | custom-call | flops 10000000000 | bytes 253952 | tf_op jit(solution)/shard_map/pack/pallas_call | solution.py:70
  1.9 4.1 %collective-permute-start.22 = (bf16[496,128]{1,0:T(8,128)(2,1)S(1)}, bf16[496,128]{1,0:T(8,128)(2,1)S(1)}, u32[]{:S(2)}, u32[]{:S(2)}) collective-permute-start(bf16[496,128]{1,0:T(8,128)(2,1)S(1)} %get-tuple-element.114.refs_0_), channel_id=1, source_target_pairs={{0,4},{1,5},{2,6},{3,7},{4,0},{5,1},{6,2},{7,3},{8,12},{9,13},{10,... | collective-permute-start | bytes 380936 | tf_op jit(solution)/shard_map/ppermute | solution.py:164
  6.0 1.0 %collective-permute-start.23 = (bf16[496,128]{1,0:T(8,128)(2,1)S(1)}, bf16[496,128]{1,0:T(8,128)(2,1)S(1)}, u32[]{:S(2)}, u32[]{:S(2)}) collective-permute-start(bf16[496,128]{1,0:T(8,128)(2,1)S(1)} %get-tuple-element.114.refs_0_), channel_id=1, source_target_pairs={{0,2},{1,3},{2,4},{3,5},{4,6},{5,7},{6,0},{7,1},{8,10},{9,11},{10,... | collective-permute-start | bytes 380936 | tf_op jit(solution)/shard_map/ppermute | solution.py:164
  7.0 1.6 %collective-permute-start.29 = (bf16[496,128]{1,0:T(8,128)(2,1)S(1)}, bf16[496,128]{1,0:T(8,128)(2,1)S(1)}, u32[]{:S(2)}, u32[]{:S(2)}) collective-permute-start(bf16[496,128]{1,0:T(8,128)(2,1)S(1)} %get-tuple-element.114.refs_0_), channel_id=1, source_target_pairs={{0,8},{1,9},{2,10},{3,11},{4,12},{5,13},{6,14},{7,15},{8,0},{9,1},... | collective-permute-start | bytes 380936 | tf_op jit(solution)/shard_map/ppermute | solution.py:159
  8.6 2.2 %collective-permute-start.24 = (bf16[496,128]{1,0:T(8,128)(2,1)S(1)}, bf16[496,128]{1,0:T(8,128)(2,1)S(1)}, u32[]{:S(2)}, u32[]{:S(2)}) collective-permute-start(bf16[496,128]{1,0:T(8,128)(2,1)S(1)} %get-tuple-element.114.refs_0_), channel_id=1, source_target_pairs={{0,6},{1,7},{2,0},{3,1},{4,2},{5,3},{6,4},{7,5},{8,14},{9,15},{10,... | collective-permute-start | bytes 380936 | tf_op jit(solution)/shard_map/ppermute | solution.py:164
  10.8 0.0 collective-permute-start.25
  10.8 0.0 collective-permute-done.22.refs_1_
  10.8 0.5 %collective-permute-start.26 = (bf16[496,128]{1,0:T(8,128)(2,1)S(1)}, bf16[496,128]{1,0:T(8,128)(2,1)S(1)}, u32[]{:S(2)}, u32[]{:S(2)}) collective-permute-start(bf16[496,128]{1,0:T(8,128)(2,1)S(1)} %collective-permute-done.22.refs_1_), channel_id=1, source_target_pairs={{0,1},{1,0},{2,3},{3,2},{4,5},{5,4},{6,7},{7,6},{8,9},{9,8},{10,11... | collective-permute-start | bytes 380936 | tf_op jit(solution)/shard_map/ppermute | solution.py:167
  11.3 1.2 %collective-permute-done.23.refs_2_ = bf16[496,128]{1,0:T(8,128)(2,1)S(1)} collective-permute-done((bf16[496,128]{1,0:T(8,128)(2,1)S(1)}, bf16[496,128]{1,0:T(8,128)(2,1)S(1)}, u32[]{:S(2)}, u32[]{:S(2)}) %collective-permute-start.23) | collective-permute-done | bytes 127008 | tf_op jit(solution)/shard_map/ppermute | solution.py:164
  12.5 0.0 collective-permute-start.27
  12.5 0.0 collective-permute-done.29.refs_0_
  12.5 2.4 %collective-permute-start.30 = (bf16[496,128]{1,0:T(8,128)(2,1)S(1)}, bf16[496,128]{1,0:T(8,128)(2,1)S(1)}, u32[]{:S(2)}, u32[]{:S(2)}) collective-permute-start(bf16[496,128]{1,0:T(8,128)(2,1)S(1)} %collective-permute-done.29.refs_0_), channel_id=1, source_target_pairs={{0,4},{1,5},{2,6},{3,7},{4,0},{5,1},{6,2},{7,3},{8,12},{9,13},{10,... | collective-permute-start | bytes 380936 | tf_op jit(solution)/shard_map/ppermute | solution.py:164
  14.9 0.0 collective-permute-done.24.refs_3_
  14.9 0.1 collective-permute-start.31
  15.0 0.0 collective-permute-done.25.refs_4_
  15.0 3.2 %collective-permute-start.32 = (bf16[496,128]{1,0:T(8,128)(2,1)S(1)}, bf16[496,128]{1,0:T(8,128)(2,1)S(1)}, u32[]{:S(2)}, u32[]{:S(2)}) collective-permute-start(bf16[496,128]{1,0:T(8,128)(2,1)S(1)} %collective-permute-done.29.refs_0_), channel_id=1, source_target_pairs={{0,6},{1,7},{2,0},{3,1},{4,2},{5,3},{6,4},{7,5},{8,14},{9,15},{10,... | collective-permute-start | bytes 380936 | tf_op jit(solution)/shard_map/ppermute | solution.py:164
  18.2 0.0 collective-permute-done.26.refs_5_
  18.2 0.0 collective-permute-start.28
  18.2 0.0 collective-permute-done.27.refs_6_
  18.2 0.5 %collective-permute-start.33 = (bf16[496,128]{1,0:T(8,128)(2,1)S(1)}, bf16[496,128]{1,0:T(8,128)(2,1)S(1)}, u32[]{:S(2)}, u32[]{:S(2)}) collective-permute-start(bf16[496,128]{1,0:T(8,128)(2,1)S(1)} %collective-permute-done.29.refs_0_), channel_id=1, source_target_pairs={{0,1},{1,0},{2,3},{3,2},{4,5},{5,4},{6,7},{7,6},{8,9},{9,8},{10,11... | collective-permute-start | bytes 380936 | tf_op jit(solution)/shard_map/ppermute | solution.py:167
  18.7 1.6 %collective-permute-done.30.refs_1_ = bf16[496,128]{1,0:T(8,128)(2,1)S(1)} collective-permute-done((bf16[496,128]{1,0:T(8,128)(2,1)S(1)}, bf16[496,128]{1,0:T(8,128)(2,1)S(1)}, u32[]{:S(2)}, u32[]{:S(2)}) %collective-permute-start.30) | collective-permute-done | bytes 127008 | tf_op jit(solution)/shard_map/ppermute | solution.py:164
  20.3 0.0 collective-permute-start.34
  20.3 2.3 %collective-permute-done.31.refs_2_ = bf16[496,128]{1,0:T(8,128)(2,1)S(1)} collective-permute-done((bf16[496,128]{1,0:T(8,128)(2,1)S(1)}, bf16[496,128]{1,0:T(8,128)(2,1)S(1)}, u32[]{:S(2)}, u32[]{:S(2)}) %collective-permute-start.31) | collective-permute-done | bytes 127008 | tf_op jit(solution)/shard_map/ppermute | solution.py:164
  22.6 0.0 collective-permute-start.35
  22.6 0.0 collective-permute-done.32.refs_3_
  22.6 0.5 %collective-permute-start.36 = (bf16[496,128]{1,0:T(8,128)(2,1)S(1)}, bf16[496,128]{1,0:T(8,128)(2,1)S(1)}, u32[]{:S(2)}, u32[]{:S(2)}) collective-permute-start(bf16[496,128]{1,0:T(8,128)(2,1)S(1)} %collective-permute-done.32.refs_3_), channel_id=1, source_target_pairs={{0,1},{1,0},{2,3},{3,2},{4,5},{5,4},{6,7},{7,6},{8,9},{9,8},{10,11... | collective-permute-start | bytes 380936 | tf_op jit(solution)/shard_map/ppermute | solution.py:167
  23.1 0.0 collective-permute-done.28.refs_7_
  23.1 0.0 copy-done
  23.1 0.0 copy-done.3
  23.1 0.0 copy-start.2
  23.1 0.0 copy-start.4
  23.1 0.0 copy-start.5
  23.1 0.0 copy-start.6
  23.1 1.8 %ladder_first.3.before_ref = f32[384,256]{1,0:T(8,128)S(1)} custom-call(s32[62]{0:T(128)S(1)} %copy-done.3, s32[2]{0:T(128)S(1)} %pad_add_fusion.place_ref, bf16[16,16,128]{2,1,0:T(8,128)(2,1)S(1)} %get-tuple-element.113.table, bf16[384,7936]{1,0:T(8,128)(2,1)S(1)} %copy-done, bf16[496,128]{1,0:T(8,128)(2,1)S(1)} %get-tuple-element.114.refs_0_, ...), custom_call_target="tpu_custom_call" | custom-call | flops 780140544 | bytes 3047424 | tf_op jit(solution)/shard_map/ladder_first/pallas_call | solution.py:174
  25.0 0.0 collective-permute-done.33.refs_4_
  25.0 0.0 collective-permute-done.34.refs_5_
  25.0 0.0 collective-permute-done.35.refs_6_
  25.0 0.0 collective-permute-done.36.refs_7_
  25.0 2.0 %ladder_last.3 = (f32[32,384]{1,0:T(8,128)S(1)}, f32[32,384]{1,0:T(8,128)S(1)}, f32[32,384]{1,0:T(8,128)S(1)}, f32[32,384]{1,0:T(8,128)S(1)}, f32[32,384]{1,0:T(...) custom-call(s32[62]{0:T(128)S(1)} %copy-done.3, s32[2]{0:T(128)S(1)} %pad_add_fusion.place_ref, ...), custom_call_target="tpu_custom_call" | custom-call | flops 780140544 | bytes 3047424 | tf_op jit(solution)/shard_map/ladder_last/pallas_call | solution.py:184
  27.0 5.7 %collective-permute-start.37 = (f32[32,384]{1,0:T(8,128)S(1)}, f32[32,384]{1,0:T(8,128)S(1)}, u32[]{:S(2)}, u32[]{:S(2)}) collective-permute-start(f32[32,384]{1,0:T(8,128)S(1)} %get-tuple-element.116), channel_id=1, source_target_pairs={{0,96},{16,112},{32,64},{48,80},{64,32},{80,48},{96,0},{112,16},{1... | collective-permute-start | bytes 147464 | tf_op jit(solution)/shard_map/ppermute | solution.py:146
  32.7 0.4 collective-permute-start.38
  33.1 5.3 %collective-permute-start.39 = (f32[32,384]{1,0:T(8,128)S(1)}, f32[32,384]{1,0:T(8,128)S(1)}, u32[]{:S(2)}, u32[]{:S(2)}) collective-permute-start(f32[32,384]{1,0:T(8,128)S(1)} %get-tuple-element.118), channel_id=1, source_target_pairs={{0,112},{16,64},{32,80},{48,96},{64,48},{80,0},{96,16},{112,32},{1... | collective-permute-start | bytes 147464 | tf_op jit(solution)/shard_map/ppermute | solution.py:146
  38.4 0.3 collective-permute-start.40
  38.7 0.0 collective-permute-start.41
  38.7 0.0 collective-permute-done.37
  38.7 1.1 %collective-permute-start.42 = (f32[32,384]{1,0:T(8,128)S(1)}, f32[32,384]{1,0:T(8,128)S(1)}, u32[]{:S(2)}, u32[]{:S(2)}) collective-permute-start(f32[32,384]{1,0:T(8,128)S(1)} %get-tuple-element.121), channel_id=1, source_target_pairs={{0,16},{16,32},{32,48},{48,0},{64,80},{80,96},{96,112},{112,64},{1... | collective-permute-start | bytes 147464 | tf_op jit(solution)/shard_map/ppermute | solution.py:146
  39.8 0.6 %collective-permute-done.38 = f32[32,384]{1,0:T(8,128)S(1)} collective-permute-done((f32[32,384]{1,0:T(8,128)S(1)}, f32[32,384]{1,0:T(8,128)S(1)}, u32[]{:S(2)}, u32[]{:S(2)}) %collective-permute-start.38) | collective-permute-done | bytes 49184 | tf_op jit(solution)/shard_map/ppermute | solution.py:146
  40.4 1.5 %collective-permute-start.43 = (f32[32,384]{1,0:T(8,128)S(1)}, f32[32,384]{1,0:T(8,128)S(1)}, u32[]{:S(2)}, u32[]{:S(2)}) collective-permute-start(f32[32,384]{1,0:T(8,128)S(1)} %get-tuple-element.122), channel_id=1, source_target_pairs={{0,48},{16,0},{32,16},{48,32},{64,112},{80,64},{96,80},{112,96},{1... | collective-permute-start | bytes 147464 | tf_op jit(solution)/shard_map/ppermute | solution.py:146
  42.6 0.0 collective-permute-done.39
  42.6 1.3 %collective-permute-done.40 = f32[32,384]{1,0:T(8,128)S(1)} collective-permute-done((f32[32,384]{1,0:T(8,128)S(1)}, f32[32,384]{1,0:T(8,128)S(1)}, u32[]{:S(2)}, u32[]{:S(2)}) %collective-permute-start.40) | collective-permute-done | bytes 49184 | tf_op jit(solution)/shard_map/ppermute | solution.py:146
  44.0 0.4 collective-permute-done.41
  44.4 0.1 collective-permute-done.42
  44.5 0.0 collective-permute-done.43
  44.5 0.0 copy-done.2
  44.5 0.0 copy-done.4
  44.5 0.0 copy-done.5
  44.6 0.0 copy-done.6
  44.6 0.4 conditional.1
  44.6 0.1 dynamic_slice.4
  44.7 0.1 fusion
  45.0 0.0 copy-start.1
  45.0 0.6 %copy-done.1 = bf16[384,32]{0,1:T(8,128)(2,1)} copy-done((bf16[384,32]{0,1:T(8,128)(2,1)}, bf16[384,32]{0,1:T(8,128)(2,1)S(1)}, u32[]{:S(2)}) %copy-start.1) | copy-done | bytes 24600
  (1 shorter events, 0.0 us)
Async XLA Ops:
  0.1 23.0 %copy-start = (bf16[384,7936]{1,0:T(8,128)(2,1)S(1)}, bf16[384,7936]{1,0:T(8,128)(2,1)}, u32[]{:S(2)}) copy-start(bf16[384,7936]{1,0:T(8,128)(2,1)} %t_ref.3) | copy-start | bytes 18284548
  0.1 23.0 %copy-start.3 = (s32[62]{0:T(128)S(1)}, s32[62]{0:T(128)}, u32[]{:S(2)}) copy-start(s32[62]{0:T(128)} %cd_ref.5) | copy-start | bytes 748
  1.9 8.9 %collective-permute-start.22 = (bf16[496,128]{1,0:T(8,128)(2,1)S(1)}, bf16[496,128]{1,0:T(8,128)(2,1)S(1)}, u32[]{:S(2)}, u32[]{:S(2)}) collective-permute-start(bf16[496,128]{1,0:T(8,128)(2,1)S(1)} %get-tuple-element.114.refs_0_), channel_id=1, source_target_pairs={{0,4},{1,5},{2,6},{3,7},{4,0},{5,1},{6,2},{7,3},{8,12},{9,13},{10,... | collective-permute-start | bytes 380936 | tf_op jit(solution)/shard_map/ppermute | solution.py:164
  6.0 6.5 %collective-permute-start.23 = (bf16[496,128]{1,0:T(8,128)(2,1)S(1)}, bf16[496,128]{1,0:T(8,128)(2,1)S(1)}, u32[]{:S(2)}, u32[]{:S(2)}) collective-permute-start(bf16[496,128]{1,0:T(8,128)(2,1)S(1)} %get-tuple-element.114.refs_0_), channel_id=1, source_target_pairs={{0,2},{1,3},{2,4},{3,5},{4,6},{5,7},{6,0},{7,1},{8,10},{9,11},{10,... | collective-permute-start | bytes 380936 | tf_op jit(solution)/shard_map/ppermute | solution.py:164
  7.0 5.5 %collective-permute-start.29 = (bf16[496,128]{1,0:T(8,128)(2,1)S(1)}, bf16[496,128]{1,0:T(8,128)(2,1)S(1)}, u32[]{:S(2)}, u32[]{:S(2)}) collective-permute-start(bf16[496,128]{1,0:T(8,128)(2,1)S(1)} %get-tuple-element.114.refs_0_), channel_id=1, source_target_pairs={{0,8},{1,9},{2,10},{3,11},{4,12},{5,13},{6,14},{7,15},{8,0},{9,1},... | collective-permute-start | bytes 380936 | tf_op jit(solution)/shard_map/ppermute | solution.py:159
  8.6 6.3 %collective-permute-start.24 = (bf16[496,128]{1,0:T(8,128)(2,1)S(1)}, bf16[496,128]{1,0:T(8,128)(2,1)S(1)}, u32[]{:S(2)}, u32[]{:S(2)}) collective-permute-start(bf16[496,128]{1,0:T(8,128)(2,1)S(1)} %get-tuple-element.114.refs_0_), channel_id=1, source_target_pairs={{0,6},{1,7},{2,0},{3,1},{4,2},{5,3},{6,4},{7,5},{8,14},{9,15},{10,... | collective-permute-start | bytes 380936 | tf_op jit(solution)/shard_map/ppermute | solution.py:164
  10.8 4.2 %collective-permute-start.25 = (bf16[496,128]{1,0:T(8,128)(2,1)S(1)}, bf16[496,128]{1,0:T(8,128)(2,1)S(1)}, u32[]{:S(2)}, u32[]{:S(2)}) collective-permute-start(bf16[496,128]{1,0:T(8,128)(2,1)S(1)} %get-tuple-element.114.refs_0_), channel_id=1, source_target_pairs={{0,1},{1,0},{2,3},{3,2},{4,5},{5,4},{6,7},{7,6},{8,9},{9,8},{10,11... | collective-permute-start | bytes 380936 | tf_op jit(solution)/shard_map/ppermute | solution.py:167
  10.8 7.4 %collective-permute-start.26 = (bf16[496,128]{1,0:T(8,128)(2,1)S(1)}, bf16[496,128]{1,0:T(8,128)(2,1)S(1)}, u32[]{:S(2)}, u32[]{:S(2)}) collective-permute-start(bf16[496,128]{1,0:T(8,128)(2,1)S(1)} %collective-permute-done.22.refs_1_), channel_id=1, source_target_pairs={{0,1},{1,0},{2,3},{3,2},{4,5},{5,4},{6,7},{7,6},{8,9},{9,8},{10,11... | collective-permute-start | bytes 380936 | tf_op jit(solution)/shard_map/ppermute | solution.py:167
  12.5 5.7 %collective-permute-start.27 = (bf16[496,128]{1,0:T(8,128)(2,1)S(1)}, bf16[496,128]{1,0:T(8,128)(2,1)S(1)}, u32[]{:S(2)}, u32[]{:S(2)}) collective-permute-start(bf16[496,128]{1,0:T(8,128)(2,1)S(1)} %collective-permute-done.23.refs_2_), channel_id=1, source_target_pairs={{0,1},{1,0},{2,3},{3,2},{4,5},{5,4},{6,7},{7,6},{8,9},{9,8},{10,11... | collective-permute-start | bytes 380936 | tf_op jit(solution)/shard_map/ppermute | solution.py:167
  12.5 7.8 %collective-permute-start.30 = (bf16[496,128]{1,0:T(8,128)(2,1)S(1)}, bf16[496,128]{1,0:T(8,128)(2,1)S(1)}, u32[]{:S(2)}, u32[]{:S(2)}) collective-permute-start(bf16[496,128]{1,0:T(8,128)(2,1)S(1)} %collective-permute-done.29.refs_0_), channel_id=1, source_target_pairs={{0,4},{1,5},{2,6},{3,7},{4,0},{5,1},{6,2},{7,3},{8,12},{9,13},{10,... | collective-permute-start | bytes 380936 | tf_op jit(solution)/shard_map/ppermute | solution.py:164
  14.9 7.6 %collective-permute-start.31 = (bf16[496,128]{1,0:T(8,128)(2,1)S(1)}, bf16[496,128]{1,0:T(8,128)(2,1)S(1)}, u32[]{:S(2)}, u32[]{:S(2)}) collective-permute-start(bf16[496,128]{1,0:T(8,128)(2,1)S(1)} %collective-permute-done.29.refs_0_), channel_id=1, source_target_pairs={{0,2},{1,3},{2,4},{3,5},{4,6},{5,7},{6,0},{7,1},{8,10},{9,11},{10,... | collective-permute-start | bytes 380936 | tf_op jit(solution)/shard_map/ppermute | solution.py:164
  15.0 7.6 %collective-permute-start.32 = (bf16[496,128]{1,0:T(8,128)(2,1)S(1)}, bf16[496,128]{1,0:T(8,128)(2,1)S(1)}, u32[]{:S(2)}, u32[]{:S(2)}) collective-permute-start(bf16[496,128]{1,0:T(8,128)(2,1)S(1)} %collective-permute-done.29.refs_0_), channel_id=1, source_target_pairs={{0,6},{1,7},{2,0},{3,1},{4,2},{5,3},{6,4},{7,5},{8,14},{9,15},{10,... | collective-permute-start | bytes 380936 | tf_op jit(solution)/shard_map/ppermute | solution.py:164
  18.2 4.9 %collective-permute-start.28 = (bf16[496,128]{1,0:T(8,128)(2,1)S(1)}, bf16[496,128]{1,0:T(8,128)(2,1)S(1)}, u32[]{:S(2)}, u32[]{:S(2)}) collective-permute-start(bf16[496,128]{1,0:T(8,128)(2,1)S(1)} %collective-permute-done.24.refs_3_), channel_id=1, source_target_pairs={{0,1},{1,0},{2,3},{3,2},{4,5},{5,4},{6,7},{7,6},{8,9},{9,8},{10,11... | collective-permute-start | bytes 380936 | tf_op jit(solution)/shard_map/ppermute | solution.py:167
  18.2 6.8 %collective-permute-start.33 = (bf16[496,128]{1,0:T(8,128)(2,1)S(1)}, bf16[496,128]{1,0:T(8,128)(2,1)S(1)}, u32[]{:S(2)}, u32[]{:S(2)}) collective-permute-start(bf16[496,128]{1,0:T(8,128)(2,1)S(1)} %collective-permute-done.29.refs_0_), channel_id=1, source_target_pairs={{0,1},{1,0},{2,3},{3,2},{4,5},{5,4},{6,7},{7,6},{8,9},{9,8},{10,11... | collective-permute-start | bytes 380936 | tf_op jit(solution)/shard_map/ppermute | solution.py:167
  20.3 4.7 %collective-permute-start.34 = (bf16[496,128]{1,0:T(8,128)(2,1)S(1)}, bf16[496,128]{1,0:T(8,128)(2,1)S(1)}, u32[]{:S(2)}, u32[]{:S(2)}) collective-permute-start(bf16[496,128]{1,0:T(8,128)(2,1)S(1)} %collective-permute-done.30.refs_1_), channel_id=1, source_target_pairs={{0,1},{1,0},{2,3},{3,2},{4,5},{5,4},{6,7},{7,6},{8,9},{9,8},{10,11... | collective-permute-start | bytes 380936 | tf_op jit(solution)/shard_map/ppermute | solution.py:167
  22.6 2.4 %collective-permute-start.35 = (bf16[496,128]{1,0:T(8,128)(2,1)S(1)}, bf16[496,128]{1,0:T(8,128)(2,1)S(1)}, u32[]{:S(2)}, u32[]{:S(2)}) collective-permute-start(bf16[496,128]{1,0:T(8,128)(2,1)S(1)} %collective-permute-done.31.refs_2_), channel_id=1, source_target_pairs={{0,1},{1,0},{2,3},{3,2},{4,5},{5,4},{6,7},{7,6},{8,9},{9,8},{10,11... | collective-permute-start | bytes 380936 | tf_op jit(solution)/shard_map/ppermute | solution.py:167
  22.6 2.4 %collective-permute-start.36 = (bf16[496,128]{1,0:T(8,128)(2,1)S(1)}, bf16[496,128]{1,0:T(8,128)(2,1)S(1)}, u32[]{:S(2)}, u32[]{:S(2)}) collective-permute-start(bf16[496,128]{1,0:T(8,128)(2,1)S(1)} %collective-permute-done.32.refs_3_), channel_id=1, source_target_pairs={{0,1},{1,0},{2,3},{3,2},{4,5},{5,4},{6,7},{7,6},{8,9},{9,8},{10,11... | collective-permute-start | bytes 380936 | tf_op jit(solution)/shard_map/ppermute | solution.py:167
  23.1 21.4 %copy-start.2 = (f32[384]{0:T(512)S(1)}, f32[384]{0:T(512)}, u32[]{:S(2)}) copy-start(f32[384]{0:T(512)} %param.12) | copy-start | bytes 4612
  23.1 21.4 %copy-start.4 = (bf16[496,256]{1,0:T(8,128)(2,1)S(1)}, bf16[496,256]{1,0:T(8,128)(2,1)}, u32[]{:S(2)}) copy-start(bf16[496,256]{1,0:T(8,128)(2,1)} %v_ref.1) | copy-start | bytes 761860
  23.1 21.4 %copy-start.5 = (f32[256]{0:T(256)S(1)}, f32[256]{0:T(256)}, u32[]{:S(2)}) copy-start(f32[256]{0:T(256)} %param.13) | copy-start | bytes 3076
  23.1 21.4 %copy-start.6 = (s32[4]{0:T(128)S(1)}, s32[4]{0:T(128)}, u32[]{:S(2)}) copy-start(s32[4]{0:T(128)} %ab_ref.1) | copy-start | bytes 52
  27.0 11.7 %collective-permute-start.37 = (f32[32,384]{1,0:T(8,128)S(1)}, f32[32,384]{1,0:T(8,128)S(1)}, u32[]{:S(2)}, u32[]{:S(2)}) collective-permute-start(f32[32,384]{1,0:T(8,128)S(1)} %get-tuple-element.116), channel_id=1, source_target_pairs={{0,96},{16,112},{32,64},{48,80},{64,32},{80,48},{96,0},{112,16},{1... | collective-permute-start | bytes 147464 | tf_op jit(solution)/shard_map/ppermute | solution.py:146
  32.7 7.7 %collective-permute-start.38 = (f32[32,384]{1,0:T(8,128)S(1)}, f32[32,384]{1,0:T(8,128)S(1)}, u32[]{:S(2)}, u32[]{:S(2)}) collective-permute-start(f32[32,384]{1,0:T(8,128)S(1)} %get-tuple-element.117), channel_id=1, source_target_pairs={{0,80},{16,96},{32,112},{48,64},{64,16},{80,32},{96,48},{112,0},{1... | collective-permute-start | bytes 147464 | tf_op jit(solution)/shard_map/ppermute | solution.py:146
  33.1 9.5 %collective-permute-start.39 = (f32[32,384]{1,0:T(8,128)S(1)}, f32[32,384]{1,0:T(8,128)S(1)}, u32[]{:S(2)}, u32[]{:S(2)}) collective-permute-start(f32[32,384]{1,0:T(8,128)S(1)} %get-tuple-element.118), channel_id=1, source_target_pairs={{0,112},{16,64},{32,80},{48,96},{64,48},{80,0},{96,16},{112,32},{1... | collective-permute-start | bytes 147464 | tf_op jit(solution)/shard_map/ppermute | solution.py:146
  38.4 5.6 %collective-permute-start.40 = (f32[32,384]{1,0:T(8,128)S(1)}, f32[32,384]{1,0:T(8,128)S(1)}, u32[]{:S(2)}, u32[]{:S(2)}) collective-permute-start(f32[32,384]{1,0:T(8,128)S(1)} %get-tuple-element.119), channel_id=1, source_target_pairs={{0,64},{16,80},{32,96},{48,112},{64,0},{80,16},{96,32},{112,48},{1... | collective-permute-start | bytes 147464 | tf_op jit(solution)/shard_map/ppermute | solution.py:146
  38.7 5.7 %collective-permute-start.41 = (f32[32,384]{1,0:T(8,128)S(1)}, f32[32,384]{1,0:T(8,128)S(1)}, u32[]{:S(2)}, u32[]{:S(2)}) collective-permute-start(f32[32,384]{1,0:T(8,128)S(1)} %get-tuple-element.120), channel_id=1, source_target_pairs={{0,32},{16,48},{32,0},{48,16},{64,96},{80,112},{96,64},{112,80},{1... | collective-permute-start | bytes 147464 | tf_op jit(solution)/shard_map/ppermute | solution.py:146
  38.7 5.8 %collective-permute-start.42 = (f32[32,384]{1,0:T(8,128)S(1)}, f32[32,384]{1,0:T(8,128)S(1)}, u32[]{:S(2)}, u32[]{:S(2)}) collective-permute-start(f32[32,384]{1,0:T(8,128)S(1)} %get-tuple-element.121), channel_id=1, source_target_pairs={{0,16},{16,32},{32,48},{48,0},{64,80},{80,96},{96,112},{112,64},{1... | collective-permute-start | bytes 147464 | tf_op jit(solution)/shard_map/ppermute | solution.py:146
  40.4 4.1 %collective-permute-start.43 = (f32[32,384]{1,0:T(8,128)S(1)}, f32[32,384]{1,0:T(8,128)S(1)}, u32[]{:S(2)}, u32[]{:S(2)}) collective-permute-start(f32[32,384]{1,0:T(8,128)S(1)} %get-tuple-element.122), channel_id=1, source_target_pairs={{0,48},{16,0},{32,16},{48,32},{64,112},{80,64},{96,80},{112,96},{1... | collective-permute-start | bytes 147464 | tf_op jit(solution)/shard_map/ppermute | solution.py:146
  45.0 0.6 %copy-start.1 = (bf16[384,32]{0,1:T(8,128)(2,1)}, bf16[384,32]{0,1:T(8,128)(2,1)S(1)}, u32[]{:S(2)}) copy-start(bf16[384,32]{0,1:T(8,128)(2,1)S(1)} %get-tuple-element.222) | copy-start | bytes 73732

commit v4 on v3

--- a/solution.py
+++ b/solution.py
@@ -1,5 +1,3 @@
-import functools
-
 import jax
 import jax.numpy as jnp
 from jax import lax
@@ -13,6 +11,7 @@
 SUB = 16
 LANES = 128
 LABELS = 4
+KINDS = 3
 VMEM = pltpu.VMEM
 SMEM = pltpu.SMEM
 IN_SMEM = pl.BlockSpec(memory_space=SMEM)
@@ -23,20 +22,20 @@
     return jnp.concatenate([x[:, ABLK:], x[:, :ABLK]], axis=1)
 
 
-def ranks(ab_ref, base):
+def ranks(ab_ref):
     out = []
     for b in range(4):
-        count = jnp.int32(-base)
+        count = jnp.int32(0)
         for earlier in range(b):
             count = count + jnp.where(ab_ref[earlier] == ab_ref[b], 1, 0)
         out.append(count)
     return out
 
 
-def fill_factors(ab_ref, base, table):
+def fill_factors(ab_ref, table):
     lane = lax.broadcasted_iota(jnp.int32, (SUB, LANES), 1)
     low = lane < ABLK
-    rank = ranks(ab_ref, base)
+    rank = ranks(ab_ref)
     for t in range(2):
         own = jnp.where(low, ab_ref[2 * t], ab_ref[2 * t + 1])
         slot = jnp.where(low, rank[2 * t], rank[2 * t + 1])
@@ -44,13 +43,14 @@
         for label in range(LABELS):
             for kind, want in enumerate((half, 1 - half)):
                 hit = jnp.where(own == label, jnp.where(slot == want, 1.0, 0.0), 0.0)
-                table[(label * 2 + t) * 2 + kind] = hit.astype(jnp.bfloat16)
-
-
-def pack_kernel(base, cd_ref, ab_ref, place_ref, v_ref, o_ref, most_ref, table):
-    fill_factors(ab_ref, base, table)
+                table[(label * 2 + t) * KINDS + kind] = hit.astype(jnp.bfloat16)
+            table[(label * 2 + t) * KINDS + 2] = jnp.where(own == label, 1.0, 0.0).astype(jnp.bfloat16)
+
+
+def pack_kernel(cd_ref, ab_ref, place_ref, v_ref, o_ref, most_ref, table):
+    fill_factors(ab_ref, table)
     most = jnp.int32(0)
-    for count in ranks(ab_ref, 0):
+    for count in ranks(ab_ref):
         most = jnp.maximum(most, count)
     most_ref[0] = most + 1
     subs = v_ref.shape[0] // SUB
@@ -60,19 +60,20 @@
         straight = crossed = None
         for t in range(2):
             x = v_ref[j * SUB:(j + 1) * SUB, t * LANES:(t + 1) * LANES]
-            s, c = x * table[label * 4 + t * 2], x * table[label * 4 + t * 2 + 1]
+            at = (label * 2 + t) * KINDS
+            s, c = x * table[at], x * table[at + 1]
             straight = s if straight is None else straight + s
             crossed = c if crossed is None else crossed + c
         o_ref[j * SUB:(j + 1) * SUB, :] = straight + swap_halves(crossed)
 
 
-def pack(base, cd_irrep, ab_irrep, place, integrals):
+def pack(cd_irrep, ab_irrep, place, integrals):
     return pl.pallas_call(
-        functools.partial(pack_kernel, base),
+        pack_kernel,
         out_shape=(
             jax.ShapeDtypeStruct((integrals.shape[0], LANES), jnp.bfloat16),
             jax.ShapeDtypeStruct((1,), jnp.int32),
-            jax.ShapeDtypeStruct((LABELS * 4, SUB, LANES), jnp.bfloat16),
+            jax.ShapeDtypeStruct((LABELS * 2 * KINDS, SUB, LANES), jnp.bfloat16),
         ),
         in_specs=[IN_SMEM, IN_SMEM, IN_SMEM, IN_VMEM],
         out_specs=(IN_VMEM, IN_SMEM, IN_VMEM),
@@ -93,14 +94,18 @@
         at = (lax.rem(z + 4 - dz, 4) * 2 + from_core) * depth
         held[pl.ds(pl.multiple_of(at, SUB), depth), :] = ref[...]
     blocks = held.shape[0] // KBLK
+    wide = held.shape[1] > LANES
     for blk in range(blocks):
         at = slice(blk * KBLK, (blk + 1) * KBLK)
-        x = held[at, :]
-        y = swap_halves(x)
         label = cd_ref[half * blocks + blk]
         for t in range(2):
-            same, other = [jnp.concatenate([table[label * 4 + t * 2 + kind]] * (KBLK // SUB), 0) for kind in range(2)]
-            masked[at, t * LANES:(t + 1) * LANES] = x * same + y * other
+            lanes = slice(t * LANES, (t + 1) * LANES)
+            same, other, match = [jnp.concatenate([table[(label * 2 + t) * KINDS + kind]] * (KBLK // SUB), 0) for kind in range(3)]
+            if wide:
+                masked[at, lanes] = held[at, lanes] * match
+            else:
+                x = held[at, :]
+                masked[at, lanes] = x * same + swap_halves(x) * other
 
 
 def half_place(place_ref, dy):
@@ -168,7 +173,7 @@
         pieces.append(mine + theirs)
     ij, cds = amplitudes.shape
     width, cols = 2 * LANES, cds // 2
-    scratch = [VMEM((cols, LANES), jnp.bfloat16), VMEM((cols, width), jnp.bfloat16)]
+    scratch = [VMEM((cols, packed.shape[1]), jnp.bfloat16), VMEM((cols, width), jnp.bfloat16)]
     cost = pl.CostEstimate(flops=ij * cds * width, bytes_accessed=ij * cds, transcendentals=0)
     limits = pltpu.CompilerParams(vmem_limit_bytes=12 * 2**20)
     half = pl.pallas_call(
@@ -195,27 +200,21 @@
 
 def shards(amplitudes, integrals, cd_irrep, ab_irrep, pair_energy, panel_energy):
     place = jnp.stack([lax.axis_index("col"), lax.axis_index("row")]).astype(jnp.int32)
-    packed, most, table = pack(0, cd_irrep, ab_irrep, place, integrals)
-    parts = reduce_parts(partial_ladder(packed, table, amplitudes, cd_irrep, place))
-
-    def finish(parts, pair_energy, panel_energy):
-        share = parts[0].shape[0]
-        summed = sum(parts[1:], parts[0])
-        energy_cols = lax.dynamic_slice_in_dim(panel_energy, lax.axis_index("row") * share, share, 0)
-        denom = energy_cols[:, None] - pair_energy[None, :]
-        return (summed / denom).astype(jnp.bfloat16).T
-
-    def more(parts, pair_energy, panel_energy, amplitudes, integrals, cd_irrep, ab_irrep, place):
-        rest, _, table = pack(2, cd_irrep, ab_irrep, place, integrals)
-        extra = reduce_parts(partial_ladder(rest, table, amplitudes, cd_irrep, place))
-        return finish([p + e for p, e in zip(parts, extra)], pair_energy, panel_energy)
-
-    def enough(parts, pair_energy, panel_energy, *unused):
-        return finish(parts, pair_energy, panel_energy)
-
-    parts = lax.optimization_barrier(parts)
-    operands = (parts, pair_energy, panel_energy, amplitudes, integrals, cd_irrep, ab_irrep, place)
-    return lax.cond(most[0] > 2, more, enough, *operands)
+    packed, most, table = pack(cd_irrep, ab_irrep, place, integrals)
+
+    def narrow(packed, integrals, *rest):
+        return partial_ladder(packed, *rest)
+
+    def whole(packed, integrals, *rest):
+        return partial_ladder(integrals, *rest)
+
+    blocks = lax.cond(most[0] > 2, whole, narrow, packed, integrals, table, amplitudes, cd_irrep, place)
+    parts = reduce_parts(blocks)
+    share = parts[0].shape[0]
+    summed = sum(parts[1:], parts[0])
+    energy_cols = lax.dynamic_slice_in_dim(panel_energy, lax.axis_index("row") * share, share, 0)
+    denom = energy_cols[:, None] - pair_energy[None, :]
+    return (summed / denom).astype(jnp.bfloat16).T
 
 
 def solution(mesh):

time: 45.8 us -> 47.2 us (1.031)
  other arithmetic: 0.16 us -> 0.77 us
  waiting for transfers between devices: 7.67 us -> 8.26 us
    transpose x1, other arithmetic: 0.09 us -> 0.69 us  [shards(): return (summed / denom).astype(jnp.bfloat16).T]
    ppermute x7, waiting for transfers between devices: 2.56 us -> 3.15 us  [reduce_parts(): parts.append(lax.ppermute(block, 'row', row_hop(*TARGETS[n])))]
where the time goes in v4:
time: 47.2 us; the launch traced here: 47 us
  starting transfers between devices  30.4 us (64%)
  waiting for transfers between devices  8.26 us (18%)
  Pallas kernels  5.69 us (12%)
  local copies, waits for them, and re-layouts  0.97 us (2%)
  between operations  0.82 us (2%)
  other arithmetic  0.77 us (2%)
    ppermute x7, starting transfers between devices, reduce_parts(): parts.append(lax.ppermute(block, 'row', row_hop(*TARGETS[n])))  14.3 us
    ppermute x6, starting transfers between devices, partial_ladder(): mine.append(lax.ppermute(start, 'col', hop(0, dz)))  12.9 us
    ppermute x6, waiting for transfers between devices, partial_ladder(): mine.append(lax.ppermute(start, 'col', hop(0, dz)))  5.08 us
    ppermute x7, waiting for transfers between devices, reduce_parts(): parts.append(lax.ppermute(block, 'row', row_hop(*TARGETS[n])))  3.15 us
    pallas_call x1, Pallas kernels, partial_ladder(): pl.pallas_call(last_kernel, out_shape=[jax.ShapeDtypeStruct((width // 8,...  2 us
    pallas_call x1, Pallas kernels, partial_ladder(): pl.pallas_call(first_kernel, out_shape=jax.ShapeDtypeStruct((ij, width),...  1.86 us
    pallas_call x1, Pallas kernels, pack(): pl.pallas_call(pack_kernel, out_shape=(jax.ShapeDtypeStruct((integrals.sh...  1.83 us
    ppermute x1, starting transfers between devices, partial_ladder(): across = lax.ppermute(packed, 'col', hop(1, 0))  1.58 us
  transfers between devices with their start and end apart: 22, of which 7 were waited for; matrix products, arithmetic and copies ran while one was open for 0% of the time, Pallas kernels for 4%

profile of v4, /device:TPU:0, one launch (start us, length us, event | category | flops | bytes accessed | tf_op | source)
XLA Modules:
  0.0 47.0 jit_solution(7767307119364488818)
XLA Ops:
  0.0 0.1 pad_add_fusion.place_ref
  0.1 0.0 copy-start
  0.1 0.7 %copy-done = s32[4]{0:T(128)S(1)} copy-done((s32[4]{0:T(128)S(1)}, s32[4]{0:T(128)}, u32[]{:S(2)}) %copy-start) | copy-done | bytes 40
  0.7 0.0 copy-start.1
  0.7 0.0 copy-start.4
  0.7 0.0 copy-start.5
  0.7 1.8 %pack.1 = (bf16[496,128]{1,0:T(8,128)(2,1)S(1)}, s32[1]{0:T(128)}, bf16[24,16,128]{2,1,0:T(8,128)(2,1)S(1)}) custom-call(s32[62]{0:T(128)} %cd_ref.1, s32[4]{0:T(128)S(1)} %copy-done, s32[2]{0:T(128)S(1)} %pad_add_fusion.place_ref, bf16[496,256]{1,0:T(8,128)(2,1)} %v_ref.1), custom_call_target="tpu_custom_call" | custom-call | flops 10000000000 | bytes 253952 | tf_op jit(solution)/shard_map/pack/pallas_call | solution.py:71
  3.4 0.2 copy-done.1
  3.6 0.0 copy-done.4
  3.6 0.0 copy-done.5
  3.6 0.0 copy-start.7
  3.6 0.0 copy-start.6
  3.6 25.1 %conditional.1 = ((f32[32,384]{1,0:T(8,128)S(1)}, f32[32,384]{1,0:T(8,128)S(1)}, f32[32,384]{1,0:T(8,128)S(1)}, f32[32,384]{1,0:T(8,128)S(1)}, f32[32,384]{1,0:T...) conditional(s32[]{:T(128)} %bitcast.2, (bf16[496,128]{1,0:T(8,128)(2,1)S(1)}, ...), branch_computations={%region_0.0_spmd, %region_1.0_spmd} | conditional | flops 1560281088 | bytes 70091416 | solution.py:211
  3.6 4.1 %collective-permute-start = (bf16[496,128]{1,0:T(8,128)(2,1)S(1)}, bf16[496,128]{1,0:T(8,128)(2,1)S(1)}, u32[]{:S(2)}, u32[]{:S(2)}) collective-permute-start(bf16[496,128]{1,0:T(8,128)(2,1)S(1)} %get-tuple-element.29.refs_0_), channel_id=1, source_target_pairs={{0,4},{1,5},{2,6},{3,7},{4,0},{5,1},{6,2},{7,3},{8,12},{9,13},{10,... | collective-permute-start | bytes 380936 | tf_op jit(solution)/shard_map/cond/branch_0_fun/ppermute | solution.py:169
  7.7 1.0 %collective-permute-start.1 = (bf16[496,128]{1,0:T(8,128)(2,1)S(1)}, bf16[496,128]{1,0:T(8,128)(2,1)S(1)}, u32[]{:S(2)}, u32[]{:S(2)}) collective-permute-start(bf16[496,128]{1,0:T(8,128)(2,1)S(1)} %get-tuple-element.29.refs_0_), channel_id=1, source_target_pairs={{0,2},{1,3},{2,4},{3,5},{4,6},{5,7},{6,0},{7,1},{8,10},{9,11},{10,... | collective-permute-start | bytes 380936 | tf_op jit(solution)/shard_map/cond/branch_0_fun/ppermute | solution.py:169
  8.7 1.6 %collective-permute-start.7 = (bf16[496,128]{1,0:T(8,128)(2,1)S(1)}, bf16[496,128]{1,0:T(8,128)(2,1)S(1)}, u32[]{:S(2)}, u32[]{:S(2)}) collective-permute-start(bf16[496,128]{1,0:T(8,128)(2,1)S(1)} %get-tuple-element.29.refs_0_), channel_id=1, source_target_pairs={{0,8},{1,9},{2,10},{3,11},{4,12},{5,13},{6,14},{7,15},{8,0},{9,1},... | collective-permute-start | bytes 380936 | tf_op jit(solution)/shard_map/cond/branch_0_fun/ppermute | solution.py:164
  10.3 2.2 %collective-permute-start.2 = (bf16[496,128]{1,0:T(8,128)(2,1)S(1)}, bf16[496,128]{1,0:T(8,128)(2,1)S(1)}, u32[]{:S(2)}, u32[]{:S(2)}) collective-permute-start(bf16[496,128]{1,0:T(8,128)(2,1)S(1)} %get-tuple-element.29.refs_0_), channel_id=1, source_target_pairs={{0,6},{1,7},{2,0},{3,1},{4,2},{5,3},{6,4},{7,5},{8,14},{9,15},{10,... | collective-permute-start | bytes 380936 | tf_op jit(solution)/shard_map/cond/branch_0_fun/ppermute | solution.py:169
  12.5 0.0 collective-permute-start.3
  12.5 0.0 collective-permute-done.refs_1_
  12.5 0.5 %collective-permute-start.4 = (bf16[496,128]{1,0:T(8,128)(2,1)S(1)}, bf16[496,128]{1,0:T(8,128)(2,1)S(1)}, u32[]{:S(2)}, u32[]{:S(2)}) collective-permute-start(bf16[496,128]{1,0:T(8,128)(2,1)S(1)} %collective-permute-done.refs_1_), channel_id=1, source_target_pairs={{0,1},{1,0},{2,3},{3,2},{4,5},{5,4},{6,7},{7,6},{8,9},{9,8},{10,11... | collective-permute-start | bytes 380936 | tf_op jit(solution)/shard_map/cond/branch_0_fun/ppermute | solution.py:172
  13.0 1.2 %collective-permute-done.1.refs_2_ = bf16[496,128]{1,0:T(8,128)(2,1)S(1)} collective-permute-done((bf16[496,128]{1,0:T(8,128)(2,1)S(1)}, bf16[496,128]{1,0:T(8,128)(2,1)S(1)}, u32[]{:S(2)}, u32[]{:S(2)}) %collective-permute-start.1) | collective-permute-done | bytes 127008 | tf_op jit(solution)/shard_map/cond/branch_0_fun/ppermute | solution.py:169
  14.2 0.0 collective-permute-start.5
  14.2 0.0 collective-permute-done.7.refs_0_
  14.2 2.4 %collective-permute-start.8 = (bf16[496,128]{1,0:T(8,128)(2,1)S(1)}, bf16[496,128]{1,0:T(8,128)(2,1)S(1)}, u32[]{:S(2)}, u32[]{:S(2)}) collective-permute-start(bf16[496,128]{1,0:T(8,128)(2,1)S(1)} %collective-permute-done.7.refs_0_), channel_id=1, source_target_pairs={{0,4},{1,5},{2,6},{3,7},{4,0},{5,1},{6,2},{7,3},{8,12},{9,13},{10,... | collective-permute-start | bytes 380936 | tf_op jit(solution)/shard_map/cond/branch_0_fun/ppermute | solution.py:169
  16.6 0.0 collective-permute-done.2.refs_3_
  16.6 0.1 collective-permute-start.9
  16.7 0.0 collective-permute-done.3.refs_4_
  16.7 3.2 %collective-permute-start.10 = (bf16[496,128]{1,0:T(8,128)(2,1)S(1)}, bf16[496,128]{1,0:T(8,128)(2,1)S(1)}, u32[]{:S(2)}, u32[]{:S(2)}) collective-permute-start(bf16[496,128]{1,0:T(8,128)(2,1)S(1)} %collective-permute-done.7.refs_0_), channel_id=1, source_target_pairs={{0,6},{1,7},{2,0},{3,1},{4,2},{5,3},{6,4},{7,5},{8,14},{9,15},{10,... | collective-permute-start | bytes 380936 | tf_op jit(solution)/shard_map/cond/branch_0_fun/ppermute | solution.py:169
  19.9 0.0 collective-permute-done.4.refs_5_
  19.9 0.0 collective-permute-start.6
  19.9 0.0 collective-permute-done.5.refs_6_
  19.9 0.5 %collective-permute-start.11 = (bf16[496,128]{1,0:T(8,128)(2,1)S(1)}, bf16[496,128]{1,0:T(8,128)(2,1)S(1)}, u32[]{:S(2)}, u32[]{:S(2)}) collective-permute-start(bf16[496,128]{1,0:T(8,128)(2,1)S(1)} %collective-permute-done.7.refs_0_), channel_id=1, source_target_pairs={{0,1},{1,0},{2,3},{3,2},{4,5},{5,4},{6,7},{7,6},{8,9},{9,8},{10,11... | collective-permute-start | bytes 380936 | tf_op jit(solution)/shard_map/cond/branch_0_fun/ppermute | solution.py:172
  20.4 1.6 %collective-permute-done.8.refs_1_ = bf16[496,128]{1,0:T(8,128)(2,1)S(1)} collective-permute-done((bf16[496,128]{1,0:T(8,128)(2,1)S(1)}, bf16[496,128]{1,0:T(8,128)(2,1)S(1)}, u32[]{:S(2)}, u32[]{:S(2)}) %collective-permute-start.8) | collective-permute-done | bytes 127008 | tf_op jit(solution)/shard_map/cond/branch_0_fun/ppermute | solution.py:169
  22.0 0.0 collective-permute-start.12
  22.0 2.3 %collective-permute-done.9.refs_2_ = bf16[496,128]{1,0:T(8,128)(2,1)S(1)} collective-permute-done((bf16[496,128]{1,0:T(8,128)(2,1)S(1)}, bf16[496,128]{1,0:T(8,128)(2,1)S(1)}, u32[]{:S(2)}, u32[]{:S(2)}) %collective-permute-start.9) | collective-permute-done | bytes 127008 | tf_op jit(solution)/shard_map/cond/branch_0_fun/ppermute | solution.py:169
  24.3 0.0 collective-permute-start.13
  24.3 0.0 collective-permute-done.10.refs_3_
  24.3 0.5 %collective-permute-start.14 = (bf16[496,128]{1,0:T(8,128)(2,1)S(1)}, bf16[496,128]{1,0:T(8,128)(2,1)S(1)}, u32[]{:S(2)}, u32[]{:S(2)}) collective-permute-start(bf16[496,128]{1,0:T(8,128)(2,1)S(1)} %collective-permute-done.10.refs_3_), channel_id=1, source_target_pairs={{0,1},{1,0},{2,3},{3,2},{4,5},{5,4},{6,7},{7,6},{8,9},{9,8},{10,11... | collective-permute-start | bytes 380936 | tf_op jit(solution)/shard_map/cond/branch_0_fun/ppermute | solution.py:172
  24.8 0.0 collective-permute-done.6.refs_7_
  24.8 1.9 %ladder_first.2.before_ref = f32[384,256]{1,0:T(8,128)S(1)} custom-call(s32[62]{0:T(128)S(1)} %get-tuple-element.25.cd_ref, s32[2]{0:T(128)S(1)} %get-tuple-element.26.place_ref, bf16[24,16,128]{2,1,0:T(8,128)(2,1)S(1)} %get-tuple-element.27.table, bf16[384,7936]{1,0:T(8,128)(2,1)S(1)} %get-tuple-element.28.t_ref, ...), custom_call_target="tpu_custom_call" | custom-call | flops 780140544 | bytes 3047424 | tf_op jit(solution)/shard_map/cond/branch_0_fun/ladder_first/pallas_call | solution.py:179
  26.6 0.0 collective-permute-done.11.refs_4_
  26.7 0.0 collective-permute-done.12.refs_5_
  26.7 0.0 collective-permute-done.13.refs_6_
  26.7 0.0 collective-permute-done.14.refs_7_
  26.7 2.0 %ladder_last.2 = (f32[32,384]{1,0:T(8,128)S(1)}, f32[32,384]{1,0:T(8,128)S(1)}, f32[32,384]{1,0:T(8,128)S(1)}, f32[32,384]{1,0:T(8,128)S(1)}, f32[32,384]{1,0:T(...) custom-call(s32[62]{0:T(128)S(1)} %get-tuple-element.25.cd_ref, ...), custom_call_target="tpu_custom_call" | custom-call | flops 780140544 | bytes 3047424 | tf_op jit(solution)/shard_map/cond/branch_0_fun/ladder_last/pallas_call | solution.py:189
  28.7 5.7 %collective-permute-start.30 = (f32[32,384]{1,0:T(8,128)S(1)}, f32[32,384]{1,0:T(8,128)S(1)}, u32[]{:S(2)}, u32[]{:S(2)}) collective-permute-start(f32[32,384]{1,0:T(8,128)S(1)} %get-tuple-element.50), channel_id=1, source_target_pairs={{0,96},{16,112},{32,64},{48,80},{64,32},{80,48},{96,0},{112,16},{1... | collective-permute-start | bytes 147464 | tf_op jit(solution)/shard_map/ppermute | solution.py:151
  34.4 0.4 collective-permute-start.31
  34.8 5.3 %collective-permute-start.32 = (f32[32,384]{1,0:T(8,128)S(1)}, f32[32,384]{1,0:T(8,128)S(1)}, u32[]{:S(2)}, u32[]{:S(2)}) collective-permute-start(f32[32,384]{1,0:T(8,128)S(1)} %get-tuple-element.52), channel_id=1, source_target_pairs={{0,112},{16,64},{32,80},{48,96},{64,48},{80,0},{96,16},{112,32},{1... | collective-permute-start | bytes 147464 | tf_op jit(solution)/shard_map/ppermute | solution.py:151
  40.1 0.3 collective-permute-start.33
  40.4 0.0 collective-permute-start.34
  40.4 0.0 collective-permute-done.30
  40.4 1.1 %collective-permute-start.35 = (f32[32,384]{1,0:T(8,128)S(1)}, f32[32,384]{1,0:T(8,128)S(1)}, u32[]{:S(2)}, u32[]{:S(2)}) collective-permute-start(f32[32,384]{1,0:T(8,128)S(1)} %get-tuple-element.55), channel_id=1, source_target_pairs={{0,16},{16,32},{32,48},{48,0},{64,80},{80,96},{96,112},{112,64},{1... | collective-permute-start | bytes 147464 | tf_op jit(solution)/shard_map/ppermute | solution.py:151
  41.5 0.6 %collective-permute-done.31 = f32[32,384]{1,0:T(8,128)S(1)} collective-permute-done((f32[32,384]{1,0:T(8,128)S(1)}, f32[32,384]{1,0:T(8,128)S(1)}, u32[]{:S(2)}, u32[]{:S(2)}) %collective-permute-start.31) | collective-permute-done | bytes 49184 | tf_op jit(solution)/shard_map/ppermute | solution.py:151
  42.1 1.5 %collective-permute-start.36 = (f32[32,384]{1,0:T(8,128)S(1)}, f32[32,384]{1,0:T(8,128)S(1)}, u32[]{:S(2)}, u32[]{:S(2)}) collective-permute-start(f32[32,384]{1,0:T(8,128)S(1)} %get-tuple-element.56), channel_id=1, source_target_pairs={{0,48},{16,0},{32,16},{48,32},{64,112},{80,64},{96,80},{112,96},{1... | collective-permute-start | bytes 147464 | tf_op jit(solution)/shard_map/ppermute | solution.py:151
  43.7 0.0 copy-done.7
  43.7 0.1 dynamic_slice.3
  43.7 0.0 collective-permute-done.32
  43.7 1.9 %collective-permute-done.33 = f32[32,384]{1,0:T(8,128)S(1)} collective-permute-done((f32[32,384]{1,0:T(8,128)S(1)}, f32[32,384]{1,0:T(8,128)S(1)}, u32[]{:S(2)}, u32[]{:S(2)}) %collective-permute-start.33) | collective-permute-done | bytes 49184 | tf_op jit(solution)/shard_map/ppermute | solution.py:151
  45.7 0.4 collective-permute-done.34
  46.1 0.1 collective-permute-done.35
  46.3 0.0 collective-permute-done.36
  46.3 0.0 copy-done.6
  46.3 0.7 %fusion = bf16[384,32]{0,1:T(8,128)(2,1)} fusion(f32[384]{0:T(512)S(1)} %copy-done.6, f32[32]{0:T(128)S(1)} %dynamic_slice.3, f32[32,384]{1,0:T(8,128)S(1)} %collective-permute-done.36, f32[32,384]{1,0:T(8,128)S(1)} %collective-permute-done.35, f32[32,384]{1,0:T(8,128)S(1)} %collective-permute-done.34, f32[32,384]{1,0:T(8,128)S(1)} %collective-permute-done.33, ...), kind=kLoop, calls=%fused_computation.1 | loop fusion | flops 122880 | bytes 419456 | tf_op jit(solution)/shard_map/transpose | solution.py:217
Async XLA Ops:
  0.1 0.7 %copy-start = (s32[4]{0:T(128)S(1)}, s32[4]{0:T(128)}, u32[]{:S(2)}) copy-start(s32[4]{0:T(128)} %ab_ref.1) | copy-start | bytes 52
  0.7 2.9 %copy-start.1 = (bf16[384,7936]{1,0:T(8,128)(2,1)S(1)}, bf16[384,7936]{1,0:T(8,128)(2,1)}, u32[]{:S(2)}) copy-start(bf16[384,7936]{1,0:T(8,128)(2,1)} %param.8) | copy-start | bytes 18284548
  0.7 2.9 %copy-start.4 = (bf16[496,256]{1,0:T(8,128)(2,1)S(1)}, bf16[496,256]{1,0:T(8,128)(2,1)}, u32[]{:S(2)}) copy-start(bf16[496,256]{1,0:T(8,128)(2,1)} %v_ref.1) | copy-start | bytes 761860
  0.7 2.9 %copy-start.5 = (s32[62]{0:T(128)S(1)}, s32[62]{0:T(128)}, u32[]{:S(2)}) copy-start(s32[62]{0:T(128)} %cd_ref.1) | copy-start | bytes 748
  3.6 40.1 %copy-start.7 = (f32[256]{0:T(256)S(1)}, f32[256]{0:T(256)}, u32[]{:S(2)}) copy-start(f32[256]{0:T(256)} %param.13) | copy-start | bytes 3076
  3.6 42.7 %copy-start.6 = (f32[384]{0:T(512)S(1)}, f32[384]{0:T(512)}, u32[]{:S(2)}) copy-start(f32[384]{0:T(512)} %param.12) | copy-start | bytes 4612
  3.6 8.9 %collective-permute-start = (bf16[496,128]{1,0:T(8,128)(2,1)S(1)}, bf16[496,128]{1,0:T(8,128)(2,1)S(1)}, u32[]{:S(2)}, u32[]{:S(2)}) collective-permute-start(bf16[496,128]{1,0:T(8,128)(2,1)S(1)} %get-tuple-element.29.refs_0_), channel_id=1, source_target_pairs={{0,4},{1,5},{2,6},{3,7},{4,0},{5,1},{6,2},{7,3},{8,12},{9,13},{10,... | collective-permute-start | bytes 380936 | tf_op jit(solution)/shard_map/cond/branch_0_fun/ppermute | solution.py:169
  7.7 6.5 %collective-permute-start.1 = (bf16[496,128]{1,0:T(8,128)(2,1)S(1)}, bf16[496,128]{1,0:T(8,128)(2,1)S(1)}, u32[]{:S(2)}, u32[]{:S(2)}) collective-permute-start(bf16[496,128]{1,0:T(8,128)(2,1)S(1)} %get-tuple-element.29.refs_0_), channel_id=1, source_target_pairs={{0,2},{1,3},{2,4},{3,5},{4,6},{5,7},{6,0},{7,1},{8,10},{9,11},{10,... | collective-permute-start | bytes 380936 | tf_op jit(solution)/shard_map/cond/branch_0_fun/ppermute | solution.py:169
  8.7 5.5 %collective-permute-start.7 = (bf16[496,128]{1,0:T(8,128)(2,1)S(1)}, bf16[496,128]{1,0:T(8,128)(2,1)S(1)}, u32[]{:S(2)}, u32[]{:S(2)}) collective-permute-start(bf16[496,128]{1,0:T(8,128)(2,1)S(1)} %get-tuple-element.29.refs_0_), channel_id=1, source_target_pairs={{0,8},{1,9},{2,10},{3,11},{4,12},{5,13},{6,14},{7,15},{8,0},{9,1},... | collective-permute-start | bytes 380936 | tf_op jit(solution)/shard_map/cond/branch_0_fun/ppermute | solution.py:164
  10.3 6.3 %collective-permute-start.2 = (bf16[496,128]{1,0:T(8,128)(2,1)S(1)}, bf16[496,128]{1,0:T(8,128)(2,1)S(1)}, u32[]{:S(2)}, u32[]{:S(2)}) collective-permute-start(bf16[496,128]{1,0:T(8,128)(2,1)S(1)} %get-tuple-element.29.refs_0_), channel_id=1, source_target_pairs={{0,6},{1,7},{2,0},{3,1},{4,2},{5,3},{6,4},{7,5},{8,14},{9,15},{10,... | collective-permute-start | bytes 380936 | tf_op jit(solution)/shard_map/cond/branch_0_fun/ppermute | solution.py:169
  12.5 4.2 %collective-permute-start.3 = (bf16[496,128]{1,0:T(8,128)(2,1)S(1)}, bf16[496,128]{1,0:T(8,128)(2,1)S(1)}, u32[]{:S(2)}, u32[]{:S(2)}) collective-permute-start(bf16[496,128]{1,0:T(8,128)(2,1)S(1)} %get-tuple-element.29.refs_0_), channel_id=1, source_target_pairs={{0,1},{1,0},{2,3},{3,2},{4,5},{5,4},{6,7},{7,6},{8,9},{9,8},{10,11... | collective-permute-start | bytes 380936 | tf_op jit(solution)/shard_map/cond/branch_0_fun/ppermute | solution.py:172
  12.5 7.4 %collective-permute-start.4 = (bf16[496,128]{1,0:T(8,128)(2,1)S(1)}, bf16[496,128]{1,0:T(8,128)(2,1)S(1)}, u32[]{:S(2)}, u32[]{:S(2)}) collective-permute-start(bf16[496,128]{1,0:T(8,128)(2,1)S(1)} %collective-permute-done.refs_1_), channel_id=1, source_target_pairs={{0,1},{1,0},{2,3},{3,2},{4,5},{5,4},{6,7},{7,6},{8,9},{9,8},{10,11... | collective-permute-start | bytes 380936 | tf_op jit(solution)/shard_map/cond/branch_0_fun/ppermute | solution.py:172
  14.2 5.7 %collective-permute-start.5 = (bf16[496,128]{1,0:T(8,128)(2,1)S(1)}, bf16[496,128]{1,0:T(8,128)(2,1)S(1)}, u32[]{:S(2)}, u32[]{:S(2)}) collective-permute-start(bf16[496,128]{1,0:T(8,128)(2,1)S(1)} %collective-permute-done.1.refs_2_), channel_id=1, source_target_pairs={{0,1},{1,0},{2,3},{3,2},{4,5},{5,4},{6,7},{7,6},{8,9},{9,8},{10,11... | collective-permute-start | bytes 380936 | tf_op jit(solution)/shard_map/cond/branch_0_fun/ppermute | solution.py:172
  14.2 7.8 %collective-permute-start.8 = (bf16[496,128]{1,0:T(8,128)(2,1)S(1)}, bf16[496,128]{1,0:T(8,128)(2,1)S(1)}, u32[]{:S(2)}, u32[]{:S(2)}) collective-permute-start(bf16[496,128]{1,0:T(8,128)(2,1)S(1)} %collective-permute-done.7.refs_0_), channel_id=1, source_target_pairs={{0,4},{1,5},{2,6},{3,7},{4,0},{5,1},{6,2},{7,3},{8,12},{9,13},{10,... | collective-permute-start | bytes 380936 | tf_op jit(solution)/shard_map/cond/branch_0_fun/ppermute | solution.py:169
  16.6 7.6 %collective-permute-start.9 = (bf16[496,128]{1,0:T(8,128)(2,1)S(1)}, bf16[496,128]{1,0:T(8,128)(2,1)S(1)}, u32[]{:S(2)}, u32[]{:S(2)}) collective-permute-start(bf16[496,128]{1,0:T(8,128)(2,1)S(1)} %collective-permute-done.7.refs_0_), channel_id=1, source_target_pairs={{0,2},{1,3},{2,4},{3,5},{4,6},{5,7},{6,0},{7,1},{8,10},{9,11},{10,... | collective-permute-start | bytes 380936 | tf_op jit(solution)/shard_map/cond/branch_0_fun/ppermute | solution.py:169
  16.7 7.6 %collective-permute-start.10 = (bf16[496,128]{1,0:T(8,128)(2,1)S(1)}, bf16[496,128]{1,0:T(8,128)(2,1)S(1)}, u32[]{:S(2)}, u32[]{:S(2)}) collective-permute-start(bf16[496,128]{1,0:T(8,128)(2,1)S(1)} %collective-permute-done.7.refs_0_), channel_id=1, source_target_pairs={{0,6},{1,7},{2,0},{3,1},{4,2},{5,3},{6,4},{7,5},{8,14},{9,15},{10,... | collective-permute-start | bytes 380936 | tf_op jit(solution)/shard_map/cond/branch_0_fun/ppermute | solution.py:169
  19.9 4.9 %collective-permute-start.6 = (bf16[496,128]{1,0:T(8,128)(2,1)S(1)}, bf16[496,128]{1,0:T(8,128)(2,1)S(1)}, u32[]{:S(2)}, u32[]{:S(2)}) collective-permute-start(bf16[496,128]{1,0:T(8,128)(2,1)S(1)} %collective-permute-done.2.refs_3_), channel_id=1, source_target_pairs={{0,1},{1,0},{2,3},{3,2},{4,5},{5,4},{6,7},{7,6},{8,9},{9,8},{10,11... | collective-permute-start | bytes 380936 | tf_op jit(solution)/shard_map/cond/branch_0_fun/ppermute | solution.py:172
  19.9 6.8 %collective-permute-start.11 = (bf16[496,128]{1,0:T(8,128)(2,1)S(1)}, bf16[496,128]{1,0:T(8,128)(2,1)S(1)}, u32[]{:S(2)}, u32[]{:S(2)}) collective-permute-start(bf16[496,128]{1,0:T(8,128)(2,1)S(1)} %collective-permute-done.7.refs_0_), channel_id=1, source_target_pairs={{0,1},{1,0},{2,3},{3,2},{4,5},{5,4},{6,7},{7,6},{8,9},{9,8},{10,11... | collective-permute-start | bytes 380936 | tf_op jit(solution)/shard_map/cond/branch_0_fun/ppermute | solution.py:172
  22.0 4.7 %collective-permute-start.12 = (bf16[496,128]{1,0:T(8,128)(2,1)S(1)}, bf16[496,128]{1,0:T(8,128)(2,1)S(1)}, u32[]{:S(2)}, u32[]{:S(2)}) collective-permute-start(bf16[496,128]{1,0:T(8,128)(2,1)S(1)} %collective-permute-done.8.refs_1_), channel_id=1, source_target_pairs={{0,1},{1,0},{2,3},{3,2},{4,5},{5,4},{6,7},{7,6},{8,9},{9,8},{10,11... | collective-permute-start | bytes 380936 | tf_op jit(solution)/shard_map/cond/branch_0_fun/ppermute | solution.py:172
  24.3 2.4 %collective-permute-start.13 = (bf16[496,128]{1,0:T(8,128)(2,1)S(1)}, bf16[496,128]{1,0:T(8,128)(2,1)S(1)}, u32[]{:S(2)}, u32[]{:S(2)}) collective-permute-start(bf16[496,128]{1,0:T(8,128)(2,1)S(1)} %collective-permute-done.9.refs_2_), channel_id=1, source_target_pairs={{0,1},{1,0},{2,3},{3,2},{4,5},{5,4},{6,7},{7,6},{8,9},{9,8},{10,11... | collective-permute-start | bytes 380936 | tf_op jit(solution)/shard_map/cond/branch_0_fun/ppermute | solution.py:172
  24.3 2.4 %collective-permute-start.14 = (bf16[496,128]{1,0:T(8,128)(2,1)S(1)}, bf16[496,128]{1,0:T(8,128)(2,1)S(1)}, u32[]{:S(2)}, u32[]{:S(2)}) collective-permute-start(bf16[496,128]{1,0:T(8,128)(2,1)S(1)} %collective-permute-done.10.refs_3_), channel_id=1, source_target_pairs={{0,1},{1,0},{2,3},{3,2},{4,5},{5,4},{6,7},{7,6},{8,9},{9,8},{10,11... | collective-permute-start | bytes 380936 | tf_op jit(solution)/shard_map/cond/branch_0_fun/ppermute | solution.py:172
  28.7 11.7 %collective-permute-start.30 = (f32[32,384]{1,0:T(8,128)S(1)}, f32[32,384]{1,0:T(8,128)S(1)}, u32[]{:S(2)}, u32[]{:S(2)}) collective-permute-start(f32[32,384]{1,0:T(8,128)S(1)} %get-tuple-element.50), channel_id=1, source_target_pairs={{0,96},{16,112},{32,64},{48,80},{64,32},{80,48},{96,0},{112,16},{1... | collective-permute-start | bytes 147464 | tf_op jit(solution)/shard_map/ppermute | solution.py:151
  34.4 7.7 %collective-permute-start.31 = (f32[32,384]{1,0:T(8,128)S(1)}, f32[32,384]{1,0:T(8,128)S(1)}, u32[]{:S(2)}, u32[]{:S(2)}) collective-permute-start(f32[32,384]{1,0:T(8,128)S(1)} %get-tuple-element.51), channel_id=1, source_target_pairs={{0,80},{16,96},{32,112},{48,64},{64,16},{80,32},{96,48},{112,0},{1... | collective-permute-start | bytes 147464 | tf_op jit(solution)/shard_map/ppermute | solution.py:151
  34.8 8.9 %collective-permute-start.32 = (f32[32,384]{1,0:T(8,128)S(1)}, f32[32,384]{1,0:T(8,128)S(1)}, u32[]{:S(2)}, u32[]{:S(2)}) collective-permute-start(f32[32,384]{1,0:T(8,128)S(1)} %get-tuple-element.52), channel_id=1, source_target_pairs={{0,112},{16,64},{32,80},{48,96},{64,48},{80,0},{96,16},{112,32},{1... | collective-permute-start | bytes 147464 | tf_op jit(solution)/shard_map/ppermute | solution.py:151
  40.1 5.6 %collective-permute-start.33 = (f32[32,384]{1,0:T(8,128)S(1)}, f32[32,384]{1,0:T(8,128)S(1)}, u32[]{:S(2)}, u32[]{:S(2)}) collective-permute-start(f32[32,384]{1,0:T(8,128)S(1)} %get-tuple-element.53), channel_id=1, source_target_pairs={{0,64},{16,80},{32,96},{48,112},{64,0},{80,16},{96,32},{112,48},{1... | collective-permute-start | bytes 147464 | tf_op jit(solution)/shard_map/ppermute | solution.py:151
  40.4 5.7 %collective-permute-start.34 = (f32[32,384]{1,0:T(8,128)S(1)}, f32[32,384]{1,0:T(8,128)S(1)}, u32[]{:S(2)}, u32[]{:S(2)}) collective-permute-start(f32[32,384]{1,0:T(8,128)S(1)} %get-tuple-element.54), channel_id=1, source_target_pairs={{0,32},{16,48},{32,0},{48,16},{64,96},{80,112},{96,64},{112,80},{1... | collective-permute-start | bytes 147464 | tf_op jit(solution)/shard_map/ppermute | solution.py:151
  40.4 5.8 %collective-permute-start.35 = (f32[32,384]{1,0:T(8,128)S(1)}, f32[32,384]{1,0:T(8,128)S(1)}, u32[]{:S(2)}, u32[]{:S(2)}) collective-permute-start(f32[32,384]{1,0:T(8,128)S(1)} %get-tuple-element.55), channel_id=1, source_target_pairs={{0,16},{16,32},{32,48},{48,0},{64,80},{80,96},{96,112},{112,64},{1... | collective-permute-start | bytes 147464 | tf_op jit(solution)/shard_map/ppermute | solution.py:151
  42.1 4.1 %collective-permute-start.36 = (f32[32,384]{1,0:T(8,128)S(1)}, f32[32,384]{1,0:T(8,128)S(1)}, u32[]{:S(2)}, u32[]{:S(2)}) collective-permute-start(f32[32,384]{1,0:T(8,128)S(1)} %get-tuple-element.56), channel_id=1, source_target_pairs={{0,48},{16,0},{32,16},{48,32},{64,112},{80,64},{96,80},{112,96},{1... | collective-permute-start | bytes 147464 | tf_op jit(solution)/shard_map/ppermute | solution.py:151

commit v5 on v4

--- a/solution.py
+++ b/solution.py
@@ -12,6 +12,7 @@
 LANES = 128
 LABELS = 4
 KINDS = 3
+TABLE = pltpu.VMEM((LABELS * 2 * KINDS, SUB, LANES), jnp.bfloat16)
 VMEM = pltpu.VMEM
 SMEM = pltpu.SMEM
 IN_SMEM = pl.BlockSpec(memory_space=SMEM)
@@ -73,10 +74,10 @@
         out_shape=(
             jax.ShapeDtypeStruct((integrals.shape[0], LANES), jnp.bfloat16),
             jax.ShapeDtypeStruct((1,), jnp.int32),
-            jax.ShapeDtypeStruct((LABELS * 2 * KINDS, SUB, LANES), jnp.bfloat16),
         ),
         in_specs=[IN_SMEM, IN_SMEM, IN_SMEM, IN_VMEM],
-        out_specs=(IN_VMEM, IN_SMEM, IN_VMEM),
+        out_specs=(IN_VMEM, IN_SMEM),
+        scratch_shapes=[TABLE],
         compiler_params=pltpu.CompilerParams(vmem_limit_bytes=2 * 2**20),
         cost_estimate=pl.CostEstimate(flops=10**10, bytes_accessed=2 * integrals.size, transcendentals=0),
         name="pack",
@@ -118,16 +119,18 @@
     return jnp.dot(t_ref[:, cols], masked[...], preferred_element_type=jnp.float32)
 
 
-def first_kernel(cd_ref, place_ref, table, t_ref, *refs):
+def first_kernel(cd_ref, ab_ref, place_ref, t_ref, *refs):
     piece_refs = refs[:8]
-    o_ref, held, masked = refs[8:]
+    o_ref, held, masked, table = refs[8:]
+    fill_factors(ab_ref, table)
     half_ladder(0, cd_ref, place_ref, table, piece_refs, held, masked)
     o_ref[...] = half_product(0, place_ref, t_ref, masked)
 
 
-def last_kernel(cd_ref, place_ref, table, t_ref, before_ref, *refs):
+def last_kernel(cd_ref, ab_ref, place_ref, t_ref, before_ref, *refs):
     piece_refs, out_refs = refs[:8], refs[8:16]
-    held, masked, total = refs[16:]
+    held, masked, table, total = refs[16:]
+    fill_factors(ab_ref, table)
     half_ladder(1, cd_ref, place_ref, table, piece_refs, held, masked)
     total[...] = (before_ref[...] + half_product(1, place_ref, t_ref, masked)).T
     row = place_ref[1]
@@ -138,7 +141,7 @@
         ref[...] = total[pl.ds(pl.multiple_of(target * share, 8), share), :]
 
 
-TARGETS = [(0, 0), (1, 2), (1, 1), (1, 3), (1, 0), (0, 2), (0, 1), (0, 3)]
+TARGETS = [(0, 0), (1, 3), (1, 2), (1, 1), (1, 0), (0, 2), (0, 1), (0, 3)]
 
 
 def row_hop(dy, dx):
@@ -160,7 +163,7 @@
     return [(i, ((i // 8 ^ dy) * 4 + (i // 2 + dz) % 4) * 2 + i % 2) for i in range(16)]
 
 
-def partial_ladder(packed, table, amplitudes, cd_irrep, place):
+def partial_ladder(packed, amplitudes, cd_irrep, ab_irrep, place):
     across = lax.ppermute(packed, "col", hop(1, 0))
     pieces = []
     for start in (packed, across):
@@ -173,34 +176,34 @@
         pieces.append(mine + theirs)
     ij, cds = amplitudes.shape
     width, cols = 2 * LANES, cds // 2
-    scratch = [VMEM((cols, packed.shape[1]), jnp.bfloat16), VMEM((cols, width), jnp.bfloat16)]
+    scratch = [VMEM((cols, packed.shape[1]), jnp.bfloat16), VMEM((cols, width), jnp.bfloat16), TABLE]
     cost = pl.CostEstimate(flops=ij * cds * width, bytes_accessed=ij * cds, transcendentals=0)
     limits = pltpu.CompilerParams(vmem_limit_bytes=12 * 2**20)
     half = pl.pallas_call(
         first_kernel,
         out_shape=jax.ShapeDtypeStruct((ij, width), jnp.float32),
-        in_specs=[IN_SMEM] * 2 + [IN_VMEM] * 10,
+        in_specs=[IN_SMEM] * 3 + [IN_VMEM] * 9,
         out_specs=IN_VMEM,
         scratch_shapes=scratch,
         compiler_params=limits,
         cost_estimate=cost,
         name="ladder_first",
-    )(cd_irrep, place, table, amplitudes, *pieces[0])
+    )(cd_irrep, ab_irrep, place, amplitudes, *pieces[0])
     return pl.pallas_call(
         last_kernel,
         out_shape=[jax.ShapeDtypeStruct((width // 8, ij), jnp.float32)] * 8,
-        in_specs=[IN_SMEM] * 2 + [IN_VMEM] * 11,
+        in_specs=[IN_SMEM] * 3 + [IN_VMEM] * 10,
         out_specs=[IN_VMEM] * 8,
         scratch_shapes=scratch + [VMEM((width, ij), jnp.float32)],
         compiler_params=limits,
         cost_estimate=cost,
         name="ladder_last",
-    )(cd_irrep, place, table, amplitudes, half, *pieces[1])
+    )(cd_irrep, ab_irrep, place, amplitudes, half, *pieces[1])
 
 
 def shards(amplitudes, integrals, cd_irrep, ab_irrep, pair_energy, panel_energy):
     place = jnp.stack([lax.axis_index("col"), lax.axis_index("row")]).astype(jnp.int32)
-    packed, most, table = pack(cd_irrep, ab_irrep, place, integrals)
+    packed, most = pack(cd_irrep, ab_irrep, place, integrals)
 
     def narrow(packed, integrals, *rest):
         return partial_ladder(packed, *rest)
@@ -208,7 +211,7 @@
     def whole(packed, integrals, *rest):
         return partial_ladder(integrals, *rest)
 
-    blocks = lax.cond(most[0] > 2, whole, narrow, packed, integrals, table, amplitudes, cd_irrep, place)
+    blocks = lax.cond(most[0] > 2, whole, narrow, packed, integrals, amplitudes, cd_irrep, ab_irrep, place)
     parts = reduce_parts(blocks)
     share = parts[0].shape[0]
     summed = sum(parts[1:], parts[0])

time: 47.2 us -> 46.5 us (0.985)
  local copies, waits for them, and re-layouts: 0.97 us -> 0.31 us
    unnamed x12, local copies, waits for them, and re-layouts: 0.9 us -> 0.24 us
where the time goes in v5:
time: 46.5 us
  starting transfers between devices  30.8 us (66%)
  waiting for transfers between devices  7.94 us (17%)
  Pallas kernels  5.74 us (12%)
  between operations  0.83 us (2%)
  other arithmetic  0.77 us (2%)
    ppermute x7, starting transfers between devices, reduce_parts(): parts.append(lax.ppermute(block, 'row', row_hop(*TARGETS[n])))  14.7 us
    ppermute x6, starting transfers between devices, partial_ladder(): mine.append(lax.ppermute(start, 'col', hop(0, dz)))  12.9 us
    ppermute x6, waiting for transfers between devices, partial_ladder(): mine.append(lax.ppermute(start, 'col', hop(0, dz)))  5.08 us
    ppermute x7, waiting for transfers between devices, reduce_parts(): parts.append(lax.ppermute(block, 'row', row_hop(*TARGETS[n])))  2.83 us
    pallas_call x1, Pallas kernels, partial_ladder(): pl.pallas_call(last_kernel, out_shape=[jax.ShapeDtypeStruct((width // 8,...  2.03 us
    pallas_call x1, Pallas kernels, partial_ladder(): pl.pallas_call(first_kernel, out_shape=jax.ShapeDtypeStruct((ij, width),...  1.88 us
    pallas_call x1, Pallas kernels, pack(): pl.pallas_call(pack_kernel, out_shape=(jax.ShapeDtypeStruct((integrals.sh...  1.83 us
    ppermute x1, starting transfers between devices, partial_ladder(): across = lax.ppermute(packed, 'col', hop(1, 0))  1.58 us
  transfers between devices with their start and end apart: 22, of which 7 were waited for; matrix products, arithmetic and copies ran while one was open for 0% of the time, Pallas kernels for 4%

profile of v5, /device:TPU:0, one launch (start us, length us, event | category | flops | bytes accessed | tf_op | source)
XLA Modules:
  0.0 46.5 jit_solution(4520535002560119228)
XLA Ops:
  0.0 0.1 pad_add_fusion.place_ref
  0.1 0.0 copy-start
  0.1 0.0 copy-start.3
  0.1 0.0 copy-start.4
  0.1 0.0 copy-start.5
  0.1 1.8 %pack.1 = (bf16[496,128]{1,0:T(8,128)(2,1)S(1)}, s32[1]{0:T(128)}) custom-call(s32[62]{0:T(128)} %cd_ref.1, s32[4]{0:T(128)} %ab_ref.1, s32[2]{0:T(128)S(1)} %pad_add_fusion.place_ref, bf16[496,256]{1,0:T(8,128)(2,1)} %v_ref.1), custom_call_target="tpu_custom_call" | custom-call | flops 10000000000 | bytes 253952 | tf_op jit(solution)/shard_map/pack/pallas_call | solution.py:72
  2.7 0.2 copy-done
  2.9 0.0 copy-done.3
  2.9 0.0 copy-done.4
  2.9 0.0 copy-done.5
  2.9 0.0 copy-start.7
  2.9 0.0 copy-start.6
  3.0 25.2 %conditional.1 = ((f32[32,384]{1,0:T(8,128)S(1)}, f32[32,384]{1,0:T(8,128)S(1)}, f32[32,384]{1,0:T(8,128)S(1)}, f32[32,384]{1,0:T(8,128)S(1)}, f32[32,384]{1,0:T...) conditional(s32[]{:T(128)} %bitcast.2, (bf16[496,128]{1,0:T(8,128)(2,1)S(1)}, ...), branch_computations={%region_0.0_spmd, %region_1.0_spmd} | conditional | flops 1560281088 | bytes 70091416 | solution.py:214
  3.0 4.1 %collective-permute-start = (bf16[496,128]{1,0:T(8,128)(2,1)S(1)}, bf16[496,128]{1,0:T(8,128)(2,1)S(1)}, u32[]{:S(2)}, u32[]{:S(2)}) collective-permute-start(bf16[496,128]{1,0:T(8,128)(2,1)S(1)} %get-tuple-element.29.refs_0_), channel_id=1, source_target_pairs={{0,4},{1,5},{2,6},{3,7},{4,0},{5,1},{6,2},{7,3},{8,12},{9,13},{10,... | collective-permute-start | bytes 380936 | tf_op jit(solution)/shard_map/cond/branch_0_fun/ppermute | solution.py:172
  7.0 1.0 %collective-permute-start.1 = (bf16[496,128]{1,0:T(8,128)(2,1)S(1)}, bf16[496,128]{1,0:T(8,128)(2,1)S(1)}, u32[]{:S(2)}, u32[]{:S(2)}) collective-permute-start(bf16[496,128]{1,0:T(8,128)(2,1)S(1)} %get-tuple-element.29.refs_0_), channel_id=1, source_target_pairs={{0,2},{1,3},{2,4},{3,5},{4,6},{5,7},{6,0},{7,1},{8,10},{9,11},{10,... | collective-permute-start | bytes 380936 | tf_op jit(solution)/shard_map/cond/branch_0_fun/ppermute | solution.py:172
  8.1 1.6 %collective-permute-start.7 = (bf16[496,128]{1,0:T(8,128)(2,1)S(1)}, bf16[496,128]{1,0:T(8,128)(2,1)S(1)}, u32[]{:S(2)}, u32[]{:S(2)}) collective-permute-start(bf16[496,128]{1,0:T(8,128)(2,1)S(1)} %get-tuple-element.29.refs_0_), channel_id=1, source_target_pairs={{0,8},{1,9},{2,10},{3,11},{4,12},{5,13},{6,14},{7,15},{8,0},{9,1},... | collective-permute-start | bytes 380936 | tf_op jit(solution)/shard_map/cond/branch_0_fun/ppermute | solution.py:167
  9.6 2.2 %collective-permute-start.2 = (bf16[496,128]{1,0:T(8,128)(2,1)S(1)}, bf16[496,128]{1,0:T(8,128)(2,1)S(1)}, u32[]{:S(2)}, u32[]{:S(2)}) collective-permute-start(bf16[496,128]{1,0:T(8,128)(2,1)S(1)} %get-tuple-element.29.refs_0_), channel_id=1, source_target_pairs={{0,6},{1,7},{2,0},{3,1},{4,2},{5,3},{6,4},{7,5},{8,14},{9,15},{10,... | collective-permute-start | bytes 380936 | tf_op jit(solution)/shard_map/cond/branch_0_fun/ppermute | solution.py:172
  11.8 0.0 collective-permute-start.3
  11.8 0.0 collective-permute-done.refs_1_
  11.9 0.5 %collective-permute-start.4 = (bf16[496,128]{1,0:T(8,128)(2,1)S(1)}, bf16[496,128]{1,0:T(8,128)(2,1)S(1)}, u32[]{:S(2)}, u32[]{:S(2)}) collective-permute-start(bf16[496,128]{1,0:T(8,128)(2,1)S(1)} %collective-permute-done.refs_1_), channel_id=1, source_target_pairs={{0,1},{1,0},{2,3},{3,2},{4,5},{5,4},{6,7},{7,6},{8,9},{9,8},{10,11... | collective-permute-start | bytes 380936 | tf_op jit(solution)/shard_map/cond/branch_0_fun/ppermute | solution.py:175
  12.4 1.2 %collective-permute-done.1.refs_2_ = bf16[496,128]{1,0:T(8,128)(2,1)S(1)} collective-permute-done((bf16[496,128]{1,0:T(8,128)(2,1)S(1)}, bf16[496,128]{1,0:T(8,128)(2,1)S(1)}, u32[]{:S(2)}, u32[]{:S(2)}) %collective-permute-start.1) | collective-permute-done | bytes 127008 | tf_op jit(solution)/shard_map/cond/branch_0_fun/ppermute | solution.py:172
  13.6 0.0 collective-permute-start.5
  13.6 0.0 collective-permute-done.7.refs_0_
  13.6 2.4 %collective-permute-start.8 = (bf16[496,128]{1,0:T(8,128)(2,1)S(1)}, bf16[496,128]{1,0:T(8,128)(2,1)S(1)}, u32[]{:S(2)}, u32[]{:S(2)}) collective-permute-start(bf16[496,128]{1,0:T(8,128)(2,1)S(1)} %collective-permute-done.7.refs_0_), channel_id=1, source_target_pairs={{0,4},{1,5},{2,6},{3,7},{4,0},{5,1},{6,2},{7,3},{8,12},{9,13},{10,... | collective-permute-start | bytes 380936 | tf_op jit(solution)/shard_map/cond/branch_0_fun/ppermute | solution.py:172
  16.0 0.0 collective-permute-done.2.refs_3_
  16.0 0.1 collective-permute-start.9
  16.1 0.0 collective-permute-done.3.refs_4_
  16.1 3.2 %collective-permute-start.10 = (bf16[496,128]{1,0:T(8,128)(2,1)S(1)}, bf16[496,128]{1,0:T(8,128)(2,1)S(1)}, u32[]{:S(2)}, u32[]{:S(2)}) collective-permute-start(bf16[496,128]{1,0:T(8,128)(2,1)S(1)} %collective-permute-done.7.refs_0_), channel_id=1, source_target_pairs={{0,6},{1,7},{2,0},{3,1},{4,2},{5,3},{6,4},{7,5},{8,14},{9,15},{10,... | collective-permute-start | bytes 380936 | tf_op jit(solution)/shard_map/cond/branch_0_fun/ppermute | solution.py:172
  19.2 0.0 collective-permute-done.4.refs_5_
  19.2 0.0 collective-permute-start.6
  19.2 0.0 collective-permute-done.5.refs_6_
  19.2 0.5 %collective-permute-start.11 = (bf16[496,128]{1,0:T(8,128)(2,1)S(1)}, bf16[496,128]{1,0:T(8,128)(2,1)S(1)}, u32[]{:S(2)}, u32[]{:S(2)}) collective-permute-start(bf16[496,128]{1,0:T(8,128)(2,1)S(1)} %collective-permute-done.7.refs_0_), channel_id=1, source_target_pairs={{0,1},{1,0},{2,3},{3,2},{4,5},{5,4},{6,7},{7,6},{8,9},{9,8},{10,11... | collective-permute-start | bytes 380936 | tf_op jit(solution)/shard_map/cond/branch_0_fun/ppermute | solution.py:175
  19.7 1.6 %collective-permute-done.8.refs_1_ = bf16[496,128]{1,0:T(8,128)(2,1)S(1)} collective-permute-done((bf16[496,128]{1,0:T(8,128)(2,1)S(1)}, bf16[496,128]{1,0:T(8,128)(2,1)S(1)}, u32[]{:S(2)}, u32[]{:S(2)}) %collective-permute-start.8) | collective-permute-done | bytes 127008 | tf_op jit(solution)/shard_map/cond/branch_0_fun/ppermute | solution.py:172
  21.4 0.0 collective-permute-start.12
  21.4 2.3 %collective-permute-done.9.refs_2_ = bf16[496,128]{1,0:T(8,128)(2,1)S(1)} collective-permute-done((bf16[496,128]{1,0:T(8,128)(2,1)S(1)}, bf16[496,128]{1,0:T(8,128)(2,1)S(1)}, u32[]{:S(2)}, u32[]{:S(2)}) %collective-permute-start.9) | collective-permute-done | bytes 127008 | tf_op jit(solution)/shard_map/cond/branch_0_fun/ppermute | solution.py:172
  23.6 0.0 collective-permute-start.13
  23.6 0.0 collective-permute-done.10.refs_3_
  23.6 0.5 %collective-permute-start.14 = (bf16[496,128]{1,0:T(8,128)(2,1)S(1)}, bf16[496,128]{1,0:T(8,128)(2,1)S(1)}, u32[]{:S(2)}, u32[]{:S(2)}) collective-permute-start(bf16[496,128]{1,0:T(8,128)(2,1)S(1)} %collective-permute-done.10.refs_3_), channel_id=1, source_target_pairs={{0,1},{1,0},{2,3},{3,2},{4,5},{5,4},{6,7},{7,6},{8,9},{9,8},{10,11... | collective-permute-start | bytes 380936 | tf_op jit(solution)/shard_map/cond/branch_0_fun/ppermute | solution.py:175
  24.1 0.0 collective-permute-done.6.refs_7_
  24.1 1.9 %ladder_first.2.before_ref = f32[384,256]{1,0:T(8,128)S(1)} custom-call(s32[62]{0:T(128)S(1)} %get-tuple-element.25.cd_ref, s32[4]{0:T(128)S(1)} %get-tuple-element.26.ab_ref, s32[2]{0:T(128)S(1)} %get-tuple-element.27.place_ref, bf16[384,7936]{1,0:T(8,128)(2,1)S(1)} %get-tuple-element.28.t_ref, bf16[496,128]{1,0:T(8,128)(2,1)S(1)} %get-tuple-element.29.refs_0_, ...), custom_call_target="tpu_custom_call" | custom-call | flops 780140544 | bytes 3047424 | tf_op jit(solution)/shard_map/cond/branch_0_fun/ladder_first/pallas_call | solution.py:182
  26.0 0.0 collective-permute-done.11.refs_4_
  26.0 0.0 collective-permute-done.12.refs_5_
  26.0 0.0 collective-permute-done.13.refs_6_
  26.1 0.0 collective-permute-done.14.refs_7_
  26.1 2.0 %ladder_last.2 = (f32[32,384]{1,0:T(8,128)S(1)}, f32[32,384]{1,0:T(8,128)S(1)}, f32[32,384]{1,0:T(8,128)S(1)}, f32[32,384]{1,0:T(8,128)S(1)}, f32[32,384]{1,0:T(...) custom-call(s32[62]{0:T(128)S(1)} %get-tuple-element.25.cd_ref, ...), custom_call_target="tpu_custom_call" | custom-call | flops 780140544 | bytes 3047424 | tf_op jit(solution)/shard_map/cond/branch_0_fun/ladder_last/pallas_call | solution.py:192
  28.1 5.5 %collective-permute-start.30 = (f32[32,384]{1,0:T(8,128)S(1)}, f32[32,384]{1,0:T(8,128)S(1)}, u32[]{:S(2)}, u32[]{:S(2)}) collective-permute-start(f32[32,384]{1,0:T(8,128)S(1)} %get-tuple-element.48), channel_id=1, source_target_pairs={{0,112},{16,64},{32,80},{48,96},{64,48},{80,0},{96,16},{112,32},{1... | collective-permute-start | bytes 147464 | tf_op jit(solution)/shard_map/ppermute | solution.py:154
  33.6 0.6 %collective-permute-start.31 = (f32[32,384]{1,0:T(8,128)S(1)}, f32[32,384]{1,0:T(8,128)S(1)}, u32[]{:S(2)}, u32[]{:S(2)}) collective-permute-start(f32[32,384]{1,0:T(8,128)S(1)} %get-tuple-element.49), channel_id=1, source_target_pairs={{0,96},{16,112},{32,64},{48,80},{64,32},{80,48},{96,0},{112,16},{1... | collective-permute-start | bytes 147464 | tf_op jit(solution)/shard_map/ppermute | solution.py:154
  34.1 3.5 %collective-permute-start.32 = (f32[32,384]{1,0:T(8,128)S(1)}, f32[32,384]{1,0:T(8,128)S(1)}, u32[]{:S(2)}, u32[]{:S(2)}) collective-permute-start(f32[32,384]{1,0:T(8,128)S(1)} %get-tuple-element.50), channel_id=1, source_target_pairs={{0,80},{16,96},{32,112},{48,64},{64,16},{80,32},{96,48},{112,0},{1... | collective-permute-start | bytes 147464 | tf_op jit(solution)/shard_map/ppermute | solution.py:154
  37.7 0.3 collective-permute-start.33
  38.0 2.1 %collective-permute-start.34 = (f32[32,384]{1,0:T(8,128)S(1)}, f32[32,384]{1,0:T(8,128)S(1)}, u32[]{:S(2)}, u32[]{:S(2)}) collective-permute-start(f32[32,384]{1,0:T(8,128)S(1)} %get-tuple-element.52), channel_id=1, source_target_pairs={{0,32},{16,48},{32,0},{48,16},{64,96},{80,112},{96,64},{112,80},{1... | collective-permute-start | bytes 147464 | tf_op jit(solution)/shard_map/ppermute | solution.py:154
  40.1 0.0 collective-permute-done.30
  40.1 1.1 %collective-permute-start.35 = (f32[32,384]{1,0:T(8,128)S(1)}, f32[32,384]{1,0:T(8,128)S(1)}, u32[]{:S(2)}, u32[]{:S(2)}) collective-permute-start(f32[32,384]{1,0:T(8,128)S(1)} %get-tuple-element.53), channel_id=1, source_target_pairs={{0,16},{16,32},{32,48},{48,0},{64,80},{80,96},{96,112},{112,64},{1... | collective-permute-start | bytes 147464 | tf_op jit(solution)/shard_map/ppermute | solution.py:154
  41.2 0.5 collective-permute-done.31
  41.7 1.6 %collective-permute-start.36 = (f32[32,384]{1,0:T(8,128)S(1)}, f32[32,384]{1,0:T(8,128)S(1)}, u32[]{:S(2)}, u32[]{:S(2)}) collective-permute-start(f32[32,384]{1,0:T(8,128)S(1)} %get-tuple-element.54), channel_id=1, source_target_pairs={{0,48},{16,0},{32,16},{48,32},{64,112},{80,64},{96,80},{112,96},{1... | collective-permute-start | bytes 147464 | tf_op jit(solution)/shard_map/ppermute | solution.py:154
  43.3 0.0 copy-done.7
  43.3 0.1 dynamic_slice.3
  43.4 0.0 collective-permute-done.32
  43.4 0.0 collective-permute-done.33
  43.4 0.7 %collective-permute-done.34 = f32[32,384]{1,0:T(8,128)S(1)} collective-permute-done((f32[32,384]{1,0:T(8,128)S(1)}, f32[32,384]{1,0:T(8,128)S(1)}, u32[]{:S(2)}, u32[]{:S(2)}) %collective-permute-start.34) | collective-permute-done | bytes 49184 | tf_op jit(solution)/shard_map/ppermute | solution.py:154
  44.1 1.3 %collective-permute-done.35 = f32[32,384]{1,0:T(8,128)S(1)} collective-permute-done((f32[32,384]{1,0:T(8,128)S(1)}, f32[32,384]{1,0:T(8,128)S(1)}, u32[]{:S(2)}, u32[]{:S(2)}) %collective-permute-start.35) | collective-permute-done | bytes 49184 | tf_op jit(solution)/shard_map/ppermute | solution.py:154
  45.4 0.4 collective-permute-done.36
  45.8 0.0 copy-done.6
  45.8 0.7 %fusion = bf16[384,32]{0,1:T(8,128)(2,1)} fusion(f32[384]{0:T(512)S(1)} %copy-done.6, f32[32]{0:T(128)S(1)} %dynamic_slice.3, f32[32,384]{1,0:T(8,128)S(1)} %collective-permute-done.36, f32[32,384]{1,0:T(8,128)S(1)} %collective-permute-done.35, f32[32,384]{1,0:T(8,128)S(1)} %collective-permute-done.34, f32[32,384]{1,0:T(8,128)S(1)} %collective-permute-done.33, ...), kind=kLoop, calls=%fused_computation.1 | loop fusion | flops 122880 | bytes 419456 | tf_op jit(solution)/shard_map/transpose | solution.py:220
Async XLA Ops:
  0.1 2.9 %copy-start = (bf16[384,7936]{1,0:T(8,128)(2,1)S(1)}, bf16[384,7936]{1,0:T(8,128)(2,1)}, u32[]{:S(2)}) copy-start(bf16[384,7936]{1,0:T(8,128)(2,1)} %param.8) | copy-start | bytes 18284548
  0.1 2.9 %copy-start.3 = (bf16[496,256]{1,0:T(8,128)(2,1)S(1)}, bf16[496,256]{1,0:T(8,128)(2,1)}, u32[]{:S(2)}) copy-start(bf16[496,256]{1,0:T(8,128)(2,1)} %v_ref.1) | copy-start | bytes 761860
  0.1 2.9 %copy-start.4 = (s32[62]{0:T(128)S(1)}, s32[62]{0:T(128)}, u32[]{:S(2)}) copy-start(s32[62]{0:T(128)} %cd_ref.1) | copy-start | bytes 748
  0.1 2.9 %copy-start.5 = (s32[4]{0:T(128)S(1)}, s32[4]{0:T(128)}, u32[]{:S(2)}) copy-start(s32[4]{0:T(128)} %ab_ref.1) | copy-start | bytes 52
  2.9 40.4 %copy-start.7 = (f32[256]{0:T(256)S(1)}, f32[256]{0:T(256)}, u32[]{:S(2)}) copy-start(f32[256]{0:T(256)} %param.13) | copy-start | bytes 3076
  2.9 42.8 %copy-start.6 = (f32[384]{0:T(512)S(1)}, f32[384]{0:T(512)}, u32[]{:S(2)}) copy-start(f32[384]{0:T(512)} %param.12) | copy-start | bytes 4612
  3.0 8.9 %collective-permute-start = (bf16[496,128]{1,0:T(8,128)(2,1)S(1)}, bf16[496,128]{1,0:T(8,128)(2,1)S(1)}, u32[]{:S(2)}, u32[]{:S(2)}) collective-permute-start(bf16[496,128]{1,0:T(8,128)(2,1)S(1)} %get-tuple-element.29.refs_0_), channel_id=1, source_target_pairs={{0,4},{1,5},{2,6},{3,7},{4,0},{5,1},{6,2},{7,3},{8,12},{9,13},{10,... | collective-permute-start | bytes 380936 | tf_op jit(solution)/shard_map/cond/branch_0_fun/ppermute | solution.py:172
  7.0 6.5 %collective-permute-start.1 = (bf16[496,128]{1,0:T(8,128)(2,1)S(1)}, bf16[496,128]{1,0:T(8,128)(2,1)S(1)}, u32[]{:S(2)}, u32[]{:S(2)}) collective-permute-start(bf16[496,128]{1,0:T(8,128)(2,1)S(1)} %get-tuple-element.29.refs_0_), channel_id=1, source_target_pairs={{0,2},{1,3},{2,4},{3,5},{4,6},{5,7},{6,0},{7,1},{8,10},{9,11},{10,... | collective-permute-start | bytes 380936 | tf_op jit(solution)/shard_map/cond/branch_0_fun/ppermute | solution.py:172
  8.1 5.5 %collective-permute-start.7 = (bf16[496,128]{1,0:T(8,128)(2,1)S(1)}, bf16[496,128]{1,0:T(8,128)(2,1)S(1)}, u32[]{:S(2)}, u32[]{:S(2)}) collective-permute-start(bf16[496,128]{1,0:T(8,128)(2,1)S(1)} %get-tuple-element.29.refs_0_), channel_id=1, source_target_pairs={{0,8},{1,9},{2,10},{3,11},{4,12},{5,13},{6,14},{7,15},{8,0},{9,1},... | collective-permute-start | bytes 380936 | tf_op jit(solution)/shard_map/cond/branch_0_fun/ppermute | solution.py:167
  9.6 6.3 %collective-permute-start.2 = (bf16[496,128]{1,0:T(8,128)(2,1)S(1)}, bf16[496,128]{1,0:T(8,128)(2,1)S(1)}, u32[]{:S(2)}, u32[]{:S(2)}) collective-permute-start(bf16[496,128]{1,0:T(8,128)(2,1)S(1)} %get-tuple-element.29.refs_0_), channel_id=1, source_target_pairs={{0,6},{1,7},{2,0},{3,1},{4,2},{5,3},{6,4},{7,5},{8,14},{9,15},{10,... | collective-permute-start | bytes 380936 | tf_op jit(solution)/shard_map/cond/branch_0_fun/ppermute | solution.py:172
  11.8 4.2 %collective-permute-start.3 = (bf16[496,128]{1,0:T(8,128)(2,1)S(1)}, bf16[496,128]{1,0:T(8,128)(2,1)S(1)}, u32[]{:S(2)}, u32[]{:S(2)}) collective-permute-start(bf16[496,128]{1,0:T(8,128)(2,1)S(1)} %get-tuple-element.29.refs_0_), channel_id=1, source_target_pairs={{0,1},{1,0},{2,3},{3,2},{4,5},{5,4},{6,7},{7,6},{8,9},{9,8},{10,11... | collective-permute-start | bytes 380936 | tf_op jit(solution)/shard_map/cond/branch_0_fun/ppermute | solution.py:175
  11.9 7.4 %collective-permute-start.4 = (bf16[496,128]{1,0:T(8,128)(2,1)S(1)}, bf16[496,128]{1,0:T(8,128)(2,1)S(1)}, u32[]{:S(2)}, u32[]{:S(2)}) collective-permute-start(bf16[496,128]{1,0:T(8,128)(2,1)S(1)} %collective-permute-done.refs_1_), channel_id=1, source_target_pairs={{0,1},{1,0},{2,3},{3,2},{4,5},{5,4},{6,7},{7,6},{8,9},{9,8},{10,11... | collective-permute-start | bytes 380936 | tf_op jit(solution)/shard_map/cond/branch_0_fun/ppermute | solution.py:175
  13.6 5.7 %collective-permute-start.5 = (bf16[496,128]{1,0:T(8,128)(2,1)S(1)}, bf16[496,128]{1,0:T(8,128)(2,1)S(1)}, u32[]{:S(2)}, u32[]{:S(2)}) collective-permute-start(bf16[496,128]{1,0:T(8,128)(2,1)S(1)} %collective-permute-done.1.refs_2_), channel_id=1, source_target_pairs={{0,1},{1,0},{2,3},{3,2},{4,5},{5,4},{6,7},{7,6},{8,9},{9,8},{10,11... | collective-permute-start | bytes 380936 | tf_op jit(solution)/shard_map/cond/branch_0_fun/ppermute | solution.py:175
  13.6 7.8 %collective-permute-start.8 = (bf16[496,128]{1,0:T(8,128)(2,1)S(1)}, bf16[496,128]{1,0:T(8,128)(2,1)S(1)}, u32[]{:S(2)}, u32[]{:S(2)}) collective-permute-start(bf16[496,128]{1,0:T(8,128)(2,1)S(1)} %collective-permute-done.7.refs_0_), channel_id=1, source_target_pairs={{0,4},{1,5},{2,6},{3,7},{4,0},{5,1},{6,2},{7,3},{8,12},{9,13},{10,... | collective-permute-start | bytes 380936 | tf_op jit(solution)/shard_map/cond/branch_0_fun/ppermute | solution.py:172
  16.0 7.6 %collective-permute-start.9 = (bf16[496,128]{1,0:T(8,128)(2,1)S(1)}, bf16[496,128]{1,0:T(8,128)(2,1)S(1)}, u32[]{:S(2)}, u32[]{:S(2)}) collective-permute-start(bf16[496,128]{1,0:T(8,128)(2,1)S(1)} %collective-permute-done.7.refs_0_), channel_id=1, source_target_pairs={{0,2},{1,3},{2,4},{3,5},{4,6},{5,7},{6,0},{7,1},{8,10},{9,11},{10,... | collective-permute-start | bytes 380936 | tf_op jit(solution)/shard_map/cond/branch_0_fun/ppermute | solution.py:172
  16.1 7.6 %collective-permute-start.10 = (bf16[496,128]{1,0:T(8,128)(2,1)S(1)}, bf16[496,128]{1,0:T(8,128)(2,1)S(1)}, u32[]{:S(2)}, u32[]{:S(2)}) collective-permute-start(bf16[496,128]{1,0:T(8,128)(2,1)S(1)} %collective-permute-done.7.refs_0_), channel_id=1, source_target_pairs={{0,6},{1,7},{2,0},{3,1},{4,2},{5,3},{6,4},{7,5},{8,14},{9,15},{10,... | collective-permute-start | bytes 380936 | tf_op jit(solution)/shard_map/cond/branch_0_fun/ppermute | solution.py:172
  19.2 4.9 %collective-permute-start.6 = (bf16[496,128]{1,0:T(8,128)(2,1)S(1)}, bf16[496,128]{1,0:T(8,128)(2,1)S(1)}, u32[]{:S(2)}, u32[]{:S(2)}) collective-permute-start(bf16[496,128]{1,0:T(8,128)(2,1)S(1)} %collective-permute-done.2.refs_3_), channel_id=1, source_target_pairs={{0,1},{1,0},{2,3},{3,2},{4,5},{5,4},{6,7},{7,6},{8,9},{9,8},{10,11... | collective-permute-start | bytes 380936 | tf_op jit(solution)/shard_map/cond/branch_0_fun/ppermute | solution.py:175
  19.2 6.8 %collective-permute-start.11 = (bf16[496,128]{1,0:T(8,128)(2,1)S(1)}, bf16[496,128]{1,0:T(8,128)(2,1)S(1)}, u32[]{:S(2)}, u32[]{:S(2)}) collective-permute-start(bf16[496,128]{1,0:T(8,128)(2,1)S(1)} %collective-permute-done.7.refs_0_), channel_id=1, source_target_pairs={{0,1},{1,0},{2,3},{3,2},{4,5},{5,4},{6,7},{7,6},{8,9},{9,8},{10,11... | collective-permute-start | bytes 380936 | tf_op jit(solution)/shard_map/cond/branch_0_fun/ppermute | solution.py:175
  21.4 4.7 %collective-permute-start.12 = (bf16[496,128]{1,0:T(8,128)(2,1)S(1)}, bf16[496,128]{1,0:T(8,128)(2,1)S(1)}, u32[]{:S(2)}, u32[]{:S(2)}) collective-permute-start(bf16[496,128]{1,0:T(8,128)(2,1)S(1)} %collective-permute-done.8.refs_1_), channel_id=1, source_target_pairs={{0,1},{1,0},{2,3},{3,2},{4,5},{5,4},{6,7},{7,6},{8,9},{9,8},{10,11... | collective-permute-start | bytes 380936 | tf_op jit(solution)/shard_map/cond/branch_0_fun/ppermute | solution.py:175
  23.6 2.4 %collective-permute-start.13 = (bf16[496,128]{1,0:T(8,128)(2,1)S(1)}, bf16[496,128]{1,0:T(8,128)(2,1)S(1)}, u32[]{:S(2)}, u32[]{:S(2)}) collective-permute-start(bf16[496,128]{1,0:T(8,128)(2,1)S(1)} %collective-permute-done.9.refs_2_), channel_id=1, source_target_pairs={{0,1},{1,0},{2,3},{3,2},{4,5},{5,4},{6,7},{7,6},{8,9},{9,8},{10,11... | collective-permute-start | bytes 380936 | tf_op jit(solution)/shard_map/cond/branch_0_fun/ppermute | solution.py:175
  23.6 2.4 %collective-permute-start.14 = (bf16[496,128]{1,0:T(8,128)(2,1)S(1)}, bf16[496,128]{1,0:T(8,128)(2,1)S(1)}, u32[]{:S(2)}, u32[]{:S(2)}) collective-permute-start(bf16[496,128]{1,0:T(8,128)(2,1)S(1)} %collective-permute-done.10.refs_3_), channel_id=1, source_target_pairs={{0,1},{1,0},{2,3},{3,2},{4,5},{5,4},{6,7},{7,6},{8,9},{9,8},{10,11... | collective-permute-start | bytes 380936 | tf_op jit(solution)/shard_map/cond/branch_0_fun/ppermute | solution.py:175
  28.1 12.0 %collective-permute-start.30 = (f32[32,384]{1,0:T(8,128)S(1)}, f32[32,384]{1,0:T(8,128)S(1)}, u32[]{:S(2)}, u32[]{:S(2)}) collective-permute-start(f32[32,384]{1,0:T(8,128)S(1)} %get-tuple-element.48), channel_id=1, source_target_pairs={{0,112},{16,64},{32,80},{48,96},{64,48},{80,0},{96,16},{112,32},{1... | collective-permute-start | bytes 147464 | tf_op jit(solution)/shard_map/ppermute | solution.py:154
  33.6 8.1 %collective-permute-start.31 = (f32[32,384]{1,0:T(8,128)S(1)}, f32[32,384]{1,0:T(8,128)S(1)}, u32[]{:S(2)}, u32[]{:S(2)}) collective-permute-start(f32[32,384]{1,0:T(8,128)S(1)} %get-tuple-element.49), channel_id=1, source_target_pairs={{0,96},{16,112},{32,64},{48,80},{64,32},{80,48},{96,0},{112,16},{1... | collective-permute-start | bytes 147464 | tf_op jit(solution)/shard_map/ppermute | solution.py:154
  34.1 9.3 %collective-permute-start.32 = (f32[32,384]{1,0:T(8,128)S(1)}, f32[32,384]{1,0:T(8,128)S(1)}, u32[]{:S(2)}, u32[]{:S(2)}) collective-permute-start(f32[32,384]{1,0:T(8,128)S(1)} %get-tuple-element.50), channel_id=1, source_target_pairs={{0,80},{16,96},{32,112},{48,64},{64,16},{80,32},{96,48},{112,0},{1... | collective-permute-start | bytes 147464 | tf_op jit(solution)/shard_map/ppermute | solution.py:154
  37.7 5.7 %collective-permute-start.33 = (f32[32,384]{1,0:T(8,128)S(1)}, f32[32,384]{1,0:T(8,128)S(1)}, u32[]{:S(2)}, u32[]{:S(2)}) collective-permute-start(f32[32,384]{1,0:T(8,128)S(1)} %get-tuple-element.51), channel_id=1, source_target_pairs={{0,64},{16,80},{32,96},{48,112},{64,0},{80,16},{96,32},{112,48},{1... | collective-permute-start | bytes 147464 | tf_op jit(solution)/shard_map/ppermute | solution.py:154
  38.0 6.1 %collective-permute-start.34 = (f32[32,384]{1,0:T(8,128)S(1)}, f32[32,384]{1,0:T(8,128)S(1)}, u32[]{:S(2)}, u32[]{:S(2)}) collective-permute-start(f32[32,384]{1,0:T(8,128)S(1)} %get-tuple-element.52), channel_id=1, source_target_pairs={{0,32},{16,48},{32,0},{48,16},{64,96},{80,112},{96,64},{112,80},{1... | collective-permute-start | bytes 147464 | tf_op jit(solution)/shard_map/ppermute | solution.py:154
  40.1 5.3 %collective-permute-start.35 = (f32[32,384]{1,0:T(8,128)S(1)}, f32[32,384]{1,0:T(8,128)S(1)}, u32[]{:S(2)}, u32[]{:S(2)}) collective-permute-start(f32[32,384]{1,0:T(8,128)S(1)} %get-tuple-element.53), channel_id=1, source_target_pairs={{0,16},{16,32},{32,48},{48,0},{64,80},{80,96},{96,112},{112,64},{1... | collective-permute-start | bytes 147464 | tf_op jit(solution)/shard_map/ppermute | solution.py:154
  41.7 4.1 %collective-permute-start.36 = (f32[32,384]{1,0:T(8,128)S(1)}, f32[32,384]{1,0:T(8,128)S(1)}, u32[]{:S(2)}, u32[]{:S(2)}) collective-permute-start(f32[32,384]{1,0:T(8,128)S(1)} %get-tuple-element.54), channel_id=1, source_target_pairs={{0,48},{16,0},{32,16},{48,32},{64,112},{80,64},{96,80},{112,96},{1... | collective-permute-start | bytes 147464 | tf_op jit(solution)/shard_map/ppermute | solution.py:154

commit v6 on v5

--- a/solution.py
+++ b/solution.py
@@ -48,12 +48,12 @@
             table[(label * 2 + t) * KINDS + 2] = jnp.where(own == label, 1.0, 0.0).astype(jnp.bfloat16)
 
 
-def pack_kernel(cd_ref, ab_ref, place_ref, v_ref, o_ref, most_ref, table):
+def pack_kernel(cd_ref, ab_ref, place_ref, v_ref, o_ref, crowded_ref, table):
     fill_factors(ab_ref, table)
     most = jnp.int32(0)
     for count in ranks(ab_ref):
         most = jnp.maximum(most, count)
-    most_ref[0] = most + 1
+    crowded_ref[0] = jnp.where(most + 1 > 2, 1, 0)
     subs = v_ref.shape[0] // SUB
     first = place_ref[0] * subs
     for j in range(subs):
@@ -141,7 +141,7 @@
         ref[...] = total[pl.ds(pl.multiple_of(target * share, 8), share), :]
 
 
-TARGETS = [(0, 0), (1, 3), (1, 2), (1, 1), (1, 0), (0, 2), (0, 1), (0, 3)]
+TARGETS = [(0, 0), (0, 2), (1, 3), (1, 2), (1, 1), (1, 0), (0, 1), (0, 3)]
 
 
 def row_hop(dy, dx):
@@ -203,7 +203,7 @@
 
 def shards(amplitudes, integrals, cd_irrep, ab_irrep, pair_energy, panel_energy):
     place = jnp.stack([lax.axis_index("col"), lax.axis_index("row")]).astype(jnp.int32)
-    packed, most = pack(cd_irrep, ab_irrep, place, integrals)
+    packed, crowded = pack(cd_irrep, ab_irrep, place, integrals)
 
     def narrow(packed, integrals, *rest):
         return partial_ladder(packed, *rest)
@@ -211,7 +211,7 @@
     def whole(packed, integrals, *rest):
         return partial_ladder(integrals, *rest)
 
-    blocks = lax.cond(most[0] > 2, whole, narrow, packed, integrals, amplitudes, cd_irrep, ab_irrep, place)
+    blocks = lax.switch(crowded[0], (narrow, whole), packed, integrals, amplitudes, cd_irrep, ab_irrep, place)
     parts = reduce_parts(blocks)
     share = parts[0].shape[0]
     summed = sum(parts[1:], parts[0])

time: 46.5 us -> 46.1 us (level)
  transfers between devices with their start and end apart: 22 -> 22, of which waited for: 7 -> 8; matrix products, arithmetic and copies ran while one was open for 0% -> 0% of each run, Pallas kernels for 4% -> 4%
where the time goes in v6:
time: 46.1 us; the launch traced here: 46 us
  starting transfers between devices  30.7 us (67%)
  waiting for transfers between devices  7.63 us (17%)
  Pallas kernels  5.74 us (12%)
  between operations  0.83 us (2%)
  other arithmetic  0.77 us (2%)
    ppermute x7, starting transfers between devices, reduce_parts(): parts.append(lax.ppermute(block, 'row', row_hop(*TARGETS[n])))  14.6 us
    ppermute x6, starting transfers between devices, partial_ladder(): mine.append(lax.ppermute(start, 'col', hop(0, dz)))  12.9 us
    ppermute x6, waiting for transfers between devices, partial_ladder(): mine.append(lax.ppermute(start, 'col', hop(0, dz)))  5.08 us
    ppermute x7, waiting for transfers between devices, reduce_parts(): parts.append(lax.ppermute(block, 'row', row_hop(*TARGETS[n])))  2.52 us
    pallas_call x1, Pallas kernels, partial_ladder(): pl.pallas_call(last_kernel, out_shape=[jax.ShapeDtypeStruct((width // 8,...  2.03 us
    pallas_call x1, Pallas kernels, partial_ladder(): pl.pallas_call(first_kernel, out_shape=jax.ShapeDtypeStruct((ij, width),...  1.88 us
    pallas_call x1, Pallas kernels, pack(): pl.pallas_call(pack_kernel, out_shape=(jax.ShapeDtypeStruct((integrals.sh...  1.83 us
    ppermute x1, starting transfers between devices, partial_ladder(): across = lax.ppermute(packed, 'col', hop(1, 0))  1.58 us
  transfers between devices with their start and end apart: 22, of which 8 were waited for; matrix products, arithmetic and copies ran while one was open for 0% of the time, Pallas kernels for 4%

profile of v6, /device:TPU:0, one launch (start us, length us, event | category | flops | bytes accessed | tf_op | source)
XLA Modules:
  0.0 46.0 jit_solution(5680182524411146529)
XLA Ops:
  0.0 0.1 pad_add_fusion.place_ref
  0.1 0.0 copy-start
  0.1 0.0 copy-start.3
  0.1 0.0 copy-start.4
  0.1 0.0 copy-start.5
  0.1 1.8 %pack.1 = (bf16[496,128]{1,0:T(8,128)(2,1)S(1)}, s32[1]{0:T(128)}) custom-call(s32[62]{0:T(128)} %cd_ref.1, s32[4]{0:T(128)} %ab_ref.1, s32[2]{0:T(128)S(1)} %pad_add_fusion.place_ref, bf16[496,256]{1,0:T(8,128)(2,1)} %v_ref.1), custom_call_target="tpu_custom_call" | custom-call | flops 10000000000 | bytes 253952 | tf_op jit(solution)/shard_map/pack/pallas_call | solution.py:72
  2.7 0.2 copy-done
  2.9 0.0 copy-done.3
  2.9 0.0 copy-done.4
  2.9 0.0 copy-done.5
  2.9 0.0 copy-start.7
  2.9 0.0 copy-start.6
  3.0 25.2 %conditional.1 = ((f32[32,384]{1,0:T(8,128)S(1)}, f32[32,384]{1,0:T(8,128)S(1)}, f32[32,384]{1,0:T(8,128)S(1)}, f32[32,384]{1,0:T(8,128)S(1)}, f32[32,384]{1,0:T...) conditional(s32[]{:T(128)} %bitcast.2, (bf16[496,128]{1,0:T(8,128)(2,1)S(1)}, ...), branch_computations={%region_0.0_spmd, %region_1.0_spmd} | conditional | flops 1560281088 | bytes 70091416 | solution.py:214
  3.0 4.1 %collective-permute-start = (bf16[496,128]{1,0:T(8,128)(2,1)S(1)}, bf16[496,128]{1,0:T(8,128)(2,1)S(1)}, u32[]{:S(2)}, u32[]{:S(2)}) collective-permute-start(bf16[496,128]{1,0:T(8,128)(2,1)S(1)} %get-tuple-element.29.refs_0_), channel_id=1, source_target_pairs={{0,4},{1,5},{2,6},{3,7},{4,0},{5,1},{6,2},{7,3},{8,12},{9,13},{10,... | collective-permute-start | bytes 380936 | tf_op jit(solution)/shard_map/cond/branch_0_fun/ppermute | solution.py:172
  7.0 1.0 %collective-permute-start.1 = (bf16[496,128]{1,0:T(8,128)(2,1)S(1)}, bf16[496,128]{1,0:T(8,128)(2,1)S(1)}, u32[]{:S(2)}, u32[]{:S(2)}) collective-permute-start(bf16[496,128]{1,0:T(8,128)(2,1)S(1)} %get-tuple-element.29.refs_0_), channel_id=1, source_target_pairs={{0,2},{1,3},{2,4},{3,5},{4,6},{5,7},{6,0},{7,1},{8,10},{9,11},{10,... | collective-permute-start | bytes 380936 | tf_op jit(solution)/shard_map/cond/branch_0_fun/ppermute | solution.py:172
  8.1 1.6 %collective-permute-start.7 = (bf16[496,128]{1,0:T(8,128)(2,1)S(1)}, bf16[496,128]{1,0:T(8,128)(2,1)S(1)}, u32[]{:S(2)}, u32[]{:S(2)}) collective-permute-start(bf16[496,128]{1,0:T(8,128)(2,1)S(1)} %get-tuple-element.29.refs_0_), channel_id=1, source_target_pairs={{0,8},{1,9},{2,10},{3,11},{4,12},{5,13},{6,14},{7,15},{8,0},{9,1},... | collective-permute-start | bytes 380936 | tf_op jit(solution)/shard_map/cond/branch_0_fun/ppermute | solution.py:167
  9.6 2.2 %collective-permute-start.2 = (bf16[496,128]{1,0:T(8,128)(2,1)S(1)}, bf16[496,128]{1,0:T(8,128)(2,1)S(1)}, u32[]{:S(2)}, u32[]{:S(2)}) collective-permute-start(bf16[496,128]{1,0:T(8,128)(2,1)S(1)} %get-tuple-element.29.refs_0_), channel_id=1, source_target_pairs={{0,6},{1,7},{2,0},{3,1},{4,2},{5,3},{6,4},{7,5},{8,14},{9,15},{10,... | collective-permute-start | bytes 380936 | tf_op jit(solution)/shard_map/cond/branch_0_fun/ppermute | solution.py:172
  11.8 0.0 collective-permute-start.3
  11.9 0.0 collective-permute-done.refs_1_
  11.9 0.5 %collective-permute-start.4 = (bf16[496,128]{1,0:T(8,128)(2,1)S(1)}, bf16[496,128]{1,0:T(8,128)(2,1)S(1)}, u32[]{:S(2)}, u32[]{:S(2)}) collective-permute-start(bf16[496,128]{1,0:T(8,128)(2,1)S(1)} %collective-permute-done.refs_1_), channel_id=1, source_target_pairs={{0,1},{1,0},{2,3},{3,2},{4,5},{5,4},{6,7},{7,6},{8,9},{9,8},{10,11... | collective-permute-start | bytes 380936 | tf_op jit(solution)/shard_map/cond/branch_0_fun/ppermute | solution.py:175
  12.4 1.2 %collective-permute-done.1.refs_2_ = bf16[496,128]{1,0:T(8,128)(2,1)S(1)} collective-permute-done((bf16[496,128]{1,0:T(8,128)(2,1)S(1)}, bf16[496,128]{1,0:T(8,128)(2,1)S(1)}, u32[]{:S(2)}, u32[]{:S(2)}) %collective-permute-start.1) | collective-permute-done | bytes 127008 | tf_op jit(solution)/shard_map/cond/branch_0_fun/ppermute | solution.py:172
  13.6 0.0 collective-permute-start.5
  13.6 0.0 collective-permute-done.7.refs_0_
  13.6 2.4 %collective-permute-start.8 = (bf16[496,128]{1,0:T(8,128)(2,1)S(1)}, bf16[496,128]{1,0:T(8,128)(2,1)S(1)}, u32[]{:S(2)}, u32[]{:S(2)}) collective-permute-start(bf16[496,128]{1,0:T(8,128)(2,1)S(1)} %collective-permute-done.7.refs_0_), channel_id=1, source_target_pairs={{0,4},{1,5},{2,6},{3,7},{4,0},{5,1},{6,2},{7,3},{8,12},{9,13},{10,... | collective-permute-start | bytes 380936 | tf_op jit(solution)/shard_map/cond/branch_0_fun/ppermute | solution.py:172
  16.0 0.0 collective-permute-done.2.refs_3_
  16.0 0.1 collective-permute-start.9
  16.1 0.0 collective-permute-done.3.refs_4_
  16.1 3.2 %collective-permute-start.10 = (bf16[496,128]{1,0:T(8,128)(2,1)S(1)}, bf16[496,128]{1,0:T(8,128)(2,1)S(1)}, u32[]{:S(2)}, u32[]{:S(2)}) collective-permute-start(bf16[496,128]{1,0:T(8,128)(2,1)S(1)} %collective-permute-done.7.refs_0_), channel_id=1, source_target_pairs={{0,6},{1,7},{2,0},{3,1},{4,2},{5,3},{6,4},{7,5},{8,14},{9,15},{10,... | collective-permute-start | bytes 380936 | tf_op jit(solution)/shard_map/cond/branch_0_fun/ppermute | solution.py:172
  19.2 0.0 collective-permute-done.4.refs_5_
  19.2 0.0 collective-permute-start.6
  19.2 0.0 collective-permute-done.5.refs_6_
  19.2 0.5 %collective-permute-start.11 = (bf16[496,128]{1,0:T(8,128)(2,1)S(1)}, bf16[496,128]{1,0:T(8,128)(2,1)S(1)}, u32[]{:S(2)}, u32[]{:S(2)}) collective-permute-start(bf16[496,128]{1,0:T(8,128)(2,1)S(1)} %collective-permute-done.7.refs_0_), channel_id=1, source_target_pairs={{0,1},{1,0},{2,3},{3,2},{4,5},{5,4},{6,7},{7,6},{8,9},{9,8},{10,11... | collective-permute-start | bytes 380936 | tf_op jit(solution)/shard_map/cond/branch_0_fun/ppermute | solution.py:175
  19.7 1.6 %collective-permute-done.8.refs_1_ = bf16[496,128]{1,0:T(8,128)(2,1)S(1)} collective-permute-done((bf16[496,128]{1,0:T(8,128)(2,1)S(1)}, bf16[496,128]{1,0:T(8,128)(2,1)S(1)}, u32[]{:S(2)}, u32[]{:S(2)}) %collective-permute-start.8) | collective-permute-done | bytes 127008 | tf_op jit(solution)/shard_map/cond/branch_0_fun/ppermute | solution.py:172
  21.4 0.0 collective-permute-start.12
  21.4 2.3 %collective-permute-done.9.refs_2_ = bf16[496,128]{1,0:T(8,128)(2,1)S(1)} collective-permute-done((bf16[496,128]{1,0:T(8,128)(2,1)S(1)}, bf16[496,128]{1,0:T(8,128)(2,1)S(1)}, u32[]{:S(2)}, u32[]{:S(2)}) %collective-permute-start.9) | collective-permute-done | bytes 127008 | tf_op jit(solution)/shard_map/cond/branch_0_fun/ppermute | solution.py:172
  23.6 0.0 collective-permute-start.13
  23.6 0.0 collective-permute-done.10.refs_3_
  23.6 0.5 %collective-permute-start.14 = (bf16[496,128]{1,0:T(8,128)(2,1)S(1)}, bf16[496,128]{1,0:T(8,128)(2,1)S(1)}, u32[]{:S(2)}, u32[]{:S(2)}) collective-permute-start(bf16[496,128]{1,0:T(8,128)(2,1)S(1)} %collective-permute-done.10.refs_3_), channel_id=1, source_target_pairs={{0,1},{1,0},{2,3},{3,2},{4,5},{5,4},{6,7},{7,6},{8,9},{9,8},{10,11... | collective-permute-start | bytes 380936 | tf_op jit(solution)/shard_map/cond/branch_0_fun/ppermute | solution.py:175
  24.1 0.0 collective-permute-done.6.refs_7_
  24.1 1.9 %ladder_first.2.before_ref = f32[384,256]{1,0:T(8,128)S(1)} custom-call(s32[62]{0:T(128)S(1)} %get-tuple-element.25.cd_ref, s32[4]{0:T(128)S(1)} %get-tuple-element.26.ab_ref, s32[2]{0:T(128)S(1)} %get-tuple-element.27.place_ref, bf16[384,7936]{1,0:T(8,128)(2,1)S(1)} %get-tuple-element.28.t_ref, bf16[496,128]{1,0:T(8,128)(2,1)S(1)} %get-tuple-element.29.refs_0_, ...), custom_call_target="tpu_custom_call" | custom-call | flops 780140544 | bytes 3047424 | tf_op jit(solution)/shard_map/cond/branch_0_fun/ladder_first/pallas_call | solution.py:182
  26.0 0.0 collective-permute-done.11.refs_4_
  26.0 0.0 collective-permute-done.12.refs_5_
  26.0 0.0 collective-permute-done.13.refs_6_
  26.1 0.0 collective-permute-done.14.refs_7_
  26.1 2.0 %ladder_last.2 = (f32[32,384]{1,0:T(8,128)S(1)}, f32[32,384]{1,0:T(8,128)S(1)}, f32[32,384]{1,0:T(8,128)S(1)}, f32[32,384]{1,0:T(8,128)S(1)}, f32[32,384]{1,0:T(...) custom-call(s32[62]{0:T(128)S(1)} %get-tuple-element.25.cd_ref, ...), custom_call_target="tpu_custom_call" | custom-call | flops 780140544 | bytes 3047424 | tf_op jit(solution)/shard_map/cond/branch_0_fun/ladder_last/pallas_call | solution.py:192
  28.1 3.1 %collective-permute-start.30 = (f32[32,384]{1,0:T(8,128)S(1)}, f32[32,384]{1,0:T(8,128)S(1)}, u32[]{:S(2)}, u32[]{:S(2)}) collective-permute-start(f32[32,384]{1,0:T(8,128)S(1)} %get-tuple-element.48), channel_id=1, source_target_pairs={{0,32},{16,48},{32,0},{48,16},{64,96},{80,112},{96,64},{112,80},{1... | collective-permute-start | bytes 147464 | tf_op jit(solution)/shard_map/ppermute | solution.py:154
  31.2 3.8 %collective-permute-start.31 = (f32[32,384]{1,0:T(8,128)S(1)}, f32[32,384]{1,0:T(8,128)S(1)}, u32[]{:S(2)}, u32[]{:S(2)}) collective-permute-start(f32[32,384]{1,0:T(8,128)S(1)} %get-tuple-element.49), channel_id=1, source_target_pairs={{0,112},{16,64},{32,80},{48,96},{64,48},{80,0},{96,16},{112,32},{1... | collective-permute-start | bytes 147464 | tf_op jit(solution)/shard_map/ppermute | solution.py:154
  35.0 1.3 %collective-permute-start.32 = (f32[32,384]{1,0:T(8,128)S(1)}, f32[32,384]{1,0:T(8,128)S(1)}, u32[]{:S(2)}, u32[]{:S(2)}) collective-permute-start(f32[32,384]{1,0:T(8,128)S(1)} %get-tuple-element.50), channel_id=1, source_target_pairs={{0,96},{16,112},{32,64},{48,80},{64,32},{80,48},{96,0},{112,16},{1... | collective-permute-start | bytes 147464 | tf_op jit(solution)/shard_map/ppermute | solution.py:154
  36.3 1.9 %collective-permute-start.33 = (f32[32,384]{1,0:T(8,128)S(1)}, f32[32,384]{1,0:T(8,128)S(1)}, u32[]{:S(2)}, u32[]{:S(2)}) collective-permute-start(f32[32,384]{1,0:T(8,128)S(1)} %get-tuple-element.51), channel_id=1, source_target_pairs={{0,80},{16,96},{32,112},{48,64},{64,16},{80,32},{96,48},{112,0},{1... | collective-permute-start | bytes 147464 | tf_op jit(solution)/shard_map/ppermute | solution.py:154
  38.2 1.3 %collective-permute-start.34 = (f32[32,384]{1,0:T(8,128)S(1)}, f32[32,384]{1,0:T(8,128)S(1)}, u32[]{:S(2)}, u32[]{:S(2)}) collective-permute-start(f32[32,384]{1,0:T(8,128)S(1)} %get-tuple-element.52), channel_id=1, source_target_pairs={{0,64},{16,80},{32,96},{48,112},{64,0},{80,16},{96,32},{112,48},{1... | collective-permute-start | bytes 147464 | tf_op jit(solution)/shard_map/ppermute | solution.py:154
  39.5 0.0 collective-permute-done.30
  39.5 1.7 %collective-permute-start.35 = (f32[32,384]{1,0:T(8,128)S(1)}, f32[32,384]{1,0:T(8,128)S(1)}, u32[]{:S(2)}, u32[]{:S(2)}) collective-permute-start(f32[32,384]{1,0:T(8,128)S(1)} %get-tuple-element.53), channel_id=1, source_target_pairs={{0,16},{16,32},{32,48},{48,0},{64,80},{80,96},{96,112},{112,64},{1... | collective-permute-start | bytes 147464 | tf_op jit(solution)/shard_map/ppermute | solution.py:154
  41.2 0.0 collective-permute-done.31
  41.2 1.5 %collective-permute-start.36 = (f32[32,384]{1,0:T(8,128)S(1)}, f32[32,384]{1,0:T(8,128)S(1)}, u32[]{:S(2)}, u32[]{:S(2)}) collective-permute-start(f32[32,384]{1,0:T(8,128)S(1)} %get-tuple-element.54), channel_id=1, source_target_pairs={{0,48},{16,0},{32,16},{48,32},{64,112},{80,64},{96,80},{112,96},{1... | collective-permute-start | bytes 147464 | tf_op jit(solution)/shard_map/ppermute | solution.py:154
  42.7 0.0 copy-done.7
  42.7 0.1 dynamic_slice.3
  42.8 0.2 collective-permute-done.32
  43.0 1.1 %collective-permute-done.33 = f32[32,384]{1,0:T(8,128)S(1)} collective-permute-done((f32[32,384]{1,0:T(8,128)S(1)}, f32[32,384]{1,0:T(8,128)S(1)}, u32[]{:S(2)}, u32[]{:S(2)}) %collective-permute-start.33) | collective-permute-done | bytes 49184 | tf_op jit(solution)/shard_map/ppermute | solution.py:154
  44.1 0.2 collective-permute-done.34
  44.3 0.5 %collective-permute-done.35 = f32[32,384]{1,0:T(8,128)S(1)} collective-permute-done((f32[32,384]{1,0:T(8,128)S(1)}, f32[32,384]{1,0:T(8,128)S(1)}, u32[]{:S(2)}, u32[]{:S(2)}) %collective-permute-start.35) | collective-permute-done | bytes 49184 | tf_op jit(solution)/shard_map/ppermute | solution.py:154
  44.8 0.5 %collective-permute-done.36 = f32[32,384]{1,0:T(8,128)S(1)} collective-permute-done((f32[32,384]{1,0:T(8,128)S(1)}, f32[32,384]{1,0:T(8,128)S(1)}, u32[]{:S(2)}, u32[]{:S(2)}) %collective-permute-start.36) | collective-permute-done | bytes 49184 | tf_op jit(solution)/shard_map/ppermute | solution.py:154
  45.3 0.0 copy-done.6
  45.3 0.7 %fusion = bf16[384,32]{0,1:T(8,128)(2,1)} fusion(f32[384]{0:T(512)S(1)} %copy-done.6, f32[32]{0:T(128)S(1)} %dynamic_slice.3, f32[32,384]{1,0:T(8,128)S(1)} %collective-permute-done.36, f32[32,384]{1,0:T(8,128)S(1)} %collective-permute-done.35, f32[32,384]{1,0:T(8,128)S(1)} %collective-permute-done.34, f32[32,384]{1,0:T(8,128)S(1)} %collective-permute-done.33, ...), kind=kLoop, calls=%fused_computation.1 | loop fusion | flops 122880 | bytes 419456 | tf_op jit(solution)/shard_map/transpose | solution.py:220
Async XLA Ops:
  0.1 2.9 %copy-start = (bf16[384,7936]{1,0:T(8,128)(2,1)S(1)}, bf16[384,7936]{1,0:T(8,128)(2,1)}, u32[]{:S(2)}) copy-start(bf16[384,7936]{1,0:T(8,128)(2,1)} %param.8) | copy-start | bytes 18284548
  0.1 2.9 %copy-start.3 = (bf16[496,256]{1,0:T(8,128)(2,1)S(1)}, bf16[496,256]{1,0:T(8,128)(2,1)}, u32[]{:S(2)}) copy-start(bf16[496,256]{1,0:T(8,128)(2,1)} %v_ref.1) | copy-start | bytes 761860
  0.1 2.9 %copy-start.4 = (s32[62]{0:T(128)S(1)}, s32[62]{0:T(128)}, u32[]{:S(2)}) copy-start(s32[62]{0:T(128)} %cd_ref.1) | copy-start | bytes 748
  0.1 2.9 %copy-start.5 = (s32[4]{0:T(128)S(1)}, s32[4]{0:T(128)}, u32[]{:S(2)}) copy-start(s32[4]{0:T(128)} %ab_ref.1) | copy-start | bytes 52
  2.9 39.8 %copy-start.7 = (f32[256]{0:T(256)S(1)}, f32[256]{0:T(256)}, u32[]{:S(2)}) copy-start(f32[256]{0:T(256)} %param.13) | copy-start | bytes 3076
  2.9 42.4 %copy-start.6 = (f32[384]{0:T(512)S(1)}, f32[384]{0:T(512)}, u32[]{:S(2)}) copy-start(f32[384]{0:T(512)} %param.12) | copy-start | bytes 4612
  3.0 8.9 %collective-permute-start = (bf16[496,128]{1,0:T(8,128)(2,1)S(1)}, bf16[496,128]{1,0:T(8,128)(2,1)S(1)}, u32[]{:S(2)}, u32[]{:S(2)}) collective-permute-start(bf16[496,128]{1,0:T(8,128)(2,1)S(1)} %get-tuple-element.29.refs_0_), channel_id=1, source_target_pairs={{0,4},{1,5},{2,6},{3,7},{4,0},{5,1},{6,2},{7,3},{8,12},{9,13},{10,... | collective-permute-start | bytes 380936 | tf_op jit(solution)/shard_map/cond/branch_0_fun/ppermute | solution.py:172
  7.0 6.5 %collective-permute-start.1 = (bf16[496,128]{1,0:T(8,128)(2,1)S(1)}, bf16[496,128]{1,0:T(8,128)(2,1)S(1)}, u32[]{:S(2)}, u32[]{:S(2)}) collective-permute-start(bf16[496,128]{1,0:T(8,128)(2,1)S(1)} %get-tuple-element.29.refs_0_), channel_id=1, source_target_pairs={{0,2},{1,3},{2,4},{3,5},{4,6},{5,7},{6,0},{7,1},{8,10},{9,11},{10,... | collective-permute-start | bytes 380936 | tf_op jit(solution)/shard_map/cond/branch_0_fun/ppermute | solution.py:172
  8.1 5.5 %collective-permute-start.7 = (bf16[496,128]{1,0:T(8,128)(2,1)S(1)}, bf16[496,128]{1,0:T(8,128)(2,1)S(1)}, u32[]{:S(2)}, u32[]{:S(2)}) collective-permute-start(bf16[496,128]{1,0:T(8,128)(2,1)S(1)} %get-tuple-element.29.refs_0_), channel_id=1, source_target_pairs={{0,8},{1,9},{2,10},{3,11},{4,12},{5,13},{6,14},{7,15},{8,0},{9,1},... | collective-permute-start | bytes 380936 | tf_op jit(solution)/shard_map/cond/branch_0_fun/ppermute | solution.py:167
  9.6 6.3 %collective-permute-start.2 = (bf16[496,128]{1,0:T(8,128)(2,1)S(1)}, bf16[496,128]{1,0:T(8,128)(2,1)S(1)}, u32[]{:S(2)}, u32[]{:S(2)}) collective-permute-start(bf16[496,128]{1,0:T(8,128)(2,1)S(1)} %get-tuple-element.29.refs_0_), channel_id=1, source_target_pairs={{0,6},{1,7},{2,0},{3,1},{4,2},{5,3},{6,4},{7,5},{8,14},{9,15},{10,... | collective-permute-start | bytes 380936 | tf_op jit(solution)/shard_map/cond/branch_0_fun/ppermute | solution.py:172
  11.8 4.2 %collective-permute-start.3 = (bf16[496,128]{1,0:T(8,128)(2,1)S(1)}, bf16[496,128]{1,0:T(8,128)(2,1)S(1)}, u32[]{:S(2)}, u32[]{:S(2)}) collective-permute-start(bf16[496,128]{1,0:T(8,128)(2,1)S(1)} %get-tuple-element.29.refs_0_), channel_id=1, source_target_pairs={{0,1},{1,0},{2,3},{3,2},{4,5},{5,4},{6,7},{7,6},{8,9},{9,8},{10,11... | collective-permute-start | bytes 380936 | tf_op jit(solution)/shard_map/cond/branch_0_fun/ppermute | solution.py:175
  11.9 7.4 %collective-permute-start.4 = (bf16[496,128]{1,0:T(8,128)(2,1)S(1)}, bf16[496,128]{1,0:T(8,128)(2,1)S(1)}, u32[]{:S(2)}, u32[]{:S(2)}) collective-permute-start(bf16[496,128]{1,0:T(8,128)(2,1)S(1)} %collective-permute-done.refs_1_), channel_id=1, source_target_pairs={{0,1},{1,0},{2,3},{3,2},{4,5},{5,4},{6,7},{7,6},{8,9},{9,8},{10,11... | collective-permute-start | bytes 380936 | tf_op jit(solution)/shard_map/cond/branch_0_fun/ppermute | solution.py:175
  13.6 5.7 %collective-permute-start.5 = (bf16[496,128]{1,0:T(8,128)(2,1)S(1)}, bf16[496,128]{1,0:T(8,128)(2,1)S(1)}, u32[]{:S(2)}, u32[]{:S(2)}) collective-permute-start(bf16[496,128]{1,0:T(8,128)(2,1)S(1)} %collective-permute-done.1.refs_2_), channel_id=1, source_target_pairs={{0,1},{1,0},{2,3},{3,2},{4,5},{5,4},{6,7},{7,6},{8,9},{9,8},{10,11... | collective-permute-start | bytes 380936 | tf_op jit(solution)/shard_map/cond/branch_0_fun/ppermute | solution.py:175
  13.6 7.8 %collective-permute-start.8 = (bf16[496,128]{1,0:T(8,128)(2,1)S(1)}, bf16[496,128]{1,0:T(8,128)(2,1)S(1)}, u32[]{:S(2)}, u32[]{:S(2)}) collective-permute-start(bf16[496,128]{1,0:T(8,128)(2,1)S(1)} %collective-permute-done.7.refs_0_), channel_id=1, source_target_pairs={{0,4},{1,5},{2,6},{3,7},{4,0},{5,1},{6,2},{7,3},{8,12},{9,13},{10,... | collective-permute-start | bytes 380936 | tf_op jit(solution)/shard_map/cond/branch_0_fun/ppermute | solution.py:172
  16.0 7.6 %collective-permute-start.9 = (bf16[496,128]{1,0:T(8,128)(2,1)S(1)}, bf16[496,128]{1,0:T(8,128)(2,1)S(1)}, u32[]{:S(2)}, u32[]{:S(2)}) collective-permute-start(bf16[496,128]{1,0:T(8,128)(2,1)S(1)} %collective-permute-done.7.refs_0_), channel_id=1, source_target_pairs={{0,2},{1,3},{2,4},{3,5},{4,6},{5,7},{6,0},{7,1},{8,10},{9,11},{10,... | collective-permute-start | bytes 380936 | tf_op jit(solution)/shard_map/cond/branch_0_fun/ppermute | solution.py:172
  16.1 7.6 %collective-permute-start.10 = (bf16[496,128]{1,0:T(8,128)(2,1)S(1)}, bf16[496,128]{1,0:T(8,128)(2,1)S(1)}, u32[]{:S(2)}, u32[]{:S(2)}) collective-permute-start(bf16[496,128]{1,0:T(8,128)(2,1)S(1)} %collective-permute-done.7.refs_0_), channel_id=1, source_target_pairs={{0,6},{1,7},{2,0},{3,1},{4,2},{5,3},{6,4},{7,5},{8,14},{9,15},{10,... | collective-permute-start | bytes 380936 | tf_op jit(solution)/shard_map/cond/branch_0_fun/ppermute | solution.py:172
  19.2 4.9 %collective-permute-start.6 = (bf16[496,128]{1,0:T(8,128)(2,1)S(1)}, bf16[496,128]{1,0:T(8,128)(2,1)S(1)}, u32[]{:S(2)}, u32[]{:S(2)}) collective-permute-start(bf16[496,128]{1,0:T(8,128)(2,1)S(1)} %collective-permute-done.2.refs_3_), channel_id=1, source_target_pairs={{0,1},{1,0},{2,3},{3,2},{4,5},{5,4},{6,7},{7,6},{8,9},{9,8},{10,11... | collective-permute-start | bytes 380936 | tf_op jit(solution)/shard_map/cond/branch_0_fun/ppermute | solution.py:175
  19.2 6.8 %collective-permute-start.11 = (bf16[496,128]{1,0:T(8,128)(2,1)S(1)}, bf16[496,128]{1,0:T(8,128)(2,1)S(1)}, u32[]{:S(2)}, u32[]{:S(2)}) collective-permute-start(bf16[496,128]{1,0:T(8,128)(2,1)S(1)} %collective-permute-done.7.refs_0_), channel_id=1, source_target_pairs={{0,1},{1,0},{2,3},{3,2},{4,5},{5,4},{6,7},{7,6},{8,9},{9,8},{10,11... | collective-permute-start | bytes 380936 | tf_op jit(solution)/shard_map/cond/branch_0_fun/ppermute | solution.py:175
  21.4 4.7 %collective-permute-start.12 = (bf16[496,128]{1,0:T(8,128)(2,1)S(1)}, bf16[496,128]{1,0:T(8,128)(2,1)S(1)}, u32[]{:S(2)}, u32[]{:S(2)}) collective-permute-start(bf16[496,128]{1,0:T(8,128)(2,1)S(1)} %collective-permute-done.8.refs_1_), channel_id=1, source_target_pairs={{0,1},{1,0},{2,3},{3,2},{4,5},{5,4},{6,7},{7,6},{8,9},{9,8},{10,11... | collective-permute-start | bytes 380936 | tf_op jit(solution)/shard_map/cond/branch_0_fun/ppermute | solution.py:175
  23.6 2.4 %collective-permute-start.13 = (bf16[496,128]{1,0:T(8,128)(2,1)S(1)}, bf16[496,128]{1,0:T(8,128)(2,1)S(1)}, u32[]{:S(2)}, u32[]{:S(2)}) collective-permute-start(bf16[496,128]{1,0:T(8,128)(2,1)S(1)} %collective-permute-done.9.refs_2_), channel_id=1, source_target_pairs={{0,1},{1,0},{2,3},{3,2},{4,5},{5,4},{6,7},{7,6},{8,9},{9,8},{10,11... | collective-permute-start | bytes 380936 | tf_op jit(solution)/shard_map/cond/branch_0_fun/ppermute | solution.py:175
  23.6 2.4 %collective-permute-start.14 = (bf16[496,128]{1,0:T(8,128)(2,1)S(1)}, bf16[496,128]{1,0:T(8,128)(2,1)S(1)}, u32[]{:S(2)}, u32[]{:S(2)}) collective-permute-start(bf16[496,128]{1,0:T(8,128)(2,1)S(1)} %collective-permute-done.10.refs_3_), channel_id=1, source_target_pairs={{0,1},{1,0},{2,3},{3,2},{4,5},{5,4},{6,7},{7,6},{8,9},{9,8},{10,11... | collective-permute-start | bytes 380936 | tf_op jit(solution)/shard_map/cond/branch_0_fun/ppermute | solution.py:175
  28.1 11.4 %collective-permute-start.30 = (f32[32,384]{1,0:T(8,128)S(1)}, f32[32,384]{1,0:T(8,128)S(1)}, u32[]{:S(2)}, u32[]{:S(2)}) collective-permute-start(f32[32,384]{1,0:T(8,128)S(1)} %get-tuple-element.48), channel_id=1, source_target_pairs={{0,32},{16,48},{32,0},{48,16},{64,96},{80,112},{96,64},{112,80},{1... | collective-permute-start | bytes 147464 | tf_op jit(solution)/shard_map/ppermute | solution.py:154
  31.2 10.0 %collective-permute-start.31 = (f32[32,384]{1,0:T(8,128)S(1)}, f32[32,384]{1,0:T(8,128)S(1)}, u32[]{:S(2)}, u32[]{:S(2)}) collective-permute-start(f32[32,384]{1,0:T(8,128)S(1)} %get-tuple-element.49), channel_id=1, source_target_pairs={{0,112},{16,64},{32,80},{48,96},{64,48},{80,0},{96,16},{112,32},{1... | collective-permute-start | bytes 147464 | tf_op jit(solution)/shard_map/ppermute | solution.py:154
  35.0 8.0 %collective-permute-start.32 = (f32[32,384]{1,0:T(8,128)S(1)}, f32[32,384]{1,0:T(8,128)S(1)}, u32[]{:S(2)}, u32[]{:S(2)}) collective-permute-start(f32[32,384]{1,0:T(8,128)S(1)} %get-tuple-element.50), channel_id=1, source_target_pairs={{0,96},{16,112},{32,64},{48,80},{64,32},{80,48},{96,0},{112,16},{1... | collective-permute-start | bytes 147464 | tf_op jit(solution)/shard_map/ppermute | solution.py:154
  36.3 7.8 %collective-permute-start.33 = (f32[32,384]{1,0:T(8,128)S(1)}, f32[32,384]{1,0:T(8,128)S(1)}, u32[]{:S(2)}, u32[]{:S(2)}) collective-permute-start(f32[32,384]{1,0:T(8,128)S(1)} %get-tuple-element.51), channel_id=1, source_target_pairs={{0,80},{16,96},{32,112},{48,64},{64,16},{80,32},{96,48},{112,0},{1... | collective-permute-start | bytes 147464 | tf_op jit(solution)/shard_map/ppermute | solution.py:154
  38.2 6.1 %collective-permute-start.34 = (f32[32,384]{1,0:T(8,128)S(1)}, f32[32,384]{1,0:T(8,128)S(1)}, u32[]{:S(2)}, u32[]{:S(2)}) collective-permute-start(f32[32,384]{1,0:T(8,128)S(1)} %get-tuple-element.52), channel_id=1, source_target_pairs={{0,64},{16,80},{32,96},{48,112},{64,0},{80,16},{96,32},{112,48},{1... | collective-permute-start | bytes 147464 | tf_op jit(solution)/shard_map/ppermute | solution.py:154
  39.5 5.3 %collective-permute-start.35 = (f32[32,384]{1,0:T(8,128)S(1)}, f32[32,384]{1,0:T(8,128)S(1)}, u32[]{:S(2)}, u32[]{:S(2)}) collective-permute-start(f32[32,384]{1,0:T(8,128)S(1)} %get-tuple-element.53), channel_id=1, source_target_pairs={{0,16},{16,32},{32,48},{48,0},{64,80},{80,96},{96,112},{112,64},{1... | collective-permute-start | bytes 147464 | tf_op jit(solution)/shard_map/ppermute | solution.py:154
  41.2 4.1 %collective-permute-start.36 = (f32[32,384]{1,0:T(8,128)S(1)}, f32[32,384]{1,0:T(8,128)S(1)}, u32[]{:S(2)}, u32[]{:S(2)}) collective-permute-start(f32[32,384]{1,0:T(8,128)S(1)} %get-tuple-element.54), channel_id=1, source_target_pairs={{0,48},{16,0},{32,16},{48,32},{64,112},{80,64},{96,80},{112,96},{1... | collective-permute-start | bytes 147464 | tf_op jit(solution)/shard_map/ppermute | solution.py:154
